TPU v7x, 256 devices: a whole 4x4x8 slice. The times are simulated.
256 devices in a mesh: space: 64 (over y, x, z_hi), member: 4 (over z_lo, core).
Axes of the slice: x: 4, y: 4, z: 8 (z_hi: 4, z_lo: 2; z = z_hi * 2 + z_lo), core: 2. Of those that a mesh axis runs over, the one named last changes fastest.
Arguments:
- positions: float32 [1024, 3, 128], P('space'), may hold values from -6 to 6
- features: bfloat16 [1024, 128, 128], P('space'), may hold values from -6 to 6
- nbr_list: int32 [1024, 6], P('space'), may hold values from 0 to 1023, as said below
- nbr_count: int32 [1024], P('space'), may hold values from 3 to 6, as said below
- w_embed: bfloat16 [4, 128, 128], P('member'), may hold values from -0.5 to 0.5
- w_proj: bfloat16 [4, 128, 512], P('member'), may hold values from -0.5 to 0.5
- rates: float32 [4, 4], P('member'), may hold values from 0.05 to 1
Outputs:
- mean_force: float32 [1024, 3, 128], P('space')
- variance_grad: float32 [1024, 3, 128], P('space')
Inputs may be any that keep to these rules, and one draw needn't show every extreme that they name: `nbr_list`: with q = b // 16 the domain of block b, taken cyclically over the 64 domains: slot 0 names b itself, slot 1 a block of domain q - 1, slot 2 a block of domain q + 1, every other slot a block of domain q - 1, q or q + 1. `nbr_count`: block 0 has all 6 slots live and block 1 exactly 3.
All inputs are finite; a program needn't handle non-finite values.
Results may differ from a plain program's by a relative error of at most 0.0017.
Values may be sent and summed in bfloat16 or wider, within the bound.
No kernel may reach another device: no remote copies, remote signals or barrier semaphores. Data moves between devices by JAX's collectives and lax.ppermute only.
A program may use at most 128 MiB of HBM per device.

v0:
```python
import math

import jax
import jax.numpy as jnp
from jax import lax
from jax.sharding import PartitionSpec as P


def with_halo(block, sides, width):
    for axis, dim in sides:
        count = lax.axis_size(axis)
        forward = [(i, i + 1) for i in range(count - 1)]
        forward.append((count - 1, 0))
        backward = [(target, source) for source, target in forward]
        low = lax.ppermute(
            lax.slice_in_dim(block, block.shape[dim] - width, None, axis=dim), axis, forward
        )
        high = lax.ppermute(lax.slice_in_dim(block, 0, width, axis=dim), axis, backward)
        block = jnp.concatenate([low, block, high], axis=dim)
    return block


def total_of_pieces(array, axis):
    return lax.all_gather(array, axis).sum(0)


def pair_terms(left_proj, right_proj, left_pos, right_pos, rate_row, channels, escale):
    contraction = jnp.einsum(
        "ikc,jkc->kij", left_proj, right_proj, preferred_element_type=jnp.float32
    ) / math.sqrt(channels)
    separation = left_pos[:, :, None] - right_pos[:, None, :]
    square = jnp.sum(separation * separation, axis=0)
    radial = jnp.exp(-rate_row[:, None, None] * square[None])
    weighted = radial * contraction
    latent = jnp.sum(weighted, axis=0)
    latent_slope = -jnp.sum(rate_row[:, None, None] * weighted, axis=0)
    latent_bend = jnp.sum((rate_row * rate_row)[:, None, None] * weighted, axis=0)
    gate_value = jax.nn.sigmoid(latent)
    first_deriv = gate_value * (1.0 + latent * (1.0 - gate_value))
    second_deriv = gate_value * (1.0 - gate_value) * (2.0 + latent * (1.0 - 2.0 * gate_value))
    first_term = escale * first_deriv * latent_slope
    second_term = escale * (second_deriv * latent_slope * latent_slope + first_deriv * latent_bend)
    return (separation, first_term, second_term)


def selector(neighbours, window_blocks, dtype):
    return (neighbours[:, None] == jnp.arange(window_blocks)[None, :]).astype(dtype)


def pick_bf16(neighbours, table):
    window_blocks = table.shape[0]
    flat = table.reshape(window_blocks, -1)
    picked = jnp.dot(
        selector(neighbours, window_blocks, table.dtype), flat, preferred_element_type=jnp.float32
    )
    return picked.astype(table.dtype).reshape((neighbours.shape[0],) + table.shape[1:])


def pick_f32(neighbours, table):
    window_blocks = table.shape[0]
    flat = table.reshape(window_blocks, -1)
    picked = jnp.dot(
        selector(neighbours, window_blocks, jnp.float32),
        flat,
        precision=lax.Precision.HIGHEST,
        preferred_element_type=jnp.float32,
    )
    return picked.reshape((neighbours.shape[0],) + table.shape[1:])


def body(positions, features, nbr_list, nbr_count, w_embed, w_proj, rates):
    owned_count = positions.shape[0]
    block_rows = positions.shape[2]
    channels = features.shape[2]
    bases = rates.shape[1]
    slot_count = nbr_list.shape[1]
    escale = 1.0 / math.sqrt(slot_count * block_rows)
    domains = lax.axis_size("space")
    members = lax.axis_size("member")
    domain = lax.axis_index("space")
    rate_row = rates[0]
    position_win = with_halo(positions, (("space", 0),), owned_count)
    feature_rows = with_halo(features, (("space", 0),), owned_count)
    block_count = feature_rows.shape[0]
    hidden = jax.nn.silu(
        jnp.dot(
            feature_rows.reshape(block_count * block_rows, channels),
            w_embed[0],
            preferred_element_type=jnp.float32,
        )
    ).astype(jnp.bfloat16)
    projected = jnp.dot(hidden, w_proj[0], preferred_element_type=jnp.float32).astype(jnp.bfloat16)
    window = projected.reshape(block_count, block_rows, bases * channels)
    local_index = jnp.mod(nbr_list - (domain - 1) * owned_count, domains * owned_count)
    in_use = (jnp.arange(slot_count)[None, :] < nbr_count[:, None]).astype(jnp.float32)

    def block_terms(block_index):
        neighbours = local_index[block_index]
        left_proj = lax.dynamic_index_in_dim(window, owned_count + block_index, 0, False).reshape(
            block_rows, bases, channels
        )
        right_proj = pick_bf16(neighbours, window).reshape(slot_count, block_rows, bases, channels)
        left_pos = lax.dynamic_index_in_dim(position_win, owned_count + block_index, 0, False)
        right_pos = pick_f32(neighbours, position_win)

        def one_slot(slot_proj, slot_pos):
            return pair_terms(left_proj, slot_proj, left_pos, slot_pos, rate_row, channels, escale)

        separation, first_term, second_term = jax.vmap(one_slot)(right_proj, right_pos)
        slot_mask = lax.dynamic_index_in_dim(in_use, block_index, 0, False)[:, None, None]
        return (separation, first_term * slot_mask, second_term * slot_mask)

    def force_block(block_index):
        separation, first_term, second_term = block_terms(block_index)
        forces = -2.0 * jnp.sum(first_term[:, None] * separation, axis=(0, 3))
        return (forces, first_term, second_term)

    block_ids = jnp.arange(owned_count)
    member_force, first_all, second_all = lax.map(force_block, block_ids)
    force_total = total_of_pieces(member_force, "member")
    mean_force = force_total / members
    tangent = 2.0 / members * (member_force - mean_force)
    tangent_win = with_halo(tangent, (("space", 0),), owned_count)

    def grad_block(block_index, first_term, second_term):
        neighbours = local_index[block_index]
        left_pos = lax.dynamic_index_in_dim(position_win, owned_count + block_index, 0, False)
        right_pos = pick_f32(neighbours, position_win)
        separation = left_pos[None, :, :, None] - right_pos[:, :, None, :]
        left_tangent = lax.dynamic_index_in_dim(tangent_win, owned_count + block_index, 0, False)
        right_tangent = pick_f32(neighbours, tangent_win)
        change = right_tangent[:, :, None, :] - left_tangent[None, :, :, None]
        radial_dot = jnp.sum(separation * change, axis=1)
        hessian_vec = (
            2.0 * first_term[:, None] * change
            + 4.0 * (second_term * radial_dot)[:, None] * separation
        )
        return jnp.sum(hessian_vec, axis=(0, 3))

    member_grad = lax.map(
        lambda packed: grad_block(packed[0], packed[1], packed[2]),
        (block_ids, first_all, second_all),
    )
    variance_grad = total_of_pieces(member_grad, "member")
    return (mean_force, variance_grad)


def solution(mesh):
    return jax.shard_map(
        body,
        mesh=mesh,
        in_specs=(
            P("space", None, None),
            P("space", None, None),
            P("space", None),
            P("space"),
            P("member", None, None),
            P("member", None, None),
            P("member", None),
        ),
        out_specs=(P("space", None, None), P("space", None, None)),
        check_vma=False,
    )
```

profile of v0, /device:TPU:1, one launch (start us, length us, event | category | flops | bytes accessed | tf_op | source)
XLA Modules:
  0.0 384.9 jit_solution(5127210774510682964)
XLA Ops:
  1.4 3.9 %collective-permute-start = (f32[16,3,128]{2,1,0:T(4,128)S(1)}, f32[16,3,128]{2,1,0:T(4,128)S(1)}, u32[]{:S(2)}, u32[]{:S(2)}) collective-permute-start(f32[16,3,128]{2,1,0:T(4,128)S(1)} %copy.61), channel_id=1, source_target_pairs={{0,4},{4,8},{8,12},{12,16},{16,20},{20,24},{24,28},{28,32},{32,36}... | collective-permute-start | bytes 73736 | tf_op jit(solution)/shard_map/ppermute | solution.py:15
  5.3 7.8 %collective-permute-start.1 = (f32[16,3,128]{2,1,0:T(4,128)S(1)}, f32[16,3,128]{2,1,0:T(4,128)S(1)}, u32[]{:S(2)}, u32[]{:S(2)}) collective-permute-start(f32[16,3,128]{2,1,0:T(4,128)S(1)} %copy.61), channel_id=1, source_target_pairs={{4,0},{8,4},{12,8},{16,12},{20,16},{24,20},{28,24},{32,28},{36,32}... | collective-permute-start | bytes 73736 | tf_op jit(solution)/shard_map/ppermute | solution.py:18
  13.1 2.3 collective-permute-start.3
  18.4 19.1 %collective-permute-done.3 = bf16[16,128,128]{2,1,0:T(8,128)(2,1)S(1)} collective-permute-done((bf16[16,128,128]{2,1,0:T(8,128)(2,1)}, bf16[16,128,128]{2,1,0:T(8,128)(2,1)S(1)}, u32[]{:S(2)}, u32[]{:S(2)}) %collective-permute-start.3) | collective-permute-done | bytes 524320 | tf_op jit(solution)/shard_map/ppermute | solution.py:18
  37.5 6.5 %collective-permute-done.2 = bf16[16,128,128]{2,1,0:T(8,128)(2,1)S(1)} collective-permute-done((bf16[16,128,128]{2,1,0:T(8,128)(2,1)}, bf16[16,128,128]{2,1,0:T(8,128)(2,1)S(1)}, u32[]{:S(2)}, u32[]{:S(2)}) %collective-permute-start.2) | collective-permute-done | bytes 524320 | tf_op jit(solution)/shard_map/ppermute | solution.py:15
  44.0 1.2 pad_maximum_fusion
  45.2 4.2 %convolution_convert_fusion.1 = bf16[6144,512]{1,0:T(8,128)(2,1)} fusion(bf16[1,128,512]{2,1,0:T(8,128)(2,1)S(1)} %copy-done, bf16[6144,128]{1,0:T(8,128)(2,1)S(1)} %bitcast.227, bf16[1,128,128]{2,1,0:T(8,128)(2,1)S(1)} %copy-done.1), kind=kOutput, calls=%fused_computation.70 | convolution fusion | flops 1013710848 | bytes 8028160 | tf_op jit(solution)/shard_map/dot_general | solution.py:92
  49.5 8.1 %reshape_reshape.6 = bf16[48,65536]{1,0:T(8,128)(2,1)} reshape(bf16[6144,512]{1,0:T(8,128)(2,1)} %convolution_convert_fusion.1) | data formatting | bytes 12582912 | tf_op jit(solution)/shard_map/while/body/eval_jaxpr/reshape;reshape | solution.py:52
  57.6 193.3 %while.30 = (s32[]{:T(128)}, f32[16,3,128]{2,1,0:T(4,128)S(1)}, f32[16,6,128,128]{3,2,1,0:T(8,128)}, f32[16,6,128,128]{3,2,1,0:T(8,128)}, f32[1,4,1,1]{1,3,2,0:T...) while((s32[]{:T(128)}, f32[16,3,128]{2,1,0:T(4,128)S(1)}, ...), condition=%wide.wide.region_6.7_spmd, body=%wide.wide.region_0.6_spmd.sunk | while | flops 147898944 | bytes 15729717 | solution.py:119
  61.8 3.8 convolution_convert_fusion.4
  65.6 1.1 reshape.287
  68.4 1.2 fusion.101
  73.9 3.8 convolution_convert_fusion.4
  77.7 1.1 reshape.287
  80.5 1.2 fusion.101
  86.0 3.8 convolution_convert_fusion.4
  89.7 1.1 reshape.287
  92.6 1.2 fusion.101
  98.1 3.8 convolution_convert_fusion.4
  101.8 1.1 reshape.287
  104.7 1.2 fusion.101
  110.2 3.8 convolution_convert_fusion.4
  113.9 1.1 reshape.287
  116.8 1.2 fusion.101
  122.2 3.8 convolution_convert_fusion.4
  126.0 1.1 reshape.287
  128.8 1.2 fusion.101
  134.3 3.8 convolution_convert_fusion.4
  138.0 1.1 reshape.287
  140.9 1.2 fusion.101
  146.3 3.8 convolution_convert_fusion.4
  150.1 1.1 reshape.287
  153.0 1.2 fusion.101
  158.4 3.8 convolution_convert_fusion.4
  162.2 1.1 reshape.287
  165.1 1.2 fusion.101
  170.5 3.8 convolution_convert_fusion.4
  174.3 1.1 reshape.287
  177.1 1.2 fusion.101
  182.6 3.8 convolution_convert_fusion.4
  186.4 1.1 reshape.287
  189.2 1.2 fusion.101
  194.7 3.8 convolution_convert_fusion.4
  198.4 1.1 reshape.287
  201.3 1.2 fusion.101
  206.8 3.8 convolution_convert_fusion.4
  210.5 1.1 reshape.287
  213.4 1.2 fusion.101
  218.9 3.8 convolution_convert_fusion.4
  222.6 1.1 reshape.287
  225.5 1.2 fusion.101
  230.9 3.8 convolution_convert_fusion.4
  234.7 1.1 reshape.287
  237.6 1.2 fusion.101
  243.0 3.8 convolution_convert_fusion.4
  246.8 1.1 reshape.287
  249.6 1.2 fusion.101
  250.9 7.7 %all-gather = f32[64,3,128]{2,0,1:T(8,128)S(1)} all-gather(f32[16,3,128]{2,0,1:T(8,128)S(1)} %copy.66), channel_id=2, replica_groups=mesh['space'=64,'member'=4] {'member'}, dimensions={0}, use_global_device_ids=true | all-gather | bytes 122880 | tf_op jit(solution)/shard_map/all_gather | solution.py:24
  259.6 1.4 collective-permute-start.4
  262.4 6.4 %collective-permute-done.4 = f32[16,3,128]{2,1,0:T(4,128)S(1)} collective-permute-done((f32[16,3,128]{2,1,0:T(4,128)S(1)}, f32[16,3,128]{2,1,0:T(4,128)S(1)}, u32[]{:S(2)}, u32[]{:S(2)}) %collective-permute-start.4) | collective-permute-done | bytes 24608 | tf_op jit(solution)/shard_map/ppermute | solution.py:15
  268.8 108.7 %while.29 = (s32[]{:T(128)}, f32[16,3,128]{2,0,1:T(8,128)S(1)}, f32[16,6,128,128]{3,2,1,0:T(8,128)}, s32[16]{0:T(128)S(1)}, s32[16,6]{1,0:T(8,128)S(1)}, /*index...) while((s32[]{:T(128)}, f32[16,3,128]{2,0,1:T(8,128)S(1)}, ...), condition=%wide.region_11.12_spmd, body=%wide.region_8.11_spmd.sunk | while | flops 5800136 | bytes 3405633 | solution.py:140
  273.0 1.1 fusion.91
  279.8 1.1 fusion.91
  377.6 6.7 %all-gather.1 = f32[64,3,128]{2,0,1:T(8,128)S(1)} all-gather(f32[16,3,128]{2,0,1:T(8,128)S(1)} %get-tuple-element.265), channel_id=3, replica_groups=mesh['space'=64,'member'=4] {'member'}, dimensions={0}, use_global_device_ids=true | all-gather | bytes 122880 | tf_op jit(solution)/shard_map/all_gather | solution.py:24
  (445 shorter events, 121.4 us)
Async XLA Ops:
  0.6 44.6 %copy-start = (bf16[1,128,512]{2,1,0:T(8,128)(2,1)S(1)}, bf16[1,128,512]{2,1,0:T(8,128)(2,1)}, u32[]{:S(2)}) copy-start(bf16[1,128,512]{2,1,0:T(8,128)(2,1)} %param.16) | copy-start | bytes 393220
  1.4 16.2 %collective-permute-start = (f32[16,3,128]{2,1,0:T(4,128)S(1)}, f32[16,3,128]{2,1,0:T(4,128)S(1)}, u32[]{:S(2)}, u32[]{:S(2)}) collective-permute-start(f32[16,3,128]{2,1,0:T(4,128)S(1)} %copy.61), channel_id=1, source_target_pairs={{0,4},{4,8},{8,12},{12,16},{16,20},{20,24},{24,28},{28,32},{32,36}... | collective-permute-start | bytes 73736 | tf_op jit(solution)/shard_map/ppermute | solution.py:15
  5.3 13.1 %collective-permute-start.1 = (f32[16,3,128]{2,1,0:T(4,128)S(1)}, f32[16,3,128]{2,1,0:T(4,128)S(1)}, u32[]{:S(2)}, u32[]{:S(2)}) collective-permute-start(f32[16,3,128]{2,1,0:T(4,128)S(1)} %copy.61), channel_id=1, source_target_pairs={{4,0},{8,4},{12,8},{16,12},{20,16},{24,20},{28,24},{32,28},{36,32}... | collective-permute-start | bytes 73736 | tf_op jit(solution)/shard_map/ppermute | solution.py:18
  13.1 24.4 %collective-permute-start.3 = (bf16[16,128,128]{2,1,0:T(8,128)(2,1)}, bf16[16,128,128]{2,1,0:T(8,128)(2,1)S(1)}, u32[]{:S(2)}, u32[]{:S(2)}) collective-permute-start(bf16[16,128,128]{2,1,0:T(8,128)(2,1)} %param.12), channel_id=1, source_target_pairs={{4,0},{8,4},{12,8},{16,12},{20,16},{24,20},{28,24},{32,28},{36,32}... | collective-permute-start | bytes 1572872 | tf_op jit(solution)/shard_map/ppermute | solution.py:18
  15.4 28.6 %collective-permute-start.2 = (bf16[16,128,128]{2,1,0:T(8,128)(2,1)}, bf16[16,128,128]{2,1,0:T(8,128)(2,1)S(1)}, u32[]{:S(2)}, u32[]{:S(2)}) collective-permute-start(bf16[16,128,128]{2,1,0:T(8,128)(2,1)} %param.12), channel_id=1, source_target_pairs={{0,4},{4,8},{8,12},{12,16},{16,20},{20,24},{24,28},{28,32},{32,36}... | collective-permute-start | bytes 1572872 | tf_op jit(solution)/shard_map/ppermute | solution.py:15
  18.4 26.8 %copy-start.1 = (bf16[1,128,128]{2,1,0:T(8,128)(2,1)S(1)}, bf16[1,128,128]{2,1,0:T(8,128)(2,1)}, u32[]{:S(2)}) copy-start(bf16[1,128,128]{2,1,0:T(8,128)(2,1)} %param.15) | copy-start | bytes 98308
  49.5 8.1 %copy-start.2 = (f32[1,4]{1,0:T(1,128)S(1)}, f32[1,4]{1,0:T(1,128)}, u32[]{:S(2)}) copy-start(f32[1,4]{1,0:T(1,128)} %param.17) | copy-start | bytes 52
  258.6 3.8 collective-permute-start.5
  259.6 9.2 %collective-permute-start.4 = (f32[16,3,128]{2,1,0:T(4,128)S(1)}, f32[16,3,128]{2,1,0:T(4,128)S(1)}, u32[]{:S(2)}, u32[]{:S(2)}) collective-permute-start(f32[16,3,128]{2,1,0:T(4,128)S(1)} %get-tuple-element.376), channel_id=1, source_target_pairs={{0,4},{4,8},{8,12},{12,16},{16,20},{20,24},{24,28},{28,32},{32,36}... | collective-permute-start | bytes 73736 | tf_op jit(solution)/shard_map/ppermute | solution.py:15
where the time goes:
time: 389 us; the launch traced here: 385 us
  loops' own time  88.1 us (23%)
  matrix products  87 us (22%)
  other arithmetic  78.4 us (20%)
  local copies, waits for them, and re-layouts  67.1 us (17%)
  waiting for transfers between devices  32.7 us (8%)
  starting transfers between devices  16.5 us (4%)
  blocking collectives  14.3 us (4%)
    dot_general x16, matrix products, pick_bf16(): jnp.dot(selector(neighbours, window_blocks, table.dtype), flat, preferred...  60.1 us
    another operation x1, loops' own time, body(): lax.map(lambda packed: grad_block(packed[0], packed[1], packed[2]), (bloc...  45.3 us
    another operation x1, loops' own time, body(): member_force, first_all, second_all = lax.map(force_block, block_ids)  42.8 us
    dynamic_slice x32, local copies, waits for them, and re-layouts, body(): member_force, first_all, second_all = lax.map(force_block, block_ids)  20 us
    ppermute x3, waiting for transfers between devices, with_halo(): lax.ppermute(lax.slice_in_dim(block, 0, width, axis=dim), axis, backward)  19.8 us
    dynamic_update_slice x32, other arithmetic, body(): member_force, first_all, second_all = lax.map(force_block, block_ids)  19.7 us
    reshape x16, local copies, waits for them, and re-layouts, block_terms(): pick_bf16(neighbours, window)  17.8 us
    mul x16, other arithmetic, grad_block(): 4.0 * (second_term * radial_dot)[:, None] * separation  17 us
  transfers between devices with their start and end apart: 6, of which 4 were waited for; matrix products, arithmetic and copies ran while one was open for 1% of the time, Pallas kernels for 0%

commit v1 on v0

v1 whole, which is shorter than its diff:
```python
import math

import jax
import jax.numpy as jnp
from jax import lax
from jax.experimental import pallas as pl
from jax.experimental.pallas import tpu as pltpu
from jax.sharding import PartitionSpec as P

STEP_BLOCKS = 4
CHUNK = 32
LOG2E = 1.4426950408889634


def ring(axis, shift):
    count = lax.axis_size(axis)
    return [(i, (i + shift) % count) for i in range(count)]


def flip(axis, bit):
    return [(i, i ^ bit) for i in range(lax.axis_size(axis))]


def columns(tile):
    rows = jnp.concatenate([tile, jnp.zeros((8 - tile.shape[0], tile.shape[1]), jnp.float32)], axis=0)
    return jnp.transpose(rows)


def pair_kernel(
    idx_ref, cnt_ref, rate_ref, core_ref,
    own_ref, lo_a, lo_b, hi_a, hi_b, embed_ref, wproj_ref,
    pos_own, pos_lo, pos_hi,
    force_ref, first_ref, second_ref,
    proj_ref, col_ref,
):
    owned = own_ref.shape[0]
    half = lo_a.shape[0]
    slots = first_ref.shape[1]
    rows = first_ref.shape[2]
    channels = own_ref.shape[2]
    bases = wproj_ref.shape[1] // channels
    escale = 1.0 / math.sqrt(slots * rows)
    sigma = 1.0 / math.sqrt(channels)
    step = pl.program_id(0)

    @pl.when(step == 0)
    def _():
        def project(source, base):
            def one(i, carry):
                x = source[pl.ds(2 * i, 2)].reshape(2 * rows, channels)
                h = jnp.dot(x, embed_ref[...], preferred_element_type=jnp.float32)
                half_h = 0.5 * h
                hidden = (half_h + half_h * jnp.tanh(half_h)).astype(jnp.bfloat16)
                out = jnp.dot(hidden, wproj_ref[...], preferred_element_type=jnp.float32)
                proj_ref[pl.ds(base + 2 * i, 2)] = out.astype(jnp.bfloat16).reshape(2, rows, bases * channels)
                return carry

            lax.fori_loop(0, source.shape[0] // 2, one, 0, unroll=2)

        core = core_ref[0]
        near = core * half
        far = half - near
        project(own_ref, owned)
        project(lo_a, near)
        project(lo_b, far)
        project(hi_a, 2 * owned + near)
        project(hi_b, 2 * owned + far)

        def spread(source, base):
            def one(i, carry):
                col_ref[base + i] = columns(source[i])
                return carry

            lax.fori_loop(0, owned, one, 0, unroll=4)

        spread(pos_lo, 0)
        spread(pos_own, owned)
        spread(pos_hi, 2 * owned)

    decay = [-LOG2E * rate_ref[k] for k in range(bases)]
    slope_coef = [(-2.0 * sigma) * rate_ref[k] for k in range(bases)]
    bend_coef = [(4.0 * sigma) * rate_ref[k] * rate_ref[k] for k in range(bases)]

    for part in range(STEP_BLOCKS):
        block = step * STEP_BLOCKS + part
        count = cnt_ref[block]

        def run(live, block=block, part=part):
            left = proj_ref[owned + block]
            left_pos = [pos_own[block, pl.ds(a, 1), :] for a in range(3)]
            total = [jnp.zeros((8, rows), jnp.float32) for _ in range(3)]
            for slot in range(live):
                source = idx_ref[block * slots + slot]
                dots = [
                    lax.dot_general(
                        proj_ref[source, :, k * channels:(k + 1) * channels],
                        left[:, k * channels:(k + 1) * channels],
                        (((1,), (1,)), ((), ())),
                        preferred_element_type=jnp.float32,
                    )
                    for k in range(bases)
                ]
                for start in range(0, rows, CHUNK):
                    cols = col_ref[source, start:start + CHUNK, :]
                    delta = [left_pos[a] - cols[:, a:a + 1] for a in range(3)]
                    square = delta[0] * delta[0] + delta[1] * delta[1] + delta[2] * delta[2]
                    w = [
                        jnp.exp2(decay[k] * square) * dots[k][start:start + CHUNK]
                        for k in range(bases)
                    ]
                    lh = (0.5 * sigma) * sum(w[1:], w[0])
                    slope = sum([slope_coef[k] * w[k] for k in range(1, bases)], slope_coef[0] * w[0])
                    bend = sum([bend_coef[k] * w[k] for k in range(1, bases)], bend_coef[0] * w[0])
                    h = jnp.tanh(lh)
                    u = 1.0 - h * h
                    p1 = (1.0 + h) + lh * u
                    p2 = u * (1.0 - lh * h)
                    first = p1 * slope
                    second = p2 * (slope * slope) + p1 * bend
                    first_ref[part, slot, start:start + CHUNK, :] = first
                    second_ref[part, slot, start:start + CHUNK, :] = second
                    for a in range(3):
                        total[a] = total[a] + jnp.sum((first * delta[a]).reshape(CHUNK // 8, 8, rows), axis=0)
            force_ref[part] = jnp.concatenate(
                [(-0.5 * escale) * jnp.sum(t, axis=0, keepdims=True) for t in total], axis=0
            )

        for live in range(3, slots + 1):
            pl.when(count == live)(lambda live=live: run(live))


def grad_kernel(
    idx_ref, cnt_ref, pos_own, pos_lo, pos_hi, tan_own, tan_lo, tan_hi, first_ref, second_ref,
    grad_ref, col_ref,
):
    owned = pos_own.shape[0]
    slots = first_ref.shape[1]
    rows = first_ref.shape[2]
    escale = 1.0 / math.sqrt(slots * rows)
    step = pl.program_id(0)

    @pl.when(step == 0)
    def _():
        def spread(pos, tan, base):
            def one(i, carry):
                col_ref[base + i] = columns(jnp.concatenate([pos[i], tan[i]], axis=0))
                return carry

            lax.fori_loop(0, owned, one, 0, unroll=4)

        spread(pos_lo, tan_lo, 0)
        spread(pos_own, tan_own, owned)
        spread(pos_hi, tan_hi, 2 * owned)

    for part in range(STEP_BLOCKS):
        block = step * STEP_BLOCKS + part
        count = cnt_ref[block]

        def run(live, block=block, part=part):
            left_pos = [pos_own[block, pl.ds(a, 1), :] for a in range(3)]
            left_tan = [tan_own[block, pl.ds(a, 1), :] for a in range(3)]
            total = [jnp.zeros((8, rows), jnp.float32) for _ in range(3)]
            for slot in range(live):
                source = idx_ref[block * slots + slot]
                for start in range(0, rows, CHUNK):
                    cols = col_ref[source, start:start + CHUNK, :]
                    delta = [left_pos[a] - cols[:, a:a + 1] for a in range(3)]
                    change = [cols[:, 3 + a:4 + a] - left_tan[a] for a in range(3)]
                    first = first_ref[part, slot, start:start + CHUNK, :]
                    second = second_ref[part, slot, start:start + CHUNK, :]
                    along = second * (delta[0] * change[0] + delta[1] * change[1] + delta[2] * change[2])
                    for a in range(3):
                        term = first * change[a] + along * delta[a]
                        total[a] = total[a] + jnp.sum(term.reshape(CHUNK // 8, 8, rows), axis=0)
            grad_ref[part] = jnp.concatenate(
                [(0.5 * escale) * jnp.sum(t, axis=0, keepdims=True) for t in total], axis=0
            )

        for live in range(3, slots + 1):
            pl.when(count == live)(lambda live=live: run(live))


def whole(array):
    return pl.BlockSpec(array.shape, lambda *_: (0,) * array.ndim, pipeline_mode=pl.Buffered(1))


def stepped(shape):
    return pl.BlockSpec((STEP_BLOCKS,) + shape, lambda i, *_: (i,) + (0,) * len(shape))


def member_sum(array):
    size = lax.axis_size("member")
    others = [lax.ppermute(array, "member", flip("member", bit)) for bit in range(1, size)]
    return array + others[0] + (others[1] + others[2])


def body(positions, features, nbr_list, nbr_count, w_embed, w_proj, rates):
    owned, dims, rows = positions.shape
    channels = features.shape[2]
    slots = nbr_list.shape[1]
    width = w_proj.shape[2]
    domains = lax.axis_size("space")
    members = lax.axis_size("member")
    domain = lax.axis_index("space")
    core = lax.axis_index("member") % 2
    up, down = ring("space", 1), ring("space", -1)
    half = owned // 2

    mine = lax.dynamic_slice_in_dim(features, core * half, half, 0)
    lo_a = lax.ppermute(mine, "space", up)
    hi_a = lax.ppermute(mine, "space", down)
    pos_lo = lax.ppermute(positions, "space", up)
    pos_hi = lax.ppermute(positions, "space", down)
    swap = flip("member", 1)
    lo_b = lax.ppermute(lo_a, "member", swap)
    hi_b = lax.ppermute(hi_a, "member", swap)

    index = jnp.mod(nbr_list - (domain - 1) * owned, domains * owned).reshape(-1)
    core_arr = core.astype(jnp.int32).reshape(1)
    pairs = jax.ShapeDtypeStruct((owned, slots, rows, rows), jnp.float32)
    small = jax.ShapeDtypeStruct((owned, dims, rows), jnp.float32)
    tensors = (features, lo_a, lo_b, hi_a, hi_b, w_embed[0], w_proj[0], positions, pos_lo, pos_hi)
    force, first, second = pl.pallas_call(
        pair_kernel,
        grid_spec=pltpu.PrefetchScalarGridSpec(
            num_scalar_prefetch=4,
            grid=(owned // STEP_BLOCKS,),
            in_specs=[whole(t) for t in tensors],
            out_specs=[stepped((dims, rows)), stepped((slots, rows, rows)), stepped((slots, rows, rows))],
            scratch_shapes=[
                pltpu.VMEM((3 * owned, rows, width), jnp.bfloat16),
                pltpu.VMEM((3 * owned, rows, 8), jnp.float32),
            ],
        ),
        out_shape=[small, pairs, pairs],
        name="pair_forces",
    )(index, nbr_count, rates[0], core_arr, *tensors)

    mean_force = member_sum(force) / members
    tangent = (2.0 / members) * (force - mean_force)
    tan_lo = lax.ppermute(tangent, "space", up)
    tan_hi = lax.ppermute(tangent, "space", down)
    tensors = (positions, pos_lo, pos_hi, tangent, tan_lo, tan_hi)
    grad = pl.pallas_call(
        grad_kernel,
        grid_spec=pltpu.PrefetchScalarGridSpec(
            num_scalar_prefetch=2,
            grid=(owned // STEP_BLOCKS,),
            in_specs=[whole(t) for t in tensors] + [stepped((slots, rows, rows))] * 2,
            out_specs=stepped((dims, rows)),
            scratch_shapes=[pltpu.VMEM((3 * owned, rows, 8), jnp.float32)],
        ),
        out_shape=small,
        name="variance_gradient",
    )(index, nbr_count, *tensors, first, second)
    return (mean_force, member_sum(grad))


def solution(mesh):
    return jax.shard_map(
        body,
        mesh=mesh,
        in_specs=(
            P("space", None, None),
            P("space", None, None),
            P("space", None),
            P("space"),
            P("member", None, None),
            P("member", None, None),
            P("member", None),
        ),
        out_specs=(P("space", None, None), P("space", None, None)),
        check_vma=False,
    )
```

time: 389 us -> 112 us (0.29)
  loops' own time: 88.1 us -> 0 us
  matrix products: 87 us -> 0 us
  other arithmetic: 78.4 us -> 2.26 us
  local copies, waits for them, and re-layouts: 67.1 us -> 5 us
  Pallas kernels: 0 us -> 41.6 us
  blocking collectives: 14.3 us -> 0 us
  starting transfers between devices: 16.5 us -> 26.3 us
    another operation x2 -> x0, loops' own time: 88.1 us -> none  [the longest x1 45.3 us: body(): lax.map(lambda packed: grad_block(packed[0], packed[1], packed[2]), (bloc...]
    dot_general x81 -> x0, matrix products: 87 us -> none  [the longest x16 60.1 us: pick_bf16(): jnp.dot(selector(neighbours, window_blocks, table.dtype), flat, preferred...]
    pallas_call x0 -> x2, Pallas kernels: none -> 41.6 us  [the longest x1 25.4 us: body(): pl.pallas_call(pair_kernel, grid_spec=pltpu.PrefetchScalarGridSpec(num_sc...]
    mul x66 -> x1, other arithmetic: 37.1 us -> 0.78 us  [body(): tangent = 2.0 / members * (force - mean_force)]
    dynamic_slice x64 -> x1, local copies, waits for them, and re-layouts: 36.6 us -> 0.97 us  [body(): mine = lax.dynamic_slice_in_dim(features, core * half, half, 0)]
    dynamic_update_slice x32 -> x0, other arithmetic: 19.7 us -> none  [body(): member_force, first_all, second_all = lax.map(force_block, block_ids)]
    reduce_sum x66 -> x0, other arithmetic: 19.6 us -> none  [the longest x16 8.14 us: grad_block(): return jnp.sum(hessian_vec, axis=(0, 3))]
    reshape x16 -> x1, local copies, waits for them, and re-layouts: 17.8 us -> 0.6 us  [body(): jnp.mod(nbr_list - (domain - 1) * owned, domains * owned).reshape(-1)]
  transfers between devices with their start and end apart: 6 -> 14, of which waited for: 4 -> 9; matrix products, arithmetic and copies ran while one was open for 1% -> 2% of each run, Pallas kernels for 0% -> 0%
where the time goes in v1:
time: 112 us
  Pallas kernels  41.6 us (37%)
  waiting for transfers between devices  35.9 us (32%)
  starting transfers between devices  26.3 us (23%)
  local copies, waits for them, and re-layouts  5 us (4%)
  other arithmetic  2.26 us (2%)
    pallas_call x1, Pallas kernels, body(): pl.pallas_call(pair_kernel, grid_spec=pltpu.PrefetchScalarGridSpec(num_sc...  25.4 us
    pallas_call x1, Pallas kernels, body(): pl.pallas_call(grad_kernel, grid_spec=pltpu.PrefetchScalarGridSpec(num_sc...  16.1 us
    ppermute x1, starting transfers between devices, body(): hi_a = lax.ppermute(mine, 'space', down)  11.6 us
    ppermute x1, waiting for transfers between devices, body(): hi_a = lax.ppermute(mine, 'space', down)  10.5 us
    ppermute x1, waiting for transfers between devices, body(): tan_lo = lax.ppermute(tangent, 'space', up)  7.89 us
    ppermute x1, waiting for transfers between devices, body(): pos_lo = lax.ppermute(positions, 'space', up)  6.65 us
    ppermute x6, starting transfers between devices, member_sum(): lax.ppermute(array, 'member', flip('member', bit))  6.26 us
    ppermute x1, waiting for transfers between devices, body(): lo_a = lax.ppermute(mine, 'space', up)  5.54 us
  transfers between devices with their start and end apart: 14, of which 9 were waited for; matrix products, arithmetic and copies ran while one was open for 2% of the time, Pallas kernels for 0%

profile of v1, /device:TPU:1, one launch (start us, length us, event | category | flops | bytes accessed | tf_op | source)
XLA Modules:
  0.0 111.7 jit_solution(8912560159750678712)
XLA Ops:
  0.6 1.0 constant_dynamic-slice_fusion
  1.6 11.6 %collective-permute-start.2 = (bf16[8,128,128]{2,1,0:T(8,128)(2,1)S(1)}, bf16[8,128,128]{2,1,0:T(8,128)(2,1)S(1)}, u32[]{:S(2)}, u32[]{:S(2)}) collective-permute-start(bf16[8,128,128]{2,1,0:T(8,128)(2,1)S(1)} %constant_dynamic-slice_fusion), channel_id=1, source_target_pairs={{0,252},{4,0},{8,4},{12,8},{16,12},{20,16},{24,20},{28,24},{32,28}... | collective-permute-start | bytes 786440 | tf_op jit(solution)/shard_map/ppermute | solution.py:211
  13.2 0.0 collective-permute-start
  13.2 10.5 %collective-permute-done.2.hi_a = bf16[8,128,128]{2,1,0:T(8,128)(2,1)S(1)} collective-permute-done((bf16[8,128,128]{2,1,0:T(8,128)(2,1)S(1)}, bf16[8,128,128]{2,1,0:T(8,128)(2,1)S(1)}, u32[]{:S(2)}, u32[]{:S(2)}) %collective-permute-start.2) | collective-permute-done | bytes 262176 | tf_op jit(solution)/shard_map/ppermute | solution.py:211
  23.7 0.0 copy-start.1
  23.7 1.6 %collective-permute-start.3 = (bf16[8,128,128]{2,1,0:T(8,128)(2,1)S(1)}, bf16[8,128,128]{2,1,0:T(8,128)(2,1)S(1)}, u32[]{:S(2)}, u32[]{:S(2)}) collective-permute-start(bf16[8,128,128]{2,1,0:T(8,128)(2,1)S(1)} %collective-permute-done.2.hi_a), channel_id=1, source_target_pairs={{0,1},{1,0},{2,3},{3,2},{4,5},{5,4},{6,7},{7,6},{8,9},{9,8},{10,11... | collective-permute-start | bytes 786440 | tf_op jit(solution)/shard_map/ppermute | solution.py:216
  25.3 5.5 %collective-permute-done.lo_a = bf16[8,128,128]{2,1,0:T(8,128)(2,1)S(1)} collective-permute-done((bf16[8,128,128]{2,1,0:T(8,128)(2,1)S(1)}, bf16[8,128,128]{2,1,0:T(8,128)(2,1)S(1)}, u32[]{:S(2)}, u32[]{:S(2)}) %collective-permute-start) | collective-permute-done | bytes 262176 | tf_op jit(solution)/shard_map/ppermute | solution.py:210
  30.9 0.0 copy-start.2
  30.9 1.9 %collective-permute-start.1 = (bf16[8,128,128]{2,1,0:T(8,128)(2,1)S(1)}, bf16[8,128,128]{2,1,0:T(8,128)(2,1)S(1)}, u32[]{:S(2)}, u32[]{:S(2)}) collective-permute-start(bf16[8,128,128]{2,1,0:T(8,128)(2,1)S(1)} %collective-permute-done.lo_a), channel_id=1, source_target_pairs={{0,1},{1,0},{2,3},{3,2},{4,5},{5,4},{6,7},{7,6},{8,9},{9,8},{10,11... | collective-permute-start | bytes 786440 | tf_op jit(solution)/shard_map/ppermute | solution.py:215
  32.8 0.8 copy.19.pos_own
  33.5 0.0 copy-start
  33.5 1.3 %collective-permute-start.5 = (f32[16,3,128]{2,1,0:T(4,128)S(1)}, f32[16,3,128]{2,1,0:T(4,128)S(1)}, u32[]{:S(2)}, u32[]{:S(2)}) collective-permute-start(f32[16,3,128]{2,1,0:T(4,128)S(1)} %copy.19.pos_own), channel_id=1, source_target_pairs={{0,252},{4,0},{8,4},{12,8},{16,12},{20,16},{24,20},{28,24},{32,28}... | collective-permute-start | bytes 73736 | tf_op jit(solution)/shard_map/ppermute | solution.py:213
  34.8 1.1 %collective-permute-start.4 = (f32[16,3,128]{2,1,0:T(4,128)S(1)}, f32[16,3,128]{2,1,0:T(4,128)S(1)}, u32[]{:S(2)}, u32[]{:S(2)}) collective-permute-start(f32[16,3,128]{2,1,0:T(4,128)S(1)} %copy.19.pos_own), channel_id=1, source_target_pairs={{0,4},{4,8},{8,12},{12,16},{16,20},{20,24},{24,28},{28,32},{32,36}... | collective-permute-start | bytes 73736 | tf_op jit(solution)/shard_map/ppermute | solution.py:212
  36.0 0.7 add_select_fusion
  36.7 0.1 copy.16
  36.7 0.6 reshape.10.idx_ref
  37.3 0.0 collective-permute-done.5.pos_hi
  37.4 0.0 copy-start.5
  37.4 6.7 %collective-permute-done.4.pos_lo = f32[16,3,128]{2,1,0:T(4,128)S(1)} collective-permute-done((f32[16,3,128]{2,1,0:T(4,128)S(1)}, f32[16,3,128]{2,1,0:T(4,128)S(1)}, u32[]{:S(2)}, u32[]{:S(2)}) %collective-permute-start.4) | collective-permute-done | bytes 24608 | tf_op jit(solution)/shard_map/ppermute | solution.py:212
  44.0 0.0 copy-start.6
  44.0 0.0 collective-permute-done.3.hi_b
  44.0 0.0 copy-start.3
  44.0 0.0 collective-permute-done.1.lo_b
  44.0 0.0 copy-start.4
  44.0 0.0 copy-done.1
  44.0 0.0 copy-done.2
  44.1 0.0 copy-done
  44.1 0.0 copy-done.5
  44.1 0.5 copy-done.6
  44.6 0.1 copy-done.3
  44.7 0.1 copy-done.4
  44.8 25.4 %pair_forces.1 = (f32[16,3,128]{2,1,0:T(4,128)}, f32[16,6,128,128]{3,2,1,0:T(8,128)}, f32[16,6,128,128]{3,2,1,0:T(8,128)}) custom-call(s32[96]{0:T(128)} %reshape.10.idx_ref, s32[16]{0:T(128)} %cnt_ref.3, f32[4]{0:T(128)} %bitcast.6, s32[1]{0:T(128)} %bitcast.1.core_ref, bf16[16,128,128]{2,1,0:T(8,128)(2,1)} %own_ref.1, bf16[8,128,128]{2,1,0:T(8,128)(2,1)} %copy-done.2, ...), custom_call_target="tpu_custom_call" | custom-call | tf_op jit(solution)/shard_map/pair_forces/pallas_call | solution.py:223
  70.2 2.0 %collective-permute-start.8 = (f32[16,3,128]{2,1,0:T(4,128)}, f32[16,3,128]{2,1,0:T(4,128)S(1)}, u32[]{:S(2)}, u32[]{:S(2)}) collective-permute-start(f32[16,3,128]{2,1,0:T(4,128)} %get-tuple-element.5), channel_id=1, source_target_pairs={{0,3},{1,2},{2,1},{3,0},{4,7},{5,6},{6,5},{7,4},{8,11},{9,10},{10,... | collective-permute-start | bytes 73736 | tf_op jit(solution)/shard_map/ppermute | solution.py:193
  72.2 1.1 collective-permute-start.7
  73.3 0.0 collective-permute-start.6
  73.3 0.7 collective-permute-done.8
  74.0 1.5 %collective-permute-done.7 = f32[16,3,128]{2,1,0:T(4,128)S(1)} collective-permute-done((f32[16,3,128]{2,1,0:T(4,128)}, f32[16,3,128]{2,1,0:T(4,128)S(1)}, u32[]{:S(2)}, u32[]{:S(2)}) %collective-permute-start.7) | collective-permute-done | bytes 24608 | tf_op jit(solution)/shard_map/ppermute | solution.py:193
  75.6 0.0 collective-permute-done.6
  75.6 0.8 subtract_multiply_fusion
  76.4 0.0 copy-start.7
  76.4 2.5 %collective-permute-start.10 = (f32[16,3,128]{2,1,0:T(4,128)S(1)}, f32[16,3,128]{2,1,0:T(4,128)S(1)}, u32[]{:S(2)}, u32[]{:S(2)}) collective-permute-start(f32[16,3,128]{2,1,0:T(4,128)S(1)} %get-tuple-element.12.tan_own), channel_id=1, source_target_pairs={{0,252},{4,0},{8,4},{12,8},{16,12},{20,16},{24,20},{28,24},{32,28}... | collective-permute-start | bytes 73736 | tf_op jit(solution)/shard_map/ppermute | solution.py:242
  78.9 0.0 collective-permute-start.9
  78.9 1.2 %collective-permute-done.10.tan_hi = f32[16,3,128]{2,1,0:T(4,128)S(1)} collective-permute-done((f32[16,3,128]{2,1,0:T(4,128)S(1)}, f32[16,3,128]{2,1,0:T(4,128)S(1)}, u32[]{:S(2)}, u32[]{:S(2)}) %collective-permute-start.10) | collective-permute-done | bytes 24608 | tf_op jit(solution)/shard_map/ppermute | solution.py:242
  80.1 0.0 copy-start.8
  80.1 7.9 %collective-permute-done.9.tan_lo = f32[16,3,128]{2,1,0:T(4,128)S(1)} collective-permute-done((f32[16,3,128]{2,1,0:T(4,128)S(1)}, f32[16,3,128]{2,1,0:T(4,128)S(1)}, u32[]{:S(2)}, u32[]{:S(2)}) %collective-permute-start.9) | collective-permute-done | bytes 24608 | tf_op jit(solution)/shard_map/ppermute | solution.py:241
  88.0 0.0 copy-start.9
  88.0 0.0 copy-done.7
  88.0 0.0 copy-done.8
  88.0 0.6 copy-done.9
  88.6 16.1 %variance_gradient.1 = f32[16,3,128]{2,1,0:T(4,128)} custom-call(s32[96]{0:T(128)} %reshape.10.idx_ref, s32[16]{0:T(128)} %cnt_ref.3, f32[16,3,128]{2,1,0:T(4,128)} %copy-done, f32[16,3,128]{2,1,0:T(4,128)} %copy-done.6, f32[16,3,128]{2,1,0:T(4,128)} %copy-done.5, f32[16,3,128]{2,1,0:T(4,128)} %copy-done.7, f32[16,3,128]{2,1,0:T(4,128)} %copy-done.9, ...), custom_call_target="tpu_custom_call" | custom-call | tf_op jit(solution)/shard_map/variance_gradient/pallas_call | solution.py:244
  104.8 2.2 %collective-permute-start.13 = (f32[16,3,128]{2,1,0:T(4,128)}, f32[16,3,128]{2,1,0:T(4,128)S(1)}, u32[]{:S(2)}, u32[]{:S(2)}) collective-permute-start(f32[16,3,128]{2,1,0:T(4,128)} %variance_gradient.1), channel_id=1, source_target_pairs={{0,3},{1,2},{2,1},{3,0},{4,7},{5,6},{6,5},{7,4},{8,11},{9,10},{10,... | collective-permute-start | bytes 73736 | tf_op jit(solution)/shard_map/ppermute | solution.py:193
  106.9 1.0 collective-permute-start.12
  107.9 0.0 collective-permute-start.11
  107.9 0.6 copy.21
  108.6 0.2 collective-permute-done.13
  108.7 1.6 %collective-permute-done.12 = f32[16,3,128]{2,1,0:T(4,128)S(1)} collective-permute-done((f32[16,3,128]{2,1,0:T(4,128)}, f32[16,3,128]{2,1,0:T(4,128)S(1)}, u32[]{:S(2)}, u32[]{:S(2)}) %collective-permute-start.12) | collective-permute-done | bytes 24608 | tf_op jit(solution)/shard_map/ppermute | solution.py:193
  110.3 0.0 collective-permute-done.11
  110.3 0.8 add_add_fusion
  111.1 0.6 copy.22
Async XLA Ops:
  1.6 22.1 %collective-permute-start.2 = (bf16[8,128,128]{2,1,0:T(8,128)(2,1)S(1)}, bf16[8,128,128]{2,1,0:T(8,128)(2,1)S(1)}, u32[]{:S(2)}, u32[]{:S(2)}) collective-permute-start(bf16[8,128,128]{2,1,0:T(8,128)(2,1)S(1)} %constant_dynamic-slice_fusion), channel_id=1, source_target_pairs={{0,252},{4,0},{8,4},{12,8},{16,12},{20,16},{24,20},{28,24},{32,28}... | collective-permute-start | bytes 786440 | tf_op jit(solution)/shard_map/ppermute | solution.py:211
  13.2 17.7 %collective-permute-start = (bf16[8,128,128]{2,1,0:T(8,128)(2,1)S(1)}, bf16[8,128,128]{2,1,0:T(8,128)(2,1)S(1)}, u32[]{:S(2)}, u32[]{:S(2)}) collective-permute-start(bf16[8,128,128]{2,1,0:T(8,128)(2,1)S(1)} %constant_dynamic-slice_fusion), channel_id=1, source_target_pairs={{0,4},{4,8},{8,12},{12,16},{16,20},{20,24},{24,28},{28,32},{32,36}... | collective-permute-start | bytes 786440 | tf_op jit(solution)/shard_map/ppermute | solution.py:210
  23.7 20.3 %copy-start.1 = (bf16[8,128,128]{2,1,0:T(8,128)(2,1)}, bf16[8,128,128]{2,1,0:T(8,128)(2,1)S(1)}, u32[]{:S(2)}) copy-start(bf16[8,128,128]{2,1,0:T(8,128)(2,1)S(1)} %collective-permute-done.2.hi_a) | copy-start | bytes 786436
  23.7 20.3 %collective-permute-start.3 = (bf16[8,128,128]{2,1,0:T(8,128)(2,1)S(1)}, bf16[8,128,128]{2,1,0:T(8,128)(2,1)S(1)}, u32[]{:S(2)}, u32[]{:S(2)}) collective-permute-start(bf16[8,128,128]{2,1,0:T(8,128)(2,1)S(1)} %collective-permute-done.2.hi_a), channel_id=1, source_target_pairs={{0,1},{1,0},{2,3},{3,2},{4,5},{5,4},{6,7},{7,6},{8,9},{9,8},{10,11... | collective-permute-start | bytes 786440 | tf_op jit(solution)/shard_map/ppermute | solution.py:216
  30.9 13.2 %copy-start.2 = (bf16[8,128,128]{2,1,0:T(8,128)(2,1)}, bf16[8,128,128]{2,1,0:T(8,128)(2,1)S(1)}, u32[]{:S(2)}) copy-start(bf16[8,128,128]{2,1,0:T(8,128)(2,1)S(1)} %collective-permute-done.lo_a) | copy-start | bytes 786436
  30.9 13.2 %collective-permute-start.1 = (bf16[8,128,128]{2,1,0:T(8,128)(2,1)S(1)}, bf16[8,128,128]{2,1,0:T(8,128)(2,1)S(1)}, u32[]{:S(2)}, u32[]{:S(2)}) collective-permute-start(bf16[8,128,128]{2,1,0:T(8,128)(2,1)S(1)} %collective-permute-done.lo_a), channel_id=1, source_target_pairs={{0,1},{1,0},{2,3},{3,2},{4,5},{5,4},{6,7},{7,6},{8,9},{9,8},{10,11... | collective-permute-start | bytes 786440 | tf_op jit(solution)/shard_map/ppermute | solution.py:215
  33.5 10.6 %copy-start = (f32[16,3,128]{2,1,0:T(4,128)}, f32[16,3,128]{2,1,0:T(4,128)S(1)}, u32[]{:S(2)}) copy-start(f32[16,3,128]{2,1,0:T(4,128)S(1)} %copy.19.pos_own) | copy-start | bytes 73732
  33.5 3.8 %collective-permute-start.5 = (f32[16,3,128]{2,1,0:T(4,128)S(1)}, f32[16,3,128]{2,1,0:T(4,128)S(1)}, u32[]{:S(2)}, u32[]{:S(2)}) collective-permute-start(f32[16,3,128]{2,1,0:T(4,128)S(1)} %copy.19.pos_own), channel_id=1, source_target_pairs={{0,252},{4,0},{8,4},{12,8},{16,12},{20,16},{24,20},{28,24},{32,28}... | collective-permute-start | bytes 73736 | tf_op jit(solution)/shard_map/ppermute | solution.py:213
  34.8 9.2 %collective-permute-start.4 = (f32[16,3,128]{2,1,0:T(4,128)S(1)}, f32[16,3,128]{2,1,0:T(4,128)S(1)}, u32[]{:S(2)}, u32[]{:S(2)}) collective-permute-start(f32[16,3,128]{2,1,0:T(4,128)S(1)} %copy.19.pos_own), channel_id=1, source_target_pairs={{0,4},{4,8},{8,12},{12,16},{16,20},{20,24},{24,28},{28,32},{32,36}... | collective-permute-start | bytes 73736 | tf_op jit(solution)/shard_map/ppermute | solution.py:212
  37.4 6.7 %copy-start.5 = (f32[16,3,128]{2,1,0:T(4,128)}, f32[16,3,128]{2,1,0:T(4,128)S(1)}, u32[]{:S(2)}) copy-start(f32[16,3,128]{2,1,0:T(4,128)S(1)} %collective-permute-done.5.pos_hi) | copy-start | bytes 73732
  44.0 0.6 copy-start.6
  44.0 0.7 copy-start.3
  44.0 0.8 copy-start.4
  70.2 3.8 %collective-permute-start.8 = (f32[16,3,128]{2,1,0:T(4,128)}, f32[16,3,128]{2,1,0:T(4,128)S(1)}, u32[]{:S(2)}, u32[]{:S(2)}) collective-permute-start(f32[16,3,128]{2,1,0:T(4,128)} %get-tuple-element.5), channel_id=1, source_target_pairs={{0,3},{1,2},{2,1},{3,0},{4,7},{5,6},{6,5},{7,4},{8,11},{9,10},{10,... | collective-permute-start | bytes 73736 | tf_op jit(solution)/shard_map/ppermute | solution.py:193
  72.2 3.3 %collective-permute-start.7 = (f32[16,3,128]{2,1,0:T(4,128)}, f32[16,3,128]{2,1,0:T(4,128)S(1)}, u32[]{:S(2)}, u32[]{:S(2)}) collective-permute-start(f32[16,3,128]{2,1,0:T(4,128)} %get-tuple-element.5), channel_id=1, source_target_pairs={{0,2},{1,3},{2,0},{3,1},{4,6},{5,7},{6,4},{7,5},{8,10},{9,11},{10,... | collective-permute-start | bytes 73736 | tf_op jit(solution)/shard_map/ppermute | solution.py:193
  73.3 2.3 %collective-permute-start.6 = (f32[16,3,128]{2,1,0:T(4,128)}, f32[16,3,128]{2,1,0:T(4,128)S(1)}, u32[]{:S(2)}, u32[]{:S(2)}) collective-permute-start(f32[16,3,128]{2,1,0:T(4,128)} %get-tuple-element.5), channel_id=1, source_target_pairs={{0,1},{1,0},{2,3},{3,2},{4,5},{5,4},{6,7},{7,6},{8,9},{9,8},{10,11... | collective-permute-start | bytes 73736 | tf_op jit(solution)/shard_map/ppermute | solution.py:193
  76.4 11.7 %copy-start.7 = (f32[16,3,128]{2,1,0:T(4,128)}, f32[16,3,128]{2,1,0:T(4,128)S(1)}, u32[]{:S(2)}) copy-start(f32[16,3,128]{2,1,0:T(4,128)S(1)} %get-tuple-element.12.tan_own) | copy-start | bytes 73732
  76.4 3.7 %collective-permute-start.10 = (f32[16,3,128]{2,1,0:T(4,128)S(1)}, f32[16,3,128]{2,1,0:T(4,128)S(1)}, u32[]{:S(2)}, u32[]{:S(2)}) collective-permute-start(f32[16,3,128]{2,1,0:T(4,128)S(1)} %get-tuple-element.12.tan_own), channel_id=1, source_target_pairs={{0,252},{4,0},{8,4},{12,8},{16,12},{20,16},{24,20},{28,24},{32,28}... | collective-permute-start | bytes 73736 | tf_op jit(solution)/shard_map/ppermute | solution.py:242
  78.9 9.1 %collective-permute-start.9 = (f32[16,3,128]{2,1,0:T(4,128)S(1)}, f32[16,3,128]{2,1,0:T(4,128)S(1)}, u32[]{:S(2)}, u32[]{:S(2)}) collective-permute-start(f32[16,3,128]{2,1,0:T(4,128)S(1)} %get-tuple-element.12.tan_own), channel_id=1, source_target_pairs={{0,4},{4,8},{8,12},{12,16},{16,20},{20,24},{24,28},{28,32},{32,36}... | collective-permute-start | bytes 73736 | tf_op jit(solution)/shard_map/ppermute | solution.py:241
  80.1 7.9 %copy-start.8 = (f32[16,3,128]{2,1,0:T(4,128)}, f32[16,3,128]{2,1,0:T(4,128)S(1)}, u32[]{:S(2)}) copy-start(f32[16,3,128]{2,1,0:T(4,128)S(1)} %collective-permute-done.10.tan_hi) | copy-start | bytes 73732
  88.0 0.6 copy-start.9
  104.8 4.0 %collective-permute-start.13 = (f32[16,3,128]{2,1,0:T(4,128)}, f32[16,3,128]{2,1,0:T(4,128)S(1)}, u32[]{:S(2)}, u32[]{:S(2)}) collective-permute-start(f32[16,3,128]{2,1,0:T(4,128)} %variance_gradient.1), channel_id=1, source_target_pairs={{0,3},{1,2},{2,1},{3,0},{4,7},{5,6},{6,5},{7,4},{8,11},{9,10},{10,... | collective-permute-start | bytes 73736 | tf_op jit(solution)/shard_map/ppermute | solution.py:193
  106.9 3.4 %collective-permute-start.12 = (f32[16,3,128]{2,1,0:T(4,128)}, f32[16,3,128]{2,1,0:T(4,128)S(1)}, u32[]{:S(2)}, u32[]{:S(2)}) collective-permute-start(f32[16,3,128]{2,1,0:T(4,128)} %variance_gradient.1), channel_id=1, source_target_pairs={{0,2},{1,3},{2,0},{3,1},{4,6},{5,7},{6,4},{7,5},{8,10},{9,11},{10,... | collective-permute-start | bytes 73736 | tf_op jit(solution)/shard_map/ppermute | solution.py:193
  107.9 2.4 %collective-permute-start.11 = (f32[16,3,128]{2,1,0:T(4,128)}, f32[16,3,128]{2,1,0:T(4,128)S(1)}, u32[]{:S(2)}, u32[]{:S(2)}) collective-permute-start(f32[16,3,128]{2,1,0:T(4,128)} %variance_gradient.1), channel_id=1, source_target_pairs={{0,1},{1,0},{2,3},{3,2},{4,5},{5,4},{6,7},{7,6},{8,9},{9,8},{10,11... | collective-permute-start | bytes 73736 | tf_op jit(solution)/shard_map/ppermute | solution.py:193

commit v2 on v1

--- a/solution.py
+++ b/solution.py
@@ -9,6 +9,8 @@
 
 STEP_BLOCKS = 4
 CHUNK = 32
+PIECES = 3
+TILE = 16
 LOG2E = 1.4426950408889634
 
 
@@ -21,16 +23,48 @@
     return [(i, i ^ bit) for i in range(lax.axis_size(axis))]
 
 
-def columns(tile):
-    rows = jnp.concatenate([tile, jnp.zeros((8 - tile.shape[0], tile.shape[1]), jnp.float32)], axis=0)
-    return jnp.transpose(rows)
+def place(rows, row, value):
+    at = lax.broadcasted_iota(jnp.int32, rows.shape, 0) == row
+    return jnp.where(at, value, rows)
+
+
+def pattern(depth, base, axis, width, value):
+    row = lax.broadcasted_iota(jnp.int32, (depth, width), 0)
+    hit = row == base + axis
+    for piece in range(1, PIECES):
+        hit = hit | (row == base + 3 * piece + axis)
+    return jnp.where(hit, value, 0.0)
+
+
+def difference_rhs(rows, axis, depth):
+    rhs = pattern(depth, 0, axis, rows.shape[1], -1.0)
+    for piece in range(PIECES):
+        at = 3 * piece + axis
+        rhs = place(rhs, 3 * PIECES + piece, rows[at:at + 1])
+    return rhs.astype(jnp.bfloat16)
+
+
+def change_rhs(pieces, axis, depth):
+    rhs = pattern(depth, TILE, axis, pieces[0].shape[1], 1.0)
+    for piece in range(PIECES):
+        rhs = place(rhs, 3 * PIECES + piece, -pieces[piece][axis:axis + 1])
+    return rhs.astype(jnp.bfloat16)
+
+
+def split(array):
+    pieces = []
+    rest = array
+    for _ in range(PIECES):
+        piece = rest.astype(jnp.bfloat16).astype(jnp.float32)
+        pieces.append(piece)
+        rest = rest - piece
+    return pieces
 
 
 def pair_kernel(
     idx_ref, cnt_ref, rate_ref, core_ref,
     own_ref, lo_a, lo_b, hi_a, hi_b, embed_ref, wproj_ref,
-    pos_own, pos_lo, pos_hi,
-    force_ref, first_ref, second_ref,
+    force_ref, first_ref, second_ref, rows_ref,
     proj_ref, col_ref,
 ):
     owned = own_ref.shape[0]
@@ -47,18 +81,21 @@
     def _():
         def project(source, base):
             def one(i, carry):
-                x = source[pl.ds(2 * i, 2)].reshape(2 * rows, channels)
+                x = source[pl.ds(2 * i, 2), pl.ds(0, rows), :].reshape(2 * rows, channels)
                 h = jnp.dot(x, embed_ref[...], preferred_element_type=jnp.float32)
                 half_h = 0.5 * h
                 hidden = (half_h + half_h * jnp.tanh(half_h)).astype(jnp.bfloat16)
                 out = jnp.dot(hidden, wproj_ref[...], preferred_element_type=jnp.float32)
                 proj_ref[pl.ds(base + 2 * i, 2)] = out.astype(jnp.bfloat16).reshape(2, rows, bases * channels)
+                for j in range(2):
+                    tile = source[2 * i + j, pl.ds(rows, TILE), :]
+                    rows_ref[base + 2 * i + j] = tile
+                    col_ref[base + 2 * i + j] = jnp.transpose(tile.astype(jnp.float32)).astype(jnp.bfloat16)
                 return carry
 
             lax.fori_loop(0, source.shape[0] // 2, one, 0, unroll=2)
 
-        core = core_ref[0]
-        near = core * half
+        near = core_ref[0] * half
         far = half - near
         project(own_ref, owned)
         project(lo_a, near)
@@ -66,31 +103,23 @@
         project(hi_a, 2 * owned + near)
         project(hi_b, 2 * owned + far)
 
-        def spread(source, base):
-            def one(i, carry):
-                col_ref[base + i] = columns(source[i])
-                return carry
-
-            lax.fori_loop(0, owned, one, 0, unroll=4)
-
-        spread(pos_lo, 0)
-        spread(pos_own, owned)
-        spread(pos_hi, 2 * owned)
-
     decay = [-LOG2E * rate_ref[k] for k in range(bases)]
     slope_coef = [(-2.0 * sigma) * rate_ref[k] for k in range(bases)]
     bend_coef = [(4.0 * sigma) * rate_ref[k] * rate_ref[k] for k in range(bases)]
 
-    for part in range(STEP_BLOCKS):
+    def one_block(part, carry):
         block = step * STEP_BLOCKS + part
         count = cnt_ref[block]
 
-        def run(live, block=block, part=part):
+        def run(live):
             left = proj_ref[owned + block]
-            left_pos = [pos_own[block, pl.ds(a, 1), :] for a in range(3)]
+            tile = own_ref[block, pl.ds(rows, TILE), :].astype(jnp.float32)
+            separators = [difference_rhs(tile, a, TILE) for a in range(3)]
             total = [jnp.zeros((8, rows), jnp.float32) for _ in range(3)]
             for slot in range(live):
                 source = idx_ref[block * slots + slot]
+                cols = col_ref[source]
+                parts = [jnp.dot(cols, r, preferred_element_type=jnp.float32) for r in separators]
                 dots = [
                     lax.dot_general(
                         proj_ref[source, :, k * channels:(k + 1) * channels],
@@ -101,8 +130,7 @@
                     for k in range(bases)
                 ]
                 for start in range(0, rows, CHUNK):
-                    cols = col_ref[source, start:start + CHUNK, :]
-                    delta = [left_pos[a] - cols[:, a:a + 1] for a in range(3)]
+                    delta = [p[start:start + CHUNK] for p in parts]
                     square = delta[0] * delta[0] + delta[1] * delta[1] + delta[2] * delta[2]
                     w = [
                         jnp.exp2(decay[k] * square) * dots[k][start:start + CHUNK]
@@ -127,13 +155,16 @@
 
         for live in range(3, slots + 1):
             pl.when(count == live)(lambda live=live: run(live))
+        return carry
+
+    lax.fori_loop(0, STEP_BLOCKS, one_block, 0)
 
 
 def grad_kernel(
-    idx_ref, cnt_ref, pos_own, pos_lo, pos_hi, tan_own, tan_lo, tan_hi, first_ref, second_ref,
+    idx_ref, cnt_ref, pos_ref, tan_own, tan_lo, tan_hi, first_ref, second_ref,
     grad_ref, col_ref,
 ):
-    owned = pos_own.shape[0]
+    owned = tan_own.shape[0]
     slots = first_ref.shape[1]
     rows = first_ref.shape[2]
     escale = 1.0 / math.sqrt(slots * rows)
@@ -141,31 +172,38 @@
 
     @pl.when(step == 0)
     def _():
-        def spread(pos, tan, base):
+        def spread(tan, base):
             def one(i, carry):
-                col_ref[base + i] = columns(jnp.concatenate([pos[i], tan[i]], axis=0))
+                filler = jnp.zeros((TILE - 3 * PIECES, rows), jnp.float32)
+                tile = jnp.concatenate(
+                    [pos_ref[base + i].astype(jnp.float32)] + split(tan[i]) + [filler], axis=0
+                )
+                col_ref[base + i] = jnp.transpose(tile).astype(jnp.bfloat16)
                 return carry
 
             lax.fori_loop(0, owned, one, 0, unroll=4)
 
-        spread(pos_lo, tan_lo, 0)
-        spread(pos_own, tan_own, owned)
-        spread(pos_hi, tan_hi, 2 * owned)
-
-    for part in range(STEP_BLOCKS):
+        spread(tan_lo, 0)
+        spread(tan_own, owned)
+        spread(tan_hi, 2 * owned)
+
+    def one_block(part, carry):
         block = step * STEP_BLOCKS + part
         count = cnt_ref[block]
 
-        def run(live, block=block, part=part):
-            left_pos = [pos_own[block, pl.ds(a, 1), :] for a in range(3)]
-            left_tan = [tan_own[block, pl.ds(a, 1), :] for a in range(3)]
+        def run(live):
+            tile = pos_ref[owned + block].astype(jnp.float32)
+            pieces = split(tan_own[block])
+            sides = [difference_rhs(tile, a, 2 * TILE) for a in range(3)]
+            sides += [change_rhs(pieces, a, 2 * TILE) for a in range(3)]
             total = [jnp.zeros((8, rows), jnp.float32) for _ in range(3)]
             for slot in range(live):
                 source = idx_ref[block * slots + slot]
+                cols = col_ref[source]
+                parts = [jnp.dot(cols, r, preferred_element_type=jnp.float32) for r in sides]
                 for start in range(0, rows, CHUNK):
-                    cols = col_ref[source, start:start + CHUNK, :]
-                    delta = [left_pos[a] - cols[:, a:a + 1] for a in range(3)]
-                    change = [cols[:, 3 + a:4 + a] - left_tan[a] for a in range(3)]
+                    delta = [p[start:start + CHUNK] for p in parts[:3]]
+                    change = [p[start:start + CHUNK] for p in parts[3:]]
                     first = first_ref[part, slot, start:start + CHUNK, :]
                     second = second_ref[part, slot, start:start + CHUNK, :]
                     along = second * (delta[0] * change[0] + delta[1] * change[1] + delta[2] * change[2])
@@ -178,10 +216,26 @@
 
         for live in range(3, slots + 1):
             pl.when(count == live)(lambda live=live: run(live))
+        return carry
+
+    lax.fori_loop(0, STEP_BLOCKS, one_block, 0)
+
+
+def pack(features, positions):
+    blocks, dims, rows = positions.shape
+    pieces = []
+    rest = positions
+    for _ in range(PIECES):
+        piece = lax.reduce_precision(rest, 8, 7)
+        pieces.append(piece.astype(jnp.bfloat16))
+        rest = rest - piece
+    ones = jnp.ones((blocks, PIECES, rows), jnp.bfloat16)
+    zeros = jnp.zeros((blocks, TILE - PIECES * (dims + 1), rows), jnp.bfloat16)
+    return jnp.concatenate([features] + pieces + [ones, zeros], axis=1)
 
 
 def whole(array):
-    return pl.BlockSpec(array.shape, lambda *_: (0,) * array.ndim, pipeline_mode=pl.Buffered(1))
+    return pl.BlockSpec(array.shape, lambda *_: (0,) * len(array.shape), pipeline_mode=pl.Buffered(1))
 
 
 def stepped(shape):
@@ -206,11 +260,10 @@
     up, down = ring("space", 1), ring("space", -1)
     half = owned // 2
 
-    mine = lax.dynamic_slice_in_dim(features, core * half, half, 0)
+    packed = pack(features, positions)
+    mine = lax.dynamic_slice_in_dim(packed, core * half, half, 0)
     lo_a = lax.ppermute(mine, "space", up)
     hi_a = lax.ppermute(mine, "space", down)
-    pos_lo = lax.ppermute(positions, "space", up)
-    pos_hi = lax.ppermute(positions, "space", down)
     swap = flip("member", 1)
     lo_b = lax.ppermute(lo_a, "member", swap)
     hi_b = lax.ppermute(hi_a, "member", swap)
@@ -219,20 +272,21 @@
     core_arr = core.astype(jnp.int32).reshape(1)
     pairs = jax.ShapeDtypeStruct((owned, slots, rows, rows), jnp.float32)
     small = jax.ShapeDtypeStruct((owned, dims, rows), jnp.float32)
-    tensors = (features, lo_a, lo_b, hi_a, hi_b, w_embed[0], w_proj[0], positions, pos_lo, pos_hi)
-    force, first, second = pl.pallas_call(
+    tensors = (packed, lo_a, lo_b, hi_a, hi_b, w_embed[0], w_proj[0])
+    tiles = jax.ShapeDtypeStruct((3 * owned, TILE, rows), jnp.bfloat16)
+    force, first, second, pos_rows = pl.pallas_call(
         pair_kernel,
         grid_spec=pltpu.PrefetchScalarGridSpec(
             num_scalar_prefetch=4,
             grid=(owned // STEP_BLOCKS,),
             in_specs=[whole(t) for t in tensors],
-            out_specs=[stepped((dims, rows)), stepped((slots, rows, rows)), stepped((slots, rows, rows))],
+            out_specs=[stepped((dims, rows)), stepped((slots, rows, rows)), stepped((slots, rows, rows)), whole(tiles)],
             scratch_shapes=[
                 pltpu.VMEM((3 * owned, rows, width), jnp.bfloat16),
-                pltpu.VMEM((3 * owned, rows, 8), jnp.float32),
+                pltpu.VMEM((3 * owned, rows, TILE), jnp.bfloat16),
             ],
         ),
-        out_shape=[small, pairs, pairs],
+        out_shape=[small, pairs, pairs, tiles],
         name="pair_forces",
     )(index, nbr_count, rates[0], core_arr, *tensors)
 
@@ -240,7 +294,7 @@
     tangent = (2.0 / members) * (force - mean_force)
     tan_lo = lax.ppermute(tangent, "space", up)
     tan_hi = lax.ppermute(tangent, "space", down)
-    tensors = (positions, pos_lo, pos_hi, tangent, tan_lo, tan_hi)
+    tensors = (pos_rows, tangent, tan_lo, tan_hi)
     grad = pl.pallas_call(
         grad_kernel,
         grid_spec=pltpu.PrefetchScalarGridSpec(
@@ -248,7 +302,7 @@
             grid=(owned // STEP_BLOCKS,),
             in_specs=[whole(t) for t in tensors] + [stepped((slots, rows, rows))] * 2,
             out_specs=stepped((dims, rows)),
-            scratch_shapes=[pltpu.VMEM((3 * owned, rows, 8), jnp.float32)],
+            scratch_shapes=[pltpu.VMEM((3 * owned, rows, 2 * TILE), jnp.bfloat16)],
         ),
         out_shape=small,
         name="variance_gradient",

time: 112 us -> 100 us (0.89); the launches traced: 112 us -> 101 us
  waiting for transfers between devices: 35.9 us -> 29.3 us
  Pallas kernels: 41.6 us -> 38.1 us
  starting transfers between devices: 26.3 us -> 23.3 us
  other arithmetic: 2.26 us -> 3.77 us
    ppermute x2 -> x0, waiting for transfers between devices: 6.67 us -> none  [the longest x1 6.65 us: body(): pos_lo = lax.ppermute(positions, 'space', up)]
    pallas_call x1, Pallas kernels: 16.1 us -> 12 us  [body(): pl.pallas_call(grad_kernel, grid_spec=pltpu.PrefetchScalarGridSpec(num_sc...]
    ppermute x1, starting transfers between devices: 2.54 us -> 0.08 us  [body(): tan_hi = lax.ppermute(tangent, 'space', down)]
    ppermute x2 -> x0, starting transfers between devices: 2.44 us -> none  [the longest x1 1.3 us: body(): pos_hi = lax.ppermute(positions, 'space', down)]
    ppermute x1, starting transfers between devices: 0.01 us -> 2.35 us  [body(): tan_lo = lax.ppermute(tangent, 'space', up)]
    ppermute x1, waiting for transfers between devices: 7.89 us -> 5.6 us  [body(): tan_lo = lax.ppermute(tangent, 'space', up)]
    concatenate x0 -> x1, local copies, waits for them, and re-layouts: none -> 2.2 us  [pack(): return jnp.concatenate([features] + pieces + [ones, zeros], axis=1)]
    ppermute x1, waiting for transfers between devices: 10.5 us -> 12.6 us  [body(): hi_a = lax.ppermute(mine, 'space', down)]
  transfers between devices with their start and end apart: 14 -> 12, of which waited for: 9 -> 8; matrix products, arithmetic and copies ran while one was open for 2% -> 2% of each run, Pallas kernels for 0% -> 0%
where the time goes in v2:
time: 100 us; the launch traced here: 101 us
  Pallas kernels  38.1 us (38%)
  waiting for transfers between devices  29.3 us (29%)
  starting transfers between devices  23.3 us (23%)
  local copies, waits for them, and re-layouts  5.56 us (6%)
  other arithmetic  3.77 us (4%)
    pallas_call x1, Pallas kernels, body(): pl.pallas_call(pair_kernel, grid_spec=pltpu.PrefetchScalarGridSpec(num_sc...  26.2 us
    ppermute x1, waiting for transfers between devices, body(): hi_a = lax.ppermute(mine, 'space', down)  12.6 us
    pallas_call x1, Pallas kernels, body(): pl.pallas_call(grad_kernel, grid_spec=pltpu.PrefetchScalarGridSpec(num_sc...  12 us
    ppermute x1, starting transfers between devices, body(): hi_a = lax.ppermute(mine, 'space', down)  11.6 us
    ppermute x6, starting transfers between devices, member_sum(): lax.ppermute(array, 'member', flip('member', bit))  6.49 us
    ppermute x1, waiting for transfers between devices, body(): tan_lo = lax.ppermute(tangent, 'space', up)  5.6 us
    ppermute x1, waiting for transfers between devices, body(): lo_a = lax.ppermute(mine, 'space', up)  5.54 us
    ppermute x6, waiting for transfers between devices, member_sum(): lax.ppermute(array, 'member', flip('member', bit))  4.22 us
  transfers between devices with their start and end apart: 12, of which 8 were waited for; matrix products, arithmetic and copies ran while one was open for 2% of the time, Pallas kernels for 0%

profile of v2, /device:TPU:1, one launch (start us, length us, event | category | flops | bytes accessed | tf_op | source)
XLA Modules:
  0.0 100.9 jit_solution(8118752229858546697)
XLA Ops:
  0.6 0.7 reduce_precision.9
  1.4 0.8 fusion.1
  2.2 2.2 %concatenate.3.own_ref = bf16[16,144,128]{2,1,0:T(8,128)(2,1)S(1)} concatenate(bf16[16,128,128]{2,1,0:T(8,128)(2,1)} %param.8, bf16[16,3,128]{2,1,0:T(4,128)(2,1)S(1)} %copy.36, bf16[16,3,128]{2,1,0:T(4,128)(2,1)S(1)} %get-tuple-element.19, bf16[16,3,128]{2,1,0:T(4,128)(2,1)S(1)} %get-tuple-element.18, bf16[16,3,128]{2,1,0:T(4,128)(2,1)S(1)} %broadcast_in_dim.6, ...), dimensions={1} | concatenate | bytes 1179648 | tf_op jit(solution)/shard_map/concatenate | solution.py:234
  4.4 0.0 copy-start
  4.5 11.6 %collective-permute-start.2 = (bf16[8,144,128]{2,1,0:T(8,128)(2,1)S(1)}, bf16[8,144,128]{2,1,0:T(8,128)(2,1)S(1)}, u32[]{:S(2)}, u32[]{:S(2)}) collective-permute-start(bf16[8,144,128]{2,1,0:T(8,128)(2,1)S(1)} %constant_dynamic-slice_fusion), channel_id=1, source_target_pairs={{0,252},{4,0},{8,4},{12,8},{16,12},{20,16},{24,20},{28,24},{32,28}... | collective-permute-start | bytes 884744 | tf_op jit(solution)/shard_map/ppermute | solution.py:266
  16.0 0.0 collective-permute-start
  16.0 12.6 %collective-permute-done.2.hi_a = bf16[8,144,128]{2,1,0:T(8,128)(2,1)S(1)} collective-permute-done((bf16[8,144,128]{2,1,0:T(8,128)(2,1)S(1)}, bf16[8,144,128]{2,1,0:T(8,128)(2,1)S(1)}, u32[]{:S(2)}, u32[]{:S(2)}) %collective-permute-start.2) | collective-permute-done | bytes 294944 | tf_op jit(solution)/shard_map/ppermute | solution.py:266
  28.6 0.0 copy-start.1
  28.6 1.0 collective-permute-start.3
  29.6 5.5 %collective-permute-done.lo_a = bf16[8,144,128]{2,1,0:T(8,128)(2,1)S(1)} collective-permute-done((bf16[8,144,128]{2,1,0:T(8,128)(2,1)S(1)}, bf16[8,144,128]{2,1,0:T(8,128)(2,1)S(1)}, u32[]{:S(2)}, u32[]{:S(2)}) %collective-permute-start) | collective-permute-done | bytes 294944 | tf_op jit(solution)/shard_map/ppermute | solution.py:265
  35.1 0.0 copy-start.2
  35.1 1.9 %collective-permute-start.1 = (bf16[8,144,128]{2,1,0:T(8,128)(2,1)S(1)}, bf16[8,144,128]{2,1,0:T(8,128)(2,1)S(1)}, u32[]{:S(2)}, u32[]{:S(2)}) collective-permute-start(bf16[8,144,128]{2,1,0:T(8,128)(2,1)S(1)} %collective-permute-done.lo_a), channel_id=1, source_target_pairs={{0,1},{1,0},{2,3},{3,2},{4,5},{5,4},{6,7},{7,6},{8,9},{9,8},{10,11... | collective-permute-start | bytes 884744 | tf_op jit(solution)/shard_map/ppermute | solution.py:268
  37.0 0.7 add_select_fusion
  37.7 0.1 copy.19
  37.8 0.6 reshape.10.idx_ref
  38.4 0.0 collective-permute-done.3.hi_b
  38.4 0.0 copy-start.3
  38.4 0.0 collective-permute-done.1.lo_b
  38.4 0.0 copy-start.4
  38.4 0.0 copy-done
  38.4 0.0 copy-done.1
  38.4 0.0 copy-done.2
  38.4 0.7 copy-done.3
  39.1 0.1 copy-done.4
  39.2 26.2 %pair_forces.1 = (f32[16,3,128]{2,1,0:T(4,128)}, f32[16,6,128,128]{3,2,1,0:T(8,128)}, f32[16,6,128,128]{3,2,1,0:T(8,128)}, bf16[48,16,128]{2,1,0:T(8,128)(2,1)}) custom-call(s32[96]{0:T(128)} %reshape.10.idx_ref, s32[16]{0:T(128)} %cnt_ref.3, f32[4]{0:T(128)} %bitcast.6, s32[1]{0:T(128)} %bitcast.1.core_ref, bf16[16,144,128]{2,1,0:T(8,128)(2,1)} %copy-done, ...), custom_call_target="tpu_custom_call" | custom-call | tf_op jit(solution)/shard_map/pair_forces/pallas_call | solution.py:277
  65.4 1.9 %collective-permute-start.6 = (f32[16,3,128]{2,1,0:T(4,128)}, f32[16,3,128]{2,1,0:T(4,128)S(1)}, u32[]{:S(2)}, u32[]{:S(2)}) collective-permute-start(f32[16,3,128]{2,1,0:T(4,128)} %get-tuple-element.6), channel_id=1, source_target_pairs={{0,3},{1,2},{2,1},{3,0},{4,7},{5,6},{6,5},{7,4},{8,11},{9,10},{10,... | collective-permute-start | bytes 73736 | tf_op jit(solution)/shard_map/ppermute | solution.py:247
  67.3 0.1 collective-permute-start.5
  67.4 0.3 collective-permute-start.4
  67.8 1.4 %collective-permute-done.6 = f32[16,3,128]{2,1,0:T(4,128)S(1)} collective-permute-done((f32[16,3,128]{2,1,0:T(4,128)}, f32[16,3,128]{2,1,0:T(4,128)S(1)}, u32[]{:S(2)}, u32[]{:S(2)}) %collective-permute-start.6) | collective-permute-done | bytes 24608 | tf_op jit(solution)/shard_map/ppermute | solution.py:247
  69.2 1.1 %collective-permute-done.5 = f32[16,3,128]{2,1,0:T(4,128)S(1)} collective-permute-done((f32[16,3,128]{2,1,0:T(4,128)}, f32[16,3,128]{2,1,0:T(4,128)S(1)}, u32[]{:S(2)}, u32[]{:S(2)}) %collective-permute-start.5) | collective-permute-done | bytes 24608 | tf_op jit(solution)/shard_map/ppermute | solution.py:247
  70.2 0.0 collective-permute-done.4
  70.2 0.8 subtract_multiply_fusion
  71.0 0.0 copy-start.5
  71.0 0.1 collective-permute-start.8
  71.1 2.4 %collective-permute-start.7 = (f32[16,3,128]{2,1,0:T(4,128)S(1)}, f32[16,3,128]{2,1,0:T(4,128)S(1)}, u32[]{:S(2)}, u32[]{:S(2)}) collective-permute-start(f32[16,3,128]{2,1,0:T(4,128)S(1)} %get-tuple-element.16.tan_own), channel_id=1, source_target_pairs={{0,4},{4,8},{8,12},{12,16},{16,20},{20,24},{24,28},{28,32},{32,36}... | collective-permute-start | bytes 73736 | tf_op jit(solution)/shard_map/ppermute | solution.py:295
  73.5 1.4 %collective-permute-done.8.tan_hi = f32[16,3,128]{2,1,0:T(4,128)S(1)} collective-permute-done((f32[16,3,128]{2,1,0:T(4,128)S(1)}, f32[16,3,128]{2,1,0:T(4,128)S(1)}, u32[]{:S(2)}, u32[]{:S(2)}) %collective-permute-start.8) | collective-permute-done | bytes 24608 | tf_op jit(solution)/shard_map/ppermute | solution.py:296
  74.9 0.0 copy-start.6
  74.9 5.6 %collective-permute-done.7.tan_lo = f32[16,3,128]{2,1,0:T(4,128)S(1)} collective-permute-done((f32[16,3,128]{2,1,0:T(4,128)S(1)}, f32[16,3,128]{2,1,0:T(4,128)S(1)}, u32[]{:S(2)}, u32[]{:S(2)}) %collective-permute-start.7) | collective-permute-done | bytes 24608 | tf_op jit(solution)/shard_map/ppermute | solution.py:295
  80.5 0.0 copy-start.7
  80.5 0.0 copy-done.5
  80.5 0.0 copy-done.6
  80.5 0.6 copy-done.7
  81.1 12.0 %variance_gradient.1 = f32[16,3,128]{2,1,0:T(4,128)} custom-call(s32[96]{0:T(128)} %reshape.10.idx_ref, s32[16]{0:T(128)} %cnt_ref.3, bf16[48,16,128]{2,1,0:T(8,128)(2,1)} %get-tuple-element.7.pos_ref, f32[16,3,128]{2,1,0:T(4,128)} %copy-done.5, f32[16,3,128]{2,1,0:T(4,128)} %copy-done.7, f32[16,3,128]{2,1,0:T(4,128)} %copy-done.6, ...), custom_call_target="tpu_custom_call" | custom-call | tf_op jit(solution)/shard_map/variance_gradient/pallas_call | solution.py:298
  93.1 3.0 %collective-permute-start.11 = (f32[16,3,128]{2,1,0:T(4,128)}, f32[16,3,128]{2,1,0:T(4,128)S(1)}, u32[]{:S(2)}, u32[]{:S(2)}) collective-permute-start(f32[16,3,128]{2,1,0:T(4,128)} %variance_gradient.1), channel_id=1, source_target_pairs={{0,3},{1,2},{2,1},{3,0},{4,7},{5,6},{6,5},{7,4},{8,11},{9,10},{10,... | collective-permute-start | bytes 73736 | tf_op jit(solution)/shard_map/ppermute | solution.py:247
  96.1 1.1 %collective-permute-start.10 = (f32[16,3,128]{2,1,0:T(4,128)}, f32[16,3,128]{2,1,0:T(4,128)S(1)}, u32[]{:S(2)}, u32[]{:S(2)}) collective-permute-start(f32[16,3,128]{2,1,0:T(4,128)} %variance_gradient.1), channel_id=1, source_target_pairs={{0,2},{1,3},{2,0},{3,1},{4,6},{5,7},{6,4},{7,5},{8,10},{9,11},{10,... | collective-permute-start | bytes 73736 | tf_op jit(solution)/shard_map/ppermute | solution.py:247
  97.2 0.0 collective-permute-start.9
  97.2 0.6 copy.23
  97.8 0.1 collective-permute-done.11
  97.9 1.6 %collective-permute-done.10 = f32[16,3,128]{2,1,0:T(4,128)S(1)} collective-permute-done((f32[16,3,128]{2,1,0:T(4,128)}, f32[16,3,128]{2,1,0:T(4,128)S(1)}, u32[]{:S(2)}, u32[]{:S(2)}) %collective-permute-start.10) | collective-permute-done | bytes 24608 | tf_op jit(solution)/shard_map/ppermute | solution.py:247
  99.5 0.0 collective-permute-done.9
  99.5 0.8 add_add_fusion
  100.3 0.6 copy.24
  (4 shorter events, 0.1 us)
Async XLA Ops:
  4.4 34.0 %copy-start = (bf16[16,144,128]{2,1,0:T(8,128)(2,1)}, bf16[16,144,128]{2,1,0:T(8,128)(2,1)S(1)}, u32[]{:S(2)}) copy-start(bf16[16,144,128]{2,1,0:T(8,128)(2,1)S(1)} %concatenate.3.own_ref) | copy-start | bytes 1769476
  4.5 24.1 %collective-permute-start.2 = (bf16[8,144,128]{2,1,0:T(8,128)(2,1)S(1)}, bf16[8,144,128]{2,1,0:T(8,128)(2,1)S(1)}, u32[]{:S(2)}, u32[]{:S(2)}) collective-permute-start(bf16[8,144,128]{2,1,0:T(8,128)(2,1)S(1)} %constant_dynamic-slice_fusion), channel_id=1, source_target_pairs={{0,252},{4,0},{8,4},{12,8},{16,12},{20,16},{24,20},{28,24},{32,28}... | collective-permute-start | bytes 884744 | tf_op jit(solution)/shard_map/ppermute | solution.py:266
  16.0 19.1 %collective-permute-start = (bf16[8,144,128]{2,1,0:T(8,128)(2,1)S(1)}, bf16[8,144,128]{2,1,0:T(8,128)(2,1)S(1)}, u32[]{:S(2)}, u32[]{:S(2)}) collective-permute-start(bf16[8,144,128]{2,1,0:T(8,128)(2,1)S(1)} %constant_dynamic-slice_fusion), channel_id=1, source_target_pairs={{0,4},{4,8},{8,12},{12,16},{16,20},{20,24},{24,28},{28,32},{32,36}... | collective-permute-start | bytes 884744 | tf_op jit(solution)/shard_map/ppermute | solution.py:265
  28.6 9.8 %copy-start.1 = (bf16[8,144,128]{2,1,0:T(8,128)(2,1)}, bf16[8,144,128]{2,1,0:T(8,128)(2,1)S(1)}, u32[]{:S(2)}) copy-start(bf16[8,144,128]{2,1,0:T(8,128)(2,1)S(1)} %collective-permute-done.2.hi_a) | copy-start | bytes 884740
  28.6 9.8 %collective-permute-start.3 = (bf16[8,144,128]{2,1,0:T(8,128)(2,1)S(1)}, bf16[8,144,128]{2,1,0:T(8,128)(2,1)S(1)}, u32[]{:S(2)}, u32[]{:S(2)}) collective-permute-start(bf16[8,144,128]{2,1,0:T(8,128)(2,1)S(1)} %collective-permute-done.2.hi_a), channel_id=1, source_target_pairs={{0,1},{1,0},{2,3},{3,2},{4,5},{5,4},{6,7},{7,6},{8,9},{9,8},{10,11... | collective-permute-start | bytes 884744 | tf_op jit(solution)/shard_map/ppermute | solution.py:269
  35.1 3.3 %copy-start.2 = (bf16[8,144,128]{2,1,0:T(8,128)(2,1)}, bf16[8,144,128]{2,1,0:T(8,128)(2,1)S(1)}, u32[]{:S(2)}) copy-start(bf16[8,144,128]{2,1,0:T(8,128)(2,1)S(1)} %collective-permute-done.lo_a) | copy-start | bytes 884740
  35.1 3.3 %collective-permute-start.1 = (bf16[8,144,128]{2,1,0:T(8,128)(2,1)S(1)}, bf16[8,144,128]{2,1,0:T(8,128)(2,1)S(1)}, u32[]{:S(2)}, u32[]{:S(2)}) collective-permute-start(bf16[8,144,128]{2,1,0:T(8,128)(2,1)S(1)} %collective-permute-done.lo_a), channel_id=1, source_target_pairs={{0,1},{1,0},{2,3},{3,2},{4,5},{5,4},{6,7},{7,6},{8,9},{9,8},{10,11... | collective-permute-start | bytes 884744 | tf_op jit(solution)/shard_map/ppermute | solution.py:268
  38.4 0.7 copy-start.3
  38.4 0.8 copy-start.4
  65.4 3.8 %collective-permute-start.6 = (f32[16,3,128]{2,1,0:T(4,128)}, f32[16,3,128]{2,1,0:T(4,128)S(1)}, u32[]{:S(2)}, u32[]{:S(2)}) collective-permute-start(f32[16,3,128]{2,1,0:T(4,128)} %get-tuple-element.6), channel_id=1, source_target_pairs={{0,3},{1,2},{2,1},{3,0},{4,7},{5,6},{6,5},{7,4},{8,11},{9,10},{10,... | collective-permute-start | bytes 73736 | tf_op jit(solution)/shard_map/ppermute | solution.py:247
  67.3 3.0 %collective-permute-start.5 = (f32[16,3,128]{2,1,0:T(4,128)}, f32[16,3,128]{2,1,0:T(4,128)S(1)}, u32[]{:S(2)}, u32[]{:S(2)}) collective-permute-start(f32[16,3,128]{2,1,0:T(4,128)} %get-tuple-element.6), channel_id=1, source_target_pairs={{0,2},{1,3},{2,0},{3,1},{4,6},{5,7},{6,4},{7,5},{8,10},{9,11},{10,... | collective-permute-start | bytes 73736 | tf_op jit(solution)/shard_map/ppermute | solution.py:247
  67.4 2.8 %collective-permute-start.4 = (f32[16,3,128]{2,1,0:T(4,128)}, f32[16,3,128]{2,1,0:T(4,128)S(1)}, u32[]{:S(2)}, u32[]{:S(2)}) collective-permute-start(f32[16,3,128]{2,1,0:T(4,128)} %get-tuple-element.6), channel_id=1, source_target_pairs={{0,1},{1,0},{2,3},{3,2},{4,5},{5,4},{6,7},{7,6},{8,9},{9,8},{10,11... | collective-permute-start | bytes 73736 | tf_op jit(solution)/shard_map/ppermute | solution.py:247
  71.0 9.5 %copy-start.5 = (f32[16,3,128]{2,1,0:T(4,128)}, f32[16,3,128]{2,1,0:T(4,128)S(1)}, u32[]{:S(2)}) copy-start(f32[16,3,128]{2,1,0:T(4,128)S(1)} %get-tuple-element.16.tan_own) | copy-start | bytes 73732
  71.0 3.8 %collective-permute-start.8 = (f32[16,3,128]{2,1,0:T(4,128)S(1)}, f32[16,3,128]{2,1,0:T(4,128)S(1)}, u32[]{:S(2)}, u32[]{:S(2)}) collective-permute-start(f32[16,3,128]{2,1,0:T(4,128)S(1)} %get-tuple-element.16.tan_own), channel_id=1, source_target_pairs={{0,252},{4,0},{8,4},{12,8},{16,12},{20,16},{24,20},{28,24},{32,28}... | collective-permute-start | bytes 73736 | tf_op jit(solution)/shard_map/ppermute | solution.py:296
  71.1 9.4 %collective-permute-start.7 = (f32[16,3,128]{2,1,0:T(4,128)S(1)}, f32[16,3,128]{2,1,0:T(4,128)S(1)}, u32[]{:S(2)}, u32[]{:S(2)}) collective-permute-start(f32[16,3,128]{2,1,0:T(4,128)S(1)} %get-tuple-element.16.tan_own), channel_id=1, source_target_pairs={{0,4},{4,8},{8,12},{12,16},{16,20},{20,24},{24,28},{28,32},{32,36}... | collective-permute-start | bytes 73736 | tf_op jit(solution)/shard_map/ppermute | solution.py:295
  74.9 5.6 %copy-start.6 = (f32[16,3,128]{2,1,0:T(4,128)}, f32[16,3,128]{2,1,0:T(4,128)S(1)}, u32[]{:S(2)}) copy-start(f32[16,3,128]{2,1,0:T(4,128)S(1)} %collective-permute-done.8.tan_hi) | copy-start | bytes 73732
  80.5 0.6 copy-start.7
  93.1 4.8 %collective-permute-start.11 = (f32[16,3,128]{2,1,0:T(4,128)}, f32[16,3,128]{2,1,0:T(4,128)S(1)}, u32[]{:S(2)}, u32[]{:S(2)}) collective-permute-start(f32[16,3,128]{2,1,0:T(4,128)} %variance_gradient.1), channel_id=1, source_target_pairs={{0,3},{1,2},{2,1},{3,0},{4,7},{5,6},{6,5},{7,4},{8,11},{9,10},{10,... | collective-permute-start | bytes 73736 | tf_op jit(solution)/shard_map/ppermute | solution.py:247
  96.1 3.4 %collective-permute-start.10 = (f32[16,3,128]{2,1,0:T(4,128)}, f32[16,3,128]{2,1,0:T(4,128)S(1)}, u32[]{:S(2)}, u32[]{:S(2)}) collective-permute-start(f32[16,3,128]{2,1,0:T(4,128)} %variance_gradient.1), channel_id=1, source_target_pairs={{0,2},{1,3},{2,0},{3,1},{4,6},{5,7},{6,4},{7,5},{8,10},{9,11},{10,... | collective-permute-start | bytes 73736 | tf_op jit(solution)/shard_map/ppermute | solution.py:247
  97.2 2.4 %collective-permute-start.9 = (f32[16,3,128]{2,1,0:T(4,128)}, f32[16,3,128]{2,1,0:T(4,128)S(1)}, u32[]{:S(2)}, u32[]{:S(2)}) collective-permute-start(f32[16,3,128]{2,1,0:T(4,128)} %variance_gradient.1), channel_id=1, source_target_pairs={{0,1},{1,0},{2,3},{3,2},{4,5},{5,4},{6,7},{7,6},{8,9},{9,8},{10,11... | collective-permute-start | bytes 73736 | tf_op jit(solution)/shard_map/ppermute | solution.py:247

commit v3 on v2

--- a/solution.py
+++ b/solution.py
@@ -287,6 +287,7 @@
             ],
         ),
         out_shape=[small, pairs, pairs, tiles],
+        compiler_params=pltpu.CompilerParams(vmem_limit_bytes=26 << 20),
         name="pair_forces",
     )(index, nbr_count, rates[0], core_arr, *tensors)
 
@@ -305,6 +306,7 @@
             scratch_shapes=[pltpu.VMEM((3 * owned, rows, 2 * TILE), jnp.bfloat16)],
         ),
         out_shape=small,
+        compiler_params=pltpu.CompilerParams(vmem_limit_bytes=14 << 20),
         name="variance_gradient",
     )(index, nbr_count, *tensors, first, second)
     return (mean_force, member_sum(grad))

time: 100 us -> 92.8 us (0.928); the launches traced: 101 us -> 92.1 us
  Pallas kernels: 38.1 us -> 29.1 us
  other arithmetic: 3.77 us -> 2.25 us
  local copies, waits for them, and re-layouts: 5.56 us -> 6.62 us
    pallas_call x1, Pallas kernels: 26.2 us -> 20.5 us  [body(): pl.pallas_call(pair_kernel, grid_spec=pltpu.PrefetchScalarGridSpec(num_sc...]
    pallas_call x1, Pallas kernels: 12 us -> 8.53 us  [body(): pl.pallas_call(grad_kernel, grid_spec=pltpu.PrefetchScalarGridSpec(num_sc...]
    unnamed x18 -> x10, local copies, waits for them, and re-layouts: 2.62 us -> 4.19 us
  transfers between devices with their start and end apart: 12 -> 12, of which waited for: 8 -> 9; matrix products, arithmetic and copies ran while one was open for 2% -> 2% of each run, Pallas kernels for 0% -> 0%
where the time goes in v3:
time: 92.8 us; the launch traced here: 92.1 us
  waiting for transfers between devices  30 us (32%)
  Pallas kernels  29.1 us (31%)
  starting transfers between devices  23.5 us (25%)
  local copies, waits for them, and re-layouts  6.62 us (7%)
  other arithmetic  2.25 us (2%)
    pallas_call x1, Pallas kernels, body(): pl.pallas_call(pair_kernel, grid_spec=pltpu.PrefetchScalarGridSpec(num_sc...  20.5 us
    ppermute x1, waiting for transfers between devices, body(): hi_a = lax.ppermute(mine, 'space', down)  12.6 us
    ppermute x1, starting transfers between devices, body(): hi_a = lax.ppermute(mine, 'space', down)  11.6 us
    pallas_call x1, Pallas kernels, body(): pl.pallas_call(grad_kernel, grid_spec=pltpu.PrefetchScalarGridSpec(num_sc...  8.53 us
    ppermute x6, starting transfers between devices, member_sum(): lax.ppermute(array, 'member', flip('member', bit))  6.63 us
    ppermute x1, waiting for transfers between devices, body(): tan_lo = lax.ppermute(tangent, 'space', up)  6.28 us
    ppermute x1, waiting for transfers between devices, body(): lo_a = lax.ppermute(mine, 'space', up)  5.54 us
    unnamed x10, local copies, waits for them, and re-layouts  4.19 us
  transfers between devices with their start and end apart: 12, of which 9 were waited for; matrix products, arithmetic and copies ran while one was open for 2% of the time, Pallas kernels for 0%

profile of v3, /device:TPU:1, one launch (start us, length us, event | category | flops | bytes accessed | tf_op | source)
XLA Modules:
  0.0 92.1 jit_solution(5624869624032057423)
XLA Ops:
  0.6 0.7 reduce_precision.9
  1.4 0.8 fusion.1
  2.2 2.2 %concatenate.3.own_ref = bf16[16,144,128]{2,1,0:T(8,128)(2,1)S(1)} concatenate(bf16[16,128,128]{2,1,0:T(8,128)(2,1)} %param.8, bf16[16,3,128]{2,1,0:T(4,128)(2,1)S(1)} %copy.36, bf16[16,3,128]{2,1,0:T(4,128)(2,1)S(1)} %get-tuple-element.19, bf16[16,3,128]{2,1,0:T(4,128)(2,1)S(1)} %get-tuple-element.18, bf16[16,3,128]{2,1,0:T(4,128)(2,1)S(1)} %broadcast_in_dim.6, ...), dimensions={1} | concatenate | bytes 1179648 | tf_op jit(solution)/shard_map/concatenate | solution.py:234
  4.5 11.6 %collective-permute-start.2 = (bf16[8,144,128]{2,1,0:T(8,128)(2,1)S(1)}, bf16[8,144,128]{2,1,0:T(8,128)(2,1)S(1)}, u32[]{:S(2)}, u32[]{:S(2)}) collective-permute-start(bf16[8,144,128]{2,1,0:T(8,128)(2,1)S(1)} %constant_dynamic-slice_fusion), channel_id=1, source_target_pairs={{0,252},{4,0},{8,4},{12,8},{16,12},{20,16},{24,20},{28,24},{32,28}... | collective-permute-start | bytes 884744 | tf_op jit(solution)/shard_map/ppermute | solution.py:266
  16.0 0.0 collective-permute-start
  16.0 12.6 %collective-permute-done.2.hi_a = bf16[8,144,128]{2,1,0:T(8,128)(2,1)S(1)} collective-permute-done((bf16[8,144,128]{2,1,0:T(8,128)(2,1)S(1)}, bf16[8,144,128]{2,1,0:T(8,128)(2,1)S(1)}, u32[]{:S(2)}, u32[]{:S(2)}) %collective-permute-start.2) | collective-permute-done | bytes 294944 | tf_op jit(solution)/shard_map/ppermute | solution.py:266
  28.6 1.0 %collective-permute-start.3 = (bf16[8,144,128]{2,1,0:T(8,128)(2,1)S(1)}, bf16[8,144,128]{2,1,0:T(8,128)(2,1)S(1)}, u32[]{:S(2)}, u32[]{:S(2)}) collective-permute-start(bf16[8,144,128]{2,1,0:T(8,128)(2,1)S(1)} %collective-permute-done.2.hi_a), channel_id=1, source_target_pairs={{0,1},{1,0},{2,3},{3,2},{4,5},{5,4},{6,7},{7,6},{8,9},{9,8},{10,11... | collective-permute-start | bytes 884744 | tf_op jit(solution)/shard_map/ppermute | solution.py:269
  29.6 5.5 %collective-permute-done.lo_a = bf16[8,144,128]{2,1,0:T(8,128)(2,1)S(1)} collective-permute-done((bf16[8,144,128]{2,1,0:T(8,128)(2,1)S(1)}, bf16[8,144,128]{2,1,0:T(8,128)(2,1)S(1)}, u32[]{:S(2)}, u32[]{:S(2)}) %collective-permute-start) | collective-permute-done | bytes 294944 | tf_op jit(solution)/shard_map/ppermute | solution.py:265
  35.1 1.9 %collective-permute-start.1 = (bf16[8,144,128]{2,1,0:T(8,128)(2,1)S(1)}, bf16[8,144,128]{2,1,0:T(8,128)(2,1)S(1)}, u32[]{:S(2)}, u32[]{:S(2)}) collective-permute-start(bf16[8,144,128]{2,1,0:T(8,128)(2,1)S(1)} %collective-permute-done.lo_a), channel_id=1, source_target_pairs={{0,1},{1,0},{2,3},{3,2},{4,5},{5,4},{6,7},{7,6},{8,9},{9,8},{10,11... | collective-permute-start | bytes 884744 | tf_op jit(solution)/shard_map/ppermute | solution.py:268
  37.0 0.7 add_select_fusion
  37.7 0.1 copy.19
  37.8 0.1 reshape.10.idx_ref
  37.9 0.0 collective-permute-done.3.hi_b
  37.9 0.3 collective-permute-done.1.lo_b
  38.2 0.0 copy-start
  38.2 0.9 copy-done
  39.1 0.0 copy-start.1
  39.1 0.8 copy-done.1
  39.9 0.0 copy-start.2
  39.9 0.7 copy-done.2
  40.5 0.0 copy-start.3
  40.5 0.7 copy-done.3
  41.2 20.5 %pair_forces.1 = (f32[16,3,128]{2,1,0:T(4,128)S(1)}, f32[16,6,128,128]{3,2,1,0:T(8,128)S(1)}, f32[16,6,128,128]{3,2,1,0:T(8,128)S(1)}, bf16[48,16,128]{2,1,0:T(8,128)(2,1)S(1)}) custom-call(s32[96]{0:T(128)S(1)} %reshape.10.idx_ref, s32[16]{0:T(128)S(1)} %copy-done.2, f32[4]{0:T(128)S(1)} %bitcast.6, s32[1]{0:T(128)} %bitcast.1.core_ref, ...), custom_call_target="tpu_custom_call" | custom-call | tf_op jit(solution)/shard_map/pair_forces/pallas_call | solution.py:277
  61.7 2.2 %collective-permute-start.6 = (f32[16,3,128]{2,1,0:T(4,128)S(1)}, f32[16,3,128]{2,1,0:T(4,128)S(1)}, u32[]{:S(2)}, u32[]{:S(2)}) collective-permute-start(f32[16,3,128]{2,1,0:T(4,128)S(1)} %get-tuple-element.6), channel_id=1, source_target_pairs={{0,3},{1,2},{2,1},{3,0},{4,7},{5,6},{6,5},{7,4},{8,11},{9,10},{10,... | collective-permute-start | bytes 73736 | tf_op jit(solution)/shard_map/ppermute | solution.py:247
  63.9 0.0 collective-permute-start.5
  64.0 0.5 collective-permute-start.4
  64.4 1.1 %collective-permute-done.6 = f32[16,3,128]{2,1,0:T(4,128)S(1)} collective-permute-done((f32[16,3,128]{2,1,0:T(4,128)S(1)}, f32[16,3,128]{2,1,0:T(4,128)S(1)}, u32[]{:S(2)}, u32[]{:S(2)}) %collective-permute-start.6) | collective-permute-done | bytes 24608 | tf_op jit(solution)/shard_map/ppermute | solution.py:247
  65.5 1.2 %collective-permute-done.5 = f32[16,3,128]{2,1,0:T(4,128)S(1)} collective-permute-done((f32[16,3,128]{2,1,0:T(4,128)S(1)}, f32[16,3,128]{2,1,0:T(4,128)S(1)}, u32[]{:S(2)}, u32[]{:S(2)}) %collective-permute-start.5) | collective-permute-done | bytes 24608 | tf_op jit(solution)/shard_map/ppermute | solution.py:247
  66.7 0.0 collective-permute-done.4
  66.8 0.9 %collective-permute-start.8 = (f32[16,3,128]{2,1,0:T(4,128)S(1)}, f32[16,3,128]{2,1,0:T(4,128)S(1)}, u32[]{:S(2)}, u32[]{:S(2)}) collective-permute-start(f32[16,3,128]{2,1,0:T(4,128)S(1)} %get-tuple-element.16.tan_own), channel_id=1, source_target_pairs={{0,252},{4,0},{8,4},{12,8},{16,12},{20,16},{24,20},{28,24},{32,28}... | collective-permute-start | bytes 73736 | tf_op jit(solution)/shard_map/ppermute | solution.py:297
  67.7 1.5 %collective-permute-start.7 = (f32[16,3,128]{2,1,0:T(4,128)S(1)}, f32[16,3,128]{2,1,0:T(4,128)S(1)}, u32[]{:S(2)}, u32[]{:S(2)}) collective-permute-start(f32[16,3,128]{2,1,0:T(4,128)S(1)} %get-tuple-element.16.tan_own), channel_id=1, source_target_pairs={{0,4},{4,8},{8,12},{12,16},{16,20},{20,24},{24,28},{28,32},{32,36}... | collective-permute-start | bytes 73736 | tf_op jit(solution)/shard_map/ppermute | solution.py:296
  69.2 1.3 %collective-permute-done.8.tan_hi = f32[16,3,128]{2,1,0:T(4,128)S(1)} collective-permute-done((f32[16,3,128]{2,1,0:T(4,128)S(1)}, f32[16,3,128]{2,1,0:T(4,128)S(1)}, u32[]{:S(2)}, u32[]{:S(2)}) %collective-permute-start.8) | collective-permute-done | bytes 24608 | tf_op jit(solution)/shard_map/ppermute | solution.py:297
  70.5 6.3 %collective-permute-done.7.tan_lo = f32[16,3,128]{2,1,0:T(4,128)S(1)} collective-permute-done((f32[16,3,128]{2,1,0:T(4,128)S(1)}, f32[16,3,128]{2,1,0:T(4,128)S(1)}, u32[]{:S(2)}, u32[]{:S(2)}) %collective-permute-start.7) | collective-permute-done | bytes 24608 | tf_op jit(solution)/shard_map/ppermute | solution.py:296
  76.8 8.5 %variance_gradient.1 = f32[16,3,128]{2,1,0:T(4,128)S(1)} custom-call(s32[96]{0:T(128)S(1)} %reshape.10.idx_ref, s32[16]{0:T(128)S(1)} %copy-done.2, bf16[48,16,128]{2,1,0:T(8,128)(2,1)S(1)} %get-tuple-element.7.pos_ref, f32[16,3,128]{2,1,0:T(4,128)S(1)} %get-tuple-element.16.tan_own, f32[16,3,128]{2,1,0:T(4,128)S(1)} %collective-permute-done.7.tan_lo, ...), custom_call_target="tpu_custom_call" | custom-call | tf_op jit(solution)/shard_map/variance_gradient/pallas_call | solution.py:299
  85.3 3.4 %collective-permute-start.11 = (f32[16,3,128]{2,1,0:T(4,128)S(1)}, f32[16,3,128]{2,1,0:T(4,128)S(1)}, u32[]{:S(2)}, u32[]{:S(2)}) collective-permute-start(f32[16,3,128]{2,1,0:T(4,128)S(1)} %variance_gradient.1), channel_id=1, source_target_pairs={{0,3},{1,2},{2,1},{3,0},{4,7},{5,6},{6,5},{7,4},{8,11},{9,10},{10,... | collective-permute-start | bytes 73736 | tf_op jit(solution)/shard_map/ppermute | solution.py:247
  88.7 0.2 collective-permute-start.10
  89.0 0.3 collective-permute-start.9
  89.2 0.6 copy.23
  89.8 1.0 %collective-permute-done.11 = f32[16,3,128]{2,1,0:T(4,128)S(1)} collective-permute-done((f32[16,3,128]{2,1,0:T(4,128)S(1)}, f32[16,3,128]{2,1,0:T(4,128)S(1)}, u32[]{:S(2)}, u32[]{:S(2)}) %collective-permute-start.11) | collective-permute-done | bytes 24608 | tf_op jit(solution)/shard_map/ppermute | solution.py:247
  90.8 0.7 collective-permute-done.10
  91.5 0.0 collective-permute-done.9
  91.5 0.6 copy.24
  (6 shorter events, 0.1 us)
Async XLA Ops:
  4.5 24.1 %collective-permute-start.2 = (bf16[8,144,128]{2,1,0:T(8,128)(2,1)S(1)}, bf16[8,144,128]{2,1,0:T(8,128)(2,1)S(1)}, u32[]{:S(2)}, u32[]{:S(2)}) collective-permute-start(bf16[8,144,128]{2,1,0:T(8,128)(2,1)S(1)} %constant_dynamic-slice_fusion), channel_id=1, source_target_pairs={{0,252},{4,0},{8,4},{12,8},{16,12},{20,16},{24,20},{28,24},{32,28}... | collective-permute-start | bytes 884744 | tf_op jit(solution)/shard_map/ppermute | solution.py:266
  16.0 19.1 %collective-permute-start = (bf16[8,144,128]{2,1,0:T(8,128)(2,1)S(1)}, bf16[8,144,128]{2,1,0:T(8,128)(2,1)S(1)}, u32[]{:S(2)}, u32[]{:S(2)}) collective-permute-start(bf16[8,144,128]{2,1,0:T(8,128)(2,1)S(1)} %constant_dynamic-slice_fusion), channel_id=1, source_target_pairs={{0,4},{4,8},{8,12},{12,16},{16,20},{20,24},{24,28},{28,32},{32,36}... | collective-permute-start | bytes 884744 | tf_op jit(solution)/shard_map/ppermute | solution.py:265
  28.6 9.3 %collective-permute-start.3 = (bf16[8,144,128]{2,1,0:T(8,128)(2,1)S(1)}, bf16[8,144,128]{2,1,0:T(8,128)(2,1)S(1)}, u32[]{:S(2)}, u32[]{:S(2)}) collective-permute-start(bf16[8,144,128]{2,1,0:T(8,128)(2,1)S(1)} %collective-permute-done.2.hi_a), channel_id=1, source_target_pairs={{0,1},{1,0},{2,3},{3,2},{4,5},{5,4},{6,7},{7,6},{8,9},{9,8},{10,11... | collective-permute-start | bytes 884744 | tf_op jit(solution)/shard_map/ppermute | solution.py:269
  35.1 3.1 %collective-permute-start.1 = (bf16[8,144,128]{2,1,0:T(8,128)(2,1)S(1)}, bf16[8,144,128]{2,1,0:T(8,128)(2,1)S(1)}, u32[]{:S(2)}, u32[]{:S(2)}) collective-permute-start(bf16[8,144,128]{2,1,0:T(8,128)(2,1)S(1)} %collective-permute-done.lo_a), channel_id=1, source_target_pairs={{0,1},{1,0},{2,3},{3,2},{4,5},{5,4},{6,7},{7,6},{8,9},{9,8},{10,11... | collective-permute-start | bytes 884744 | tf_op jit(solution)/shard_map/ppermute | solution.py:268
  38.2 0.9 copy-start
  39.1 0.8 copy-start.1
  39.9 0.7 copy-start.2
  40.5 0.7 copy-start.3
  61.7 3.8 %collective-permute-start.6 = (f32[16,3,128]{2,1,0:T(4,128)S(1)}, f32[16,3,128]{2,1,0:T(4,128)S(1)}, u32[]{:S(2)}, u32[]{:S(2)}) collective-permute-start(f32[16,3,128]{2,1,0:T(4,128)S(1)} %get-tuple-element.6), channel_id=1, source_target_pairs={{0,3},{1,2},{2,1},{3,0},{4,7},{5,6},{6,5},{7,4},{8,11},{9,10},{10,... | collective-permute-start | bytes 73736 | tf_op jit(solution)/shard_map/ppermute | solution.py:247
  63.9 2.8 %collective-permute-start.5 = (f32[16,3,128]{2,1,0:T(4,128)S(1)}, f32[16,3,128]{2,1,0:T(4,128)S(1)}, u32[]{:S(2)}, u32[]{:S(2)}) collective-permute-start(f32[16,3,128]{2,1,0:T(4,128)S(1)} %get-tuple-element.6), channel_id=1, source_target_pairs={{0,2},{1,3},{2,0},{3,1},{4,6},{5,7},{6,4},{7,5},{8,10},{9,11},{10,... | collective-permute-start | bytes 73736 | tf_op jit(solution)/shard_map/ppermute | solution.py:247
  64.0 2.8 %collective-permute-start.4 = (f32[16,3,128]{2,1,0:T(4,128)S(1)}, f32[16,3,128]{2,1,0:T(4,128)S(1)}, u32[]{:S(2)}, u32[]{:S(2)}) collective-permute-start(f32[16,3,128]{2,1,0:T(4,128)S(1)} %get-tuple-element.6), channel_id=1, source_target_pairs={{0,1},{1,0},{2,3},{3,2},{4,5},{5,4},{6,7},{7,6},{8,9},{9,8},{10,11... | collective-permute-start | bytes 73736 | tf_op jit(solution)/shard_map/ppermute | solution.py:247
  66.8 3.7 %collective-permute-start.8 = (f32[16,3,128]{2,1,0:T(4,128)S(1)}, f32[16,3,128]{2,1,0:T(4,128)S(1)}, u32[]{:S(2)}, u32[]{:S(2)}) collective-permute-start(f32[16,3,128]{2,1,0:T(4,128)S(1)} %get-tuple-element.16.tan_own), channel_id=1, source_target_pairs={{0,252},{4,0},{8,4},{12,8},{16,12},{20,16},{24,20},{28,24},{32,28}... | collective-permute-start | bytes 73736 | tf_op jit(solution)/shard_map/ppermute | solution.py:297
  67.7 9.1 %collective-permute-start.7 = (f32[16,3,128]{2,1,0:T(4,128)S(1)}, f32[16,3,128]{2,1,0:T(4,128)S(1)}, u32[]{:S(2)}, u32[]{:S(2)}) collective-permute-start(f32[16,3,128]{2,1,0:T(4,128)S(1)} %get-tuple-element.16.tan_own), channel_id=1, source_target_pairs={{0,4},{4,8},{8,12},{12,16},{16,20},{20,24},{24,28},{28,32},{32,36}... | collective-permute-start | bytes 73736 | tf_op jit(solution)/shard_map/ppermute | solution.py:296
  85.3 5.5 %collective-permute-start.11 = (f32[16,3,128]{2,1,0:T(4,128)S(1)}, f32[16,3,128]{2,1,0:T(4,128)S(1)}, u32[]{:S(2)}, u32[]{:S(2)}) collective-permute-start(f32[16,3,128]{2,1,0:T(4,128)S(1)} %variance_gradient.1), channel_id=1, source_target_pairs={{0,3},{1,2},{2,1},{3,0},{4,7},{5,6},{6,5},{7,4},{8,11},{9,10},{10,... | collective-permute-start | bytes 73736 | tf_op jit(solution)/shard_map/ppermute | solution.py:247
  88.7 2.8 %collective-permute-start.10 = (f32[16,3,128]{2,1,0:T(4,128)S(1)}, f32[16,3,128]{2,1,0:T(4,128)S(1)}, u32[]{:S(2)}, u32[]{:S(2)}) collective-permute-start(f32[16,3,128]{2,1,0:T(4,128)S(1)} %variance_gradient.1), channel_id=1, source_target_pairs={{0,2},{1,3},{2,0},{3,1},{4,6},{5,7},{6,4},{7,5},{8,10},{9,11},{10,... | collective-permute-start | bytes 73736 | tf_op jit(solution)/shard_map/ppermute | solution.py:247
  89.0 2.5 %collective-permute-start.9 = (f32[16,3,128]{2,1,0:T(4,128)S(1)}, f32[16,3,128]{2,1,0:T(4,128)S(1)}, u32[]{:S(2)}, u32[]{:S(2)}) collective-permute-start(f32[16,3,128]{2,1,0:T(4,128)S(1)} %variance_gradient.1), channel_id=1, source_target_pairs={{0,1},{1,0},{2,3},{3,2},{4,5},{5,4},{6,7},{7,6},{8,9},{9,8},{10,11... | collective-permute-start | bytes 73736 | tf_op jit(solution)/shard_map/ppermute | solution.py:247

commit v4 on v2

v4 whole, which is shorter than its diff:
```python
import functools
import math

import jax
import jax.numpy as jnp
from jax import lax
from jax.experimental import pallas as pl
from jax.experimental.pallas import tpu as pltpu
from jax.sharding import PartitionSpec as P

STEP_BLOCKS = 4
CHUNK = 32
PIECES = 3
TILE = 16
LOG2E = 1.4426950408889634


def ring(axis, shift):
    count = lax.axis_size(axis)
    return [(i, (i + shift) % count) for i in range(count)]


def flip(axis, bit):
    return [(i, i ^ bit) for i in range(lax.axis_size(axis))]


def place(rows, row, value):
    at = lax.broadcasted_iota(jnp.int32, rows.shape, 0) == row
    return jnp.where(at, value, rows)


def pattern(depth, base, axis, width, value):
    row = lax.broadcasted_iota(jnp.int32, (depth, width), 0)
    hit = row == base + axis
    for piece in range(1, PIECES):
        hit = hit | (row == base + 3 * piece + axis)
    return jnp.where(hit, value, 0.0)


def difference_rhs(rows, axis, depth):
    rhs = pattern(depth, 0, axis, rows.shape[1], -1.0)
    for piece in range(PIECES):
        at = 3 * piece + axis
        rhs = place(rhs, 3 * PIECES + piece, rows[at:at + 1])
    return rhs.astype(jnp.bfloat16)


def change_rhs(pieces, axis, depth):
    rhs = pattern(depth, TILE, axis, pieces[0].shape[1], 1.0)
    for piece in range(PIECES):
        rhs = place(rhs, 3 * PIECES + piece, -pieces[piece][axis:axis + 1])
    return rhs.astype(jnp.bfloat16)


def split(array):
    pieces = []
    rest = array
    for _ in range(PIECES):
        piece = rest.astype(jnp.bfloat16).astype(jnp.float32)
        pieces.append(piece)
        rest = rest - piece
    return pieces


def coefficients(rate_ref, bases, sigma):
    rate = [rate_ref[k] for k in range(bases)]
    decay = [-LOG2E * r for r in rate]
    slope = [(-2.0 * sigma) * r for r in rate]
    bend = [(4.0 * sigma) * r * r for r in rate]
    return decay, slope, bend


def pair_terms(delta, dots, coefs, sigma):
    decay, slope_coef, bend_coef = coefs
    bases = len(dots)
    square = delta[0] * delta[0] + delta[1] * delta[1] + delta[2] * delta[2]
    w = [jnp.exp2(decay[k] * square) * dots[k] for k in range(bases)]
    lh = (0.5 * sigma) * sum(w[1:], w[0])
    slope = sum([slope_coef[k] * w[k] for k in range(1, bases)], slope_coef[0] * w[0])
    bend = sum([bend_coef[k] * w[k] for k in range(1, bases)], bend_coef[0] * w[0])
    h = jnp.tanh(lh)
    u = 1.0 - h * h
    p1 = (1.0 + h) + lh * u
    p2 = u * (1.0 - lh * h)
    return p1 * slope, p2 * (slope * slope) + p1 * bend


def slot_terms(right, left, cols, separators, coefs, sigma, total, store):
    channels = left.shape[1] // len(coefs[0])
    rows = left.shape[0]
    parts = [jnp.dot(cols, r, preferred_element_type=jnp.float32) for r in separators]
    dots = [
        lax.dot_general(
            right[:, k * channels:(k + 1) * channels],
            left[:, k * channels:(k + 1) * channels],
            (((1,), (1,)), ((), ())),
            preferred_element_type=jnp.float32,
        )
        for k in range(len(coefs[0]))
    ]
    for start in range(0, rows, CHUNK):
        delta = [p[start:start + CHUNK] for p in parts]
        first, second = pair_terms(delta, [d[start:start + CHUNK] for d in dots], coefs, sigma)
        store(start, first, second)
        for a in range(3):
            total[a] = total[a] + jnp.sum((first * delta[a]).reshape(CHUNK // 8, 8, rows), axis=0)


def gather_rows(total, factor):
    return jnp.concatenate([factor * jnp.sum(t, axis=0, keepdims=True) for t in total], axis=0)


def project(x, embed_ref, wproj_ref):
    h = jnp.dot(x, embed_ref[...], preferred_element_type=jnp.float32)
    half_h = 0.5 * h
    hidden = (half_h + half_h * jnp.tanh(half_h)).astype(jnp.bfloat16)
    out = jnp.dot(hidden, wproj_ref[...], preferred_element_type=jnp.float32)
    return out.astype(jnp.bfloat16)


def own_kernel(slots, rate_ref, own_ref, pos_ref, embed_ref, wproj_ref,
               force_ref, first_ref, second_ref, tile_ref, proj_ref):
    rows, channels = own_ref.shape[1:]
    bases = wproj_ref.shape[1] // channels
    escale = 1.0 / math.sqrt(slots * rows)
    sigma = 1.0 / math.sqrt(channels)
    coefs = coefficients(rate_ref, bases, sigma)
    flat = own_ref[...].reshape(STEP_BLOCKS * rows, channels)
    proj_ref[...] = project(flat, embed_ref, wproj_ref).reshape(STEP_BLOCKS, rows, bases * channels)
    for part in range(STEP_BLOCKS):
        ones = jnp.ones((PIECES, rows), jnp.float32)
        zeros = jnp.zeros((TILE - 4 * PIECES, rows), jnp.float32)
        tile = jnp.concatenate(split(pos_ref[part]) + [ones, zeros], axis=0)
        tile_ref[part] = tile.astype(jnp.bfloat16)
        cols = jnp.transpose(tile).astype(jnp.bfloat16)
        separators = [difference_rhs(tile, a, TILE) for a in range(3)]
        total = [jnp.zeros((8, rows), jnp.float32) for _ in range(3)]

        def store(start, first, second, part=part):
            first_ref[part, start:start + CHUNK, :] = first
            second_ref[part, start:start + CHUNK, :] = second

        left = proj_ref[part]
        slot_terms(left, left, cols, separators, coefs, sigma, total, store)
        force_ref[part] = gather_rows(total, -0.5 * escale)


def pair_kernel(
    nbr_ref, cnt_ref, rate_ref, meta_ref,
    own_proj, lo_a, lo_b, hi_a, hi_b, embed_ref, wproj_ref, own_tile, part_ref,
    force_ref, first_ref, second_ref, rows_ref,
    proj_ref, col_ref, sem,
):
    owned = own_tile.shape[0]
    half = lo_a.shape[0]
    slots = nbr_ref.shape[1]
    rows = first_ref.shape[2]
    channels = embed_ref.shape[0]
    bases = wproj_ref.shape[1] // channels
    escale = 1.0 / math.sqrt(slots * rows)
    sigma = 1.0 / math.sqrt(channels)
    step = pl.program_id(0)

    @pl.when(step == 0)
    def _():
        copy = pltpu.make_async_copy(own_proj, proj_ref.at[pl.ds(owned, owned)], sem)
        copy.start()

        def keep(tile, at):
            rows_ref[at] = tile
            col_ref[at] = jnp.transpose(tile.astype(jnp.float32)).astype(jnp.bfloat16)

        def take(source, base):
            def one(i, carry):
                x = source[pl.ds(2 * i, 2), pl.ds(0, rows), :].reshape(2 * rows, channels)
                out = project(x, embed_ref, wproj_ref)
                proj_ref[pl.ds(base + 2 * i, 2)] = out.reshape(2, rows, bases * channels)
                for j in range(2):
                    keep(source[2 * i + j, pl.ds(rows, TILE), :], base + 2 * i + j)
                return carry

            lax.fori_loop(0, half // 2, one, 0, unroll=4)

        near = meta_ref[1] * half
        far = half - near
        take(lo_a, near)
        take(hi_a, 2 * owned + near)
        take(lo_b, far)
        take(hi_b, 2 * owned + far)

        def own(i, carry):
            keep(own_tile[i], owned + i)
            return carry

        lax.fori_loop(0, owned, own, 0, unroll=4)
        copy.wait()

    coefs = coefficients(rate_ref, bases, sigma)
    offset = meta_ref[0]
    total_blocks = meta_ref[2]

    def one_block(part, carry):
        block = step * STEP_BLOCKS + part
        count = cnt_ref[block]

        def run(live):
            left = proj_ref[owned + block]
            tile = own_tile[block].astype(jnp.float32)
            separators = [difference_rhs(tile, a, TILE) for a in range(3)]
            total = [jnp.zeros((8, rows), jnp.float32) for _ in range(3)]
            for slot in range(1, live):
                source = nbr_ref[block, slot] - offset
                source = jnp.where(source < 0, source + total_blocks, source)
                source = jnp.where(source >= total_blocks, source - total_blocks, source)

                def store(start, first, second, slot=slot):
                    first_ref[part, slot - 1, start:start + CHUNK, :] = first
                    second_ref[part, slot - 1, start:start + CHUNK, :] = second

                slot_terms(proj_ref[source], left, col_ref[source], separators, coefs, sigma, total, store)
            force_ref[part] = part_ref[part] + gather_rows(total, -0.5 * escale)

        for live in range(3, slots + 1):
            pl.when(count == live)(lambda live=live: run(live))
        return carry

    lax.fori_loop(0, STEP_BLOCKS, one_block, 0)


def grad_kernel(
    nbr_ref, cnt_ref, meta_ref, pos_ref, tan_own, tan_lo, tan_hi,
    own_first, own_second, first_ref, second_ref,
    grad_ref, col_ref,
):
    owned = tan_own.shape[0]
    slots = nbr_ref.shape[1]
    rows = first_ref.shape[2]
    escale = 1.0 / math.sqrt(slots * rows)
    step = pl.program_id(0)

    @pl.when(step == 0)
    def _():
        def spread(tan, base):
            def one(i, carry):
                filler = jnp.zeros((TILE - 3 * PIECES, rows), jnp.float32)
                tile = jnp.concatenate(
                    [pos_ref[base + i].astype(jnp.float32)] + split(tan[i]) + [filler], axis=0
                )
                col_ref[base + i] = jnp.transpose(tile).astype(jnp.bfloat16)
                return carry

            lax.fori_loop(0, owned, one, 0, unroll=4)

        spread(tan_lo, 0)
        spread(tan_own, owned)
        spread(tan_hi, 2 * owned)

    offset = meta_ref[0]
    total_blocks = meta_ref[2]

    def one_block(part, carry):
        block = step * STEP_BLOCKS + part
        count = cnt_ref[block]

        def run(live):
            tile = pos_ref[owned + block].astype(jnp.float32)
            pieces = split(tan_own[block])
            sides = [difference_rhs(tile, a, 2 * TILE) for a in range(3)]
            sides += [change_rhs(pieces, a, 2 * TILE) for a in range(3)]
            total = [jnp.zeros((8, rows), jnp.float32) for _ in range(3)]
            for slot in range(live):
                source = owned + block
                if slot:
                    source = nbr_ref[block, slot] - offset
                    source = jnp.where(source < 0, source + total_blocks, source)
                    source = jnp.where(source >= total_blocks, source - total_blocks, source)
                cols = col_ref[source]
                parts = [jnp.dot(cols, r, preferred_element_type=jnp.float32) for r in sides]
                for start in range(0, rows, CHUNK):
                    delta = [p[start:start + CHUNK] for p in parts[:3]]
                    change = [p[start:start + CHUNK] for p in parts[3:]]
                    span = slice(start, start + CHUNK)
                    first = first_ref[part, slot - 1, span, :] if slot else own_first[part, span, :]
                    second = second_ref[part, slot - 1, span, :] if slot else own_second[part, span, :]
                    along = second * (delta[0] * change[0] + delta[1] * change[1] + delta[2] * change[2])
                    for a in range(3):
                        term = first * change[a] + along * delta[a]
                        total[a] = total[a] + jnp.sum(term.reshape(CHUNK // 8, 8, rows), axis=0)
            grad_ref[part] = gather_rows(total, 0.5 * escale)

        for live in range(3, slots + 1):
            pl.when(count == live)(lambda live=live: run(live))
        return carry

    lax.fori_loop(0, STEP_BLOCKS, one_block, 0)


def pack_kernel(meta_ref, feat_ref, pos_ref, out_ref):
    blocks, rows, _ = feat_ref.shape
    out_ref[:, pl.ds(0, rows), :] = feat_ref[...]
    ones = jnp.ones((PIECES, rows), jnp.float32)
    zeros = jnp.zeros((TILE - 4 * PIECES, rows), jnp.float32)
    for i in range(blocks):
        tile = jnp.concatenate(split(pos_ref[i]) + [ones, zeros], axis=0)
        out_ref[i, pl.ds(rows, TILE), :] = tile.astype(jnp.bfloat16)


def in_hbm(array):
    return pltpu.with_memory_space_constraint(array, pltpu.HBM)


def whole(array):
    return pl.BlockSpec(array.shape, lambda *_: (0,) * len(array.shape), pipeline_mode=pl.Buffered(1))


def stepped(shape):
    return pl.BlockSpec((STEP_BLOCKS,) + shape, lambda i, *_: (i,) + (0,) * len(shape))


def member_sum(array):
    size = lax.axis_size("member")
    others = [lax.ppermute(array, "member", flip("member", bit)) for bit in range(1, size)]
    return array + others[0] + (others[1] + others[2])


def body(positions, features, nbr_list, nbr_count, w_embed, w_proj, rates):
    owned, dims, rows = positions.shape
    channels = features.shape[2]
    slots = nbr_list.shape[1]
    width = w_proj.shape[2]
    domains = lax.axis_size("space")
    members = lax.axis_size("member")
    domain = lax.axis_index("space")
    core = lax.axis_index("member") % 2
    up, down = ring("space", 1), ring("space", -1)
    half = owned // 2

    offset = (domain - 1) * owned
    meta = jnp.stack([offset, core, jnp.int32(domains * owned)]).astype(jnp.int32)
    embed, proj = in_hbm(w_embed[0]), in_hbm(w_proj[0])
    rate, counts = in_hbm(rates[0]), in_hbm(nbr_count)
    mine = pl.pallas_call(
        pack_kernel,
        grid_spec=pltpu.PrefetchScalarGridSpec(
            num_scalar_prefetch=1,
            grid=(1,),
            in_specs=[
                pl.BlockSpec((half, rows, channels), lambda i, m: (m[1], 0, 0)),
                pl.BlockSpec((half, dims, rows), lambda i, m: (m[1], 0, 0)),
            ],
            out_specs=pl.BlockSpec((half, rows + TILE, channels), lambda i, m: (0, 0, 0)),
        ),
        out_shape=jax.ShapeDtypeStruct((half, rows + TILE, channels), jnp.bfloat16),
        compiler_params=pltpu.CompilerParams(vmem_limit_bytes=8 << 20),
        name="pack_halo",
    )(meta, in_hbm(features), positions)
    lo_a = lax.ppermute(mine, "space", up)
    hi_a = lax.ppermute(mine, "space", down)
    pair = (rows, rows)
    selfs = jax.ShapeDtypeStruct((owned,) + pair, jnp.float32)
    pairs = jax.ShapeDtypeStruct((owned, slots - 1) + pair, jnp.float32)
    small = jax.ShapeDtypeStruct((owned, dims, rows), jnp.float32)
    tiles = jax.ShapeDtypeStruct((owned, TILE, rows), jnp.bfloat16)
    window = jax.ShapeDtypeStruct((3 * owned, TILE, rows), jnp.bfloat16)
    table = jax.ShapeDtypeStruct((owned, rows, width), jnp.bfloat16)
    steps = (owned // STEP_BLOCKS,)
    part_force, own_first, own_second, own_tile, own_proj = pl.pallas_call(
        functools.partial(own_kernel, slots),
        grid_spec=pltpu.PrefetchScalarGridSpec(
            num_scalar_prefetch=1,
            grid=steps,
            in_specs=[stepped((rows, channels)), stepped((dims, rows)), whole(w_embed[0]), whole(w_proj[0])],
            out_specs=[
                stepped((dims, rows)), stepped(pair), stepped(pair),
                stepped((TILE, rows)), stepped((rows, width)),
            ],
        ),
        out_shape=[small, selfs, selfs, tiles, table],
        compiler_params=pltpu.CompilerParams(vmem_limit_bytes=8 << 20),
        name="own_pairs",
    )(rate, in_hbm(features), positions, embed, proj)
    lo_a, hi_a, own_tile = lax.optimization_barrier((lo_a, hi_a, own_tile))
    swap = flip("member", 1)
    lo_b = lax.ppermute(lo_a, "member", swap)
    hi_b = lax.ppermute(hi_a, "member", swap)
    halo = (lo_a, lo_b, hi_a, hi_b, embed, proj, own_tile)
    force, first, second, pos_rows = pl.pallas_call(
        pair_kernel,
        grid_spec=pltpu.PrefetchScalarGridSpec(
            num_scalar_prefetch=4,
            grid=steps,
            in_specs=[pl.BlockSpec(memory_space=pl.ANY)] + [whole(t) for t in halo] + [stepped((dims, rows))],
            out_specs=[
                stepped((dims, rows)), stepped((slots - 1,) + pair), stepped((slots - 1,) + pair), whole(window),
            ],
            scratch_shapes=[
                pltpu.VMEM((3 * owned, rows, width), jnp.bfloat16),
                pltpu.VMEM((3 * owned, rows, TILE), jnp.bfloat16),
                pltpu.SemaphoreType.DMA,
            ],
        ),
        out_shape=[small, pairs, pairs, window],
        compiler_params=pltpu.CompilerParams(vmem_limit_bytes=18 << 20),
        name="halo_pairs",
    )(nbr_list, counts, rate, meta, own_proj, *halo, in_hbm(part_force))

    mean_force = member_sum(force) / members
    tangent = (2.0 / members) * (force - mean_force)
    tan_lo = lax.ppermute(tangent, "space", up)
    tan_hi = lax.ppermute(tangent, "space", down)
    tensors = (pos_rows, tangent, tan_lo, tan_hi)
    grad = pl.pallas_call(
        grad_kernel,
        grid_spec=pltpu.PrefetchScalarGridSpec(
            num_scalar_prefetch=3,
            grid=steps,
            in_specs=[whole(t) for t in tensors] + [stepped(pair)] * 2 + [stepped((slots - 1,) + pair)] * 2,
            out_specs=stepped((dims, rows)),
            scratch_shapes=[pltpu.VMEM((3 * owned, rows, 2 * TILE), jnp.bfloat16)],
        ),
        out_shape=small,
        compiler_params=pltpu.CompilerParams(vmem_limit_bytes=10 << 20),
        name="variance_gradient",
    )(nbr_list, counts, meta, *tensors, in_hbm(own_first), in_hbm(own_second), first, second)
    return (mean_force, member_sum(grad))


def solution(mesh):
    return jax.shard_map(
        body,
        mesh=mesh,
        in_specs=(
            P("space", None, None),
            P("space", None, None),
            P("space", None),
            P("space"),
            P("member", None, None),
            P("member", None, None),
            P("member", None),
        ),
        out_specs=(P("space", None, None), P("space", None, None)),
        check_vma=False,
    )
```

time: 100 us -> 85.7 us (0.86)
  waiting for transfers between devices: 29.3 us -> 23.7 us
  Pallas kernels: 38.1 us -> 33.7 us
  other arithmetic: 3.77 us -> 0.12 us
    pallas_call x1, Pallas kernels: 26.2 us -> 16.4 us  [body(): pl.pallas_call(pair_kernel, grid_spec=pltpu.PrefetchScalarGridSpec(num_sc...]
    ppermute x1, waiting for transfers between devices: 12.6 us -> 3.97 us  [body(): hi_a = lax.ppermute(mine, 'space', down)]
    pallas_call x0 -> x2, Pallas kernels: none -> 7.52 us  [the longest x1 6 us: body(): pl.pallas_call(functools.partial(own_kernel, slots), grid_spec=pltpu.Pref...]
    unnamed x18 -> x10, local copies, waits for them, and re-layouts: 2.62 us -> 5.32 us
    concatenate x1 -> x0, local copies, waits for them, and re-layouts: 2.2 us -> none  [pack(): return jnp.concatenate([features] + pieces + [ones, zeros], axis=1)]
    pallas_call x1, Pallas kernels: 12 us -> 9.82 us  [body(): pl.pallas_call(grad_kernel, grid_spec=pltpu.PrefetchScalarGridSpec(num_sc...]
    ppermute x1, starting transfers between devices: 0.08 us -> 1.77 us  [body(): tan_hi = lax.ppermute(tangent, 'space', down)]
    ppermute x1, starting transfers between devices: 2.35 us -> 0.67 us  [body(): tan_lo = lax.ppermute(tangent, 'space', up)]
  transfers between devices with their start and end apart: 12 -> 12, of which waited for: 8 -> 10; matrix products, arithmetic and copies ran while one was open for 2% -> 2% of each run, Pallas kernels for 0% -> 7%
where the time goes in v4:
time: 85.7 us; the launch traced here: 86.1 us
  Pallas kernels  33.7 us (39%)
  waiting for transfers between devices  23.7 us (28%)
  starting transfers between devices  22.6 us (26%)
  local copies, waits for them, and re-layouts  5.32 us (6%)
    pallas_call x1, Pallas kernels, body(): pl.pallas_call(pair_kernel, grid_spec=pltpu.PrefetchScalarGridSpec(num_sc...  16.4 us
    ppermute x1, starting transfers between devices, body(): hi_a = lax.ppermute(mine, 'space', down)  11.6 us
    pallas_call x1, Pallas kernels, body(): pl.pallas_call(grad_kernel, grid_spec=pltpu.PrefetchScalarGridSpec(num_sc...  9.82 us
    ppermute x1, waiting for transfers between devices, body(): tan_lo = lax.ppermute(tangent, 'space', up)  7.02 us
    ppermute x6, starting transfers between devices, member_sum(): lax.ppermute(array, 'member', flip('member', bit))  6.68 us
    ppermute x1, waiting for transfers between devices, body(): lo_a = lax.ppermute(mine, 'space', up)  6.5 us
    pallas_call x1, Pallas kernels, body(): pl.pallas_call(functools.partial(own_kernel, slots), grid_spec=pltpu.Pref...  6 us
    unnamed x10, local copies, waits for them, and re-layouts  5.32 us
  transfers between devices with their start and end apart: 12, of which 10 were waited for; matrix products, arithmetic and copies ran while one was open for 2% of the time, Pallas kernels for 7%

profile of v4, /device:TPU:1, one launch (start us, length us, event | category | flops | bytes accessed | tf_op | source)
XLA Modules:
  0.0 86.1 jit_solution(15731703459471760060)
XLA Ops:
  0.6 0.8 copy.9.pos_ref
  1.4 0.1 pad_add_fusion.meta_ref
  1.5 1.5 %pack_halo.1 = bf16[8,144,128]{2,1,0:T(8,128)(2,1)S(1)} custom-call(s32[3]{0:T(128)S(1)} %pad_add_fusion.meta_ref, bf16[16,128,128]{2,1,0:T(8,128)(2,1)} %feat_ref.1, f32[16,3,128]{2,1,0:T(4,128)S(1)} %copy.9.pos_ref), custom_call_target="tpu_custom_call" | custom-call | tf_op jit(solution)/shard_map/pack_halo/pallas_call | solution.py:342
  3.0 11.6 %collective-permute-start.1 = (bf16[8,144,128]{2,1,0:T(8,128)(2,1)S(1)}, bf16[8,144,128]{2,1,0:T(8,128)(2,1)S(1)}, u32[]{:S(2)}, u32[]{:S(2)}) collective-permute-start(bf16[8,144,128]{2,1,0:T(8,128)(2,1)S(1)} %pack_halo.1), channel_id=1, source_target_pairs={{0,252},{4,0},{8,4},{12,8},{16,12},{20,16},{24,20},{28,24},{32,28}... | collective-permute-start | bytes 884744 | tf_op jit(solution)/shard_map/ppermute | solution.py:358
  14.6 0.0 collective-permute-start
  14.6 6.0 %own_pairs.1 = (f32[16,3,128]{2,1,0:T(4,128)S(1)}, f32[16,128,128]{2,1,0:T(8,128)S(1)}, f32[16,128,128]{2,1,0:T(8,128)S(1)}, bf16[16,16,128]{2,1,0:T(8,128)(2,1)S(1)}, bf16[16,128,512]{2,1,0:T(8,128)(2,1)S(1)}) custom-call(f32[4]{0:T(128)} %bitcast.9, bf16[16,128,128]{2,1,0:T(8,128)(2,1)} %feat_ref.1, f32[16,3,128]{2,1,0:T(4,128)S(1)} %copy.9.pos_ref, ...), custom_call_target="tpu_custom_call" | custom-call | tf_op jit(solution)/shard_map/own_pairs/pallas_call | solution.py:367
  20.6 0.0 copy-start
  20.6 1.0 %copy-done = f32[16,128,128]{2,1,0:T(8,128)} copy-done((f32[16,128,128]{2,1,0:T(8,128)}, f32[16,128,128]{2,1,0:T(8,128)S(1)}, u32[]{:S(2)}) %copy-start) | copy-done | bytes 1048600
  21.6 0.0 copy-start.1
  21.6 1.0 %copy-done.1 = f32[16,128,128]{2,1,0:T(8,128)} copy-done((f32[16,128,128]{2,1,0:T(8,128)}, f32[16,128,128]{2,1,0:T(8,128)S(1)}, u32[]{:S(2)}) %copy-start.1) | copy-done | bytes 1048600
  22.6 0.0 copy-start.2
  22.6 0.6 copy-done.2
  23.2 4.0 %collective-permute-done.1.hi_a = bf16[8,144,128]{2,1,0:T(8,128)(2,1)S(1)} collective-permute-done((bf16[8,144,128]{2,1,0:T(8,128)(2,1)S(1)}, bf16[8,144,128]{2,1,0:T(8,128)(2,1)S(1)}, u32[]{:S(2)}, u32[]{:S(2)}) %collective-permute-start.1) | collective-permute-done | bytes 294944 | tf_op jit(solution)/shard_map/ppermute | solution.py:358
  27.2 6.5 %collective-permute-done.lo_a = bf16[8,144,128]{2,1,0:T(8,128)(2,1)S(1)} collective-permute-done((bf16[8,144,128]{2,1,0:T(8,128)(2,1)S(1)}, bf16[8,144,128]{2,1,0:T(8,128)(2,1)S(1)}, u32[]{:S(2)}, u32[]{:S(2)}) %collective-permute-start) | collective-permute-done | bytes 294944 | tf_op jit(solution)/shard_map/ppermute | solution.py:357
  33.7 1.9 %collective-permute-start.2 = (bf16[8,144,128]{2,1,0:T(8,128)(2,1)S(1)}, bf16[8,144,128]{2,1,0:T(8,128)(2,1)S(1)}, u32[]{:S(2)}, u32[]{:S(2)}) collective-permute-start(bf16[8,144,128]{2,1,0:T(8,128)(2,1)S(1)} %collective-permute-done.lo_a), channel_id=1, source_target_pairs={{0,1},{1,0},{2,3},{3,2},{4,5},{5,4},{6,7},{7,6},{8,9},{9,8},{10,11... | collective-permute-start | bytes 884744 | tf_op jit(solution)/shard_map/ppermute | solution.py:384
  35.5 0.0 collective-permute-start.3
  35.5 0.8 copy.11.nbr_ref
  36.3 0.4 collective-permute-done.2.lo_b
  36.8 0.4 collective-permute-done.3.hi_b
  37.2 16.4 %halo_pairs.1 = (f32[16,3,128]{2,1,0:T(4,128)S(1)}, f32[16,5,128,128]{3,2,1,0:T(8,128)S(1)}, f32[16,5,128,128]{3,2,1,0:T(8,128)S(1)}, bf16[48,16,128]{2,1,0:T(8,128)(2,1)S(1)}) custom-call(s32[16,6]{1,0:T(8,128)S(1)} %copy.11.nbr_ref, s32[16]{0:T(128)} %cnt_ref.3, f32[4]{0:T(128)} %bitcast.10, s32[3]{0:T(128)S(1)} %pad_add_fusion.meta_ref, ...), custom_call_target="tpu_custom_call" | custom-call | tf_op jit(solution)/shard_map/halo_pairs/pallas_call | solution.py:387
  53.5 2.2 %collective-permute-start.6 = (f32[16,3,128]{2,1,0:T(4,128)S(1)}, f32[16,3,128]{2,1,0:T(4,128)S(1)}, u32[]{:S(2)}, u32[]{:S(2)}) collective-permute-start(f32[16,3,128]{2,1,0:T(4,128)S(1)} %get-tuple-element.20), channel_id=1, source_target_pairs={{0,3},{1,2},{2,1},{3,0},{4,7},{5,6},{6,5},{7,4},{8,11},{9,10},{10,... | collective-permute-start | bytes 73736 | tf_op jit(solution)/shard_map/ppermute | solution.py:322
  55.7 0.0 collective-permute-start.5
  55.7 0.5 collective-permute-start.4
  56.2 1.1 %collective-permute-done.6 = f32[16,3,128]{2,1,0:T(4,128)S(1)} collective-permute-done((f32[16,3,128]{2,1,0:T(4,128)S(1)}, f32[16,3,128]{2,1,0:T(4,128)S(1)}, u32[]{:S(2)}, u32[]{:S(2)}) %collective-permute-start.6) | collective-permute-done | bytes 24608 | tf_op jit(solution)/shard_map/ppermute | solution.py:322
  57.3 1.2 %collective-permute-done.5 = f32[16,3,128]{2,1,0:T(4,128)S(1)} collective-permute-done((f32[16,3,128]{2,1,0:T(4,128)S(1)}, f32[16,3,128]{2,1,0:T(4,128)S(1)}, u32[]{:S(2)}, u32[]{:S(2)}) %collective-permute-start.5) | collective-permute-done | bytes 24608 | tf_op jit(solution)/shard_map/ppermute | solution.py:322
  58.5 0.0 collective-permute-done.4
  58.5 1.8 %collective-permute-start.8 = (f32[16,3,128]{2,1,0:T(4,128)S(1)}, f32[16,3,128]{2,1,0:T(4,128)S(1)}, u32[]{:S(2)}, u32[]{:S(2)}) collective-permute-start(f32[16,3,128]{2,1,0:T(4,128)S(1)} %get-tuple-element.28.tan_own), channel_id=1, source_target_pairs={{0,252},{4,0},{8,4},{12,8},{16,12},{20,16},{24,20},{28,24},{32,28}... | collective-permute-start | bytes 73736 | tf_op jit(solution)/shard_map/ppermute | solution.py:410
  60.3 0.7 collective-permute-start.7
  61.0 1.4 %collective-permute-done.8.tan_hi = f32[16,3,128]{2,1,0:T(4,128)S(1)} collective-permute-done((f32[16,3,128]{2,1,0:T(4,128)S(1)}, f32[16,3,128]{2,1,0:T(4,128)S(1)}, u32[]{:S(2)}, u32[]{:S(2)}) %collective-permute-start.8) | collective-permute-done | bytes 24608 | tf_op jit(solution)/shard_map/ppermute | solution.py:410
  62.4 7.0 %collective-permute-done.7.tan_lo = f32[16,3,128]{2,1,0:T(4,128)S(1)} collective-permute-done((f32[16,3,128]{2,1,0:T(4,128)S(1)}, f32[16,3,128]{2,1,0:T(4,128)S(1)}, u32[]{:S(2)}, u32[]{:S(2)}) %collective-permute-start.7) | collective-permute-done | bytes 24608 | tf_op jit(solution)/shard_map/ppermute | solution.py:409
  69.4 9.8 %variance_gradient.1 = f32[16,3,128]{2,1,0:T(4,128)S(1)} custom-call(s32[16,6]{1,0:T(8,128)S(1)} %copy.11.nbr_ref, s32[16]{0:T(128)} %cnt_ref.3, s32[3]{0:T(128)S(1)} %pad_add_fusion.meta_ref, bf16[48,16,128]{2,1,0:T(8,128)(2,1)S(1)} %get-tuple-element.21.pos_ref, f32[16,3,128]{2,1,0:T(4,128)S(1)} %get-tuple-element.28.tan_own, ...), custom_call_target="tpu_custom_call" | custom-call | tf_op jit(solution)/shard_map/variance_gradient/pallas_call | solution.py:412
  79.2 3.5 %collective-permute-start.11 = (f32[16,3,128]{2,1,0:T(4,128)S(1)}, f32[16,3,128]{2,1,0:T(4,128)S(1)}, u32[]{:S(2)}, u32[]{:S(2)}) collective-permute-start(f32[16,3,128]{2,1,0:T(4,128)S(1)} %variance_gradient.1), channel_id=1, source_target_pairs={{0,3},{1,2},{2,1},{3,0},{4,7},{5,6},{6,5},{7,4},{8,11},{9,10},{10,... | collective-permute-start | bytes 73736 | tf_op jit(solution)/shard_map/ppermute | solution.py:322
  82.7 0.2 collective-permute-start.10
  82.9 0.3 collective-permute-start.9
  83.2 0.6 copy.13
  83.8 0.9 %collective-permute-done.11 = f32[16,3,128]{2,1,0:T(4,128)S(1)} collective-permute-done((f32[16,3,128]{2,1,0:T(4,128)S(1)}, f32[16,3,128]{2,1,0:T(4,128)S(1)}, u32[]{:S(2)}, u32[]{:S(2)}) %collective-permute-start.11) | collective-permute-done | bytes 24608 | tf_op jit(solution)/shard_map/ppermute | solution.py:322
  84.7 0.7 collective-permute-done.10
  85.5 0.0 collective-permute-done.9
  85.5 0.6 copy.14
  (2 shorter events, 0.0 us)
Async XLA Ops:
  3.0 24.1 %collective-permute-start.1 = (bf16[8,144,128]{2,1,0:T(8,128)(2,1)S(1)}, bf16[8,144,128]{2,1,0:T(8,128)(2,1)S(1)}, u32[]{:S(2)}, u32[]{:S(2)}) collective-permute-start(bf16[8,144,128]{2,1,0:T(8,128)(2,1)S(1)} %pack_halo.1), channel_id=1, source_target_pairs={{0,252},{4,0},{8,4},{12,8},{16,12},{20,16},{24,20},{28,24},{32,28}... | collective-permute-start | bytes 884744 | tf_op jit(solution)/shard_map/ppermute | solution.py:358
  14.6 19.1 %collective-permute-start = (bf16[8,144,128]{2,1,0:T(8,128)(2,1)S(1)}, bf16[8,144,128]{2,1,0:T(8,128)(2,1)S(1)}, u32[]{:S(2)}, u32[]{:S(2)}) collective-permute-start(bf16[8,144,128]{2,1,0:T(8,128)(2,1)S(1)} %pack_halo.1), channel_id=1, source_target_pairs={{0,4},{4,8},{8,12},{12,16},{16,20},{20,24},{24,28},{28,32},{32,36}... | collective-permute-start | bytes 884744 | tf_op jit(solution)/shard_map/ppermute | solution.py:357
  20.6 1.0 %copy-start = (f32[16,128,128]{2,1,0:T(8,128)}, f32[16,128,128]{2,1,0:T(8,128)S(1)}, u32[]{:S(2)}) copy-start(f32[16,128,128]{2,1,0:T(8,128)S(1)} %get-tuple-element.22.own_first) | copy-start | bytes 3145732
  21.6 1.0 %copy-start.1 = (f32[16,128,128]{2,1,0:T(8,128)}, f32[16,128,128]{2,1,0:T(8,128)S(1)}, u32[]{:S(2)}) copy-start(f32[16,128,128]{2,1,0:T(8,128)S(1)} %get-tuple-element.23.own_second) | copy-start | bytes 3145732
  22.6 0.6 copy-start.2
  33.7 3.1 %collective-permute-start.2 = (bf16[8,144,128]{2,1,0:T(8,128)(2,1)S(1)}, bf16[8,144,128]{2,1,0:T(8,128)(2,1)S(1)}, u32[]{:S(2)}, u32[]{:S(2)}) collective-permute-start(bf16[8,144,128]{2,1,0:T(8,128)(2,1)S(1)} %collective-permute-done.lo_a), channel_id=1, source_target_pairs={{0,1},{1,0},{2,3},{3,2},{4,5},{5,4},{6,7},{7,6},{8,9},{9,8},{10,11... | collective-permute-start | bytes 884744 | tf_op jit(solution)/shard_map/ppermute | solution.py:384
  35.5 1.6 %collective-permute-start.3 = (bf16[8,144,128]{2,1,0:T(8,128)(2,1)S(1)}, bf16[8,144,128]{2,1,0:T(8,128)(2,1)S(1)}, u32[]{:S(2)}, u32[]{:S(2)}) collective-permute-start(bf16[8,144,128]{2,1,0:T(8,128)(2,1)S(1)} %collective-permute-done.1.hi_a), channel_id=1, source_target_pairs={{0,1},{1,0},{2,3},{3,2},{4,5},{5,4},{6,7},{7,6},{8,9},{9,8},{10,11... | collective-permute-start | bytes 884744 | tf_op jit(solution)/shard_map/ppermute | solution.py:385
  53.5 3.8 %collective-permute-start.6 = (f32[16,3,128]{2,1,0:T(4,128)S(1)}, f32[16,3,128]{2,1,0:T(4,128)S(1)}, u32[]{:S(2)}, u32[]{:S(2)}) collective-permute-start(f32[16,3,128]{2,1,0:T(4,128)S(1)} %get-tuple-element.20), channel_id=1, source_target_pairs={{0,3},{1,2},{2,1},{3,0},{4,7},{5,6},{6,5},{7,4},{8,11},{9,10},{10,... | collective-permute-start | bytes 73736 | tf_op jit(solution)/shard_map/ppermute | solution.py:322
  55.7 2.8 %collective-permute-start.5 = (f32[16,3,128]{2,1,0:T(4,128)S(1)}, f32[16,3,128]{2,1,0:T(4,128)S(1)}, u32[]{:S(2)}, u32[]{:S(2)}) collective-permute-start(f32[16,3,128]{2,1,0:T(4,128)S(1)} %get-tuple-element.20), channel_id=1, source_target_pairs={{0,2},{1,3},{2,0},{3,1},{4,6},{5,7},{6,4},{7,5},{8,10},{9,11},{10,... | collective-permute-start | bytes 73736 | tf_op jit(solution)/shard_map/ppermute | solution.py:322
  55.7 2.8 %collective-permute-start.4 = (f32[16,3,128]{2,1,0:T(4,128)S(1)}, f32[16,3,128]{2,1,0:T(4,128)S(1)}, u32[]{:S(2)}, u32[]{:S(2)}) collective-permute-start(f32[16,3,128]{2,1,0:T(4,128)S(1)} %get-tuple-element.20), channel_id=1, source_target_pairs={{0,1},{1,0},{2,3},{3,2},{4,5},{5,4},{6,7},{7,6},{8,9},{9,8},{10,11... | collective-permute-start | bytes 73736 | tf_op jit(solution)/shard_map/ppermute | solution.py:322
  58.5 3.8 %collective-permute-start.8 = (f32[16,3,128]{2,1,0:T(4,128)S(1)}, f32[16,3,128]{2,1,0:T(4,128)S(1)}, u32[]{:S(2)}, u32[]{:S(2)}) collective-permute-start(f32[16,3,128]{2,1,0:T(4,128)S(1)} %get-tuple-element.28.tan_own), channel_id=1, source_target_pairs={{0,252},{4,0},{8,4},{12,8},{16,12},{20,16},{24,20},{28,24},{32,28}... | collective-permute-start | bytes 73736 | tf_op jit(solution)/shard_map/ppermute | solution.py:410
  60.3 9.1 %collective-permute-start.7 = (f32[16,3,128]{2,1,0:T(4,128)S(1)}, f32[16,3,128]{2,1,0:T(4,128)S(1)}, u32[]{:S(2)}, u32[]{:S(2)}) collective-permute-start(f32[16,3,128]{2,1,0:T(4,128)S(1)} %get-tuple-element.28.tan_own), channel_id=1, source_target_pairs={{0,4},{4,8},{8,12},{12,16},{16,20},{20,24},{24,28},{28,32},{32,36}... | collective-permute-start | bytes 73736 | tf_op jit(solution)/shard_map/ppermute | solution.py:409
  79.2 5.5 %collective-permute-start.11 = (f32[16,3,128]{2,1,0:T(4,128)S(1)}, f32[16,3,128]{2,1,0:T(4,128)S(1)}, u32[]{:S(2)}, u32[]{:S(2)}) collective-permute-start(f32[16,3,128]{2,1,0:T(4,128)S(1)} %variance_gradient.1), channel_id=1, source_target_pairs={{0,3},{1,2},{2,1},{3,0},{4,7},{5,6},{6,5},{7,4},{8,11},{9,10},{10,... | collective-permute-start | bytes 73736 | tf_op jit(solution)/shard_map/ppermute | solution.py:322
  82.7 2.8 %collective-permute-start.10 = (f32[16,3,128]{2,1,0:T(4,128)S(1)}, f32[16,3,128]{2,1,0:T(4,128)S(1)}, u32[]{:S(2)}, u32[]{:S(2)}) collective-permute-start(f32[16,3,128]{2,1,0:T(4,128)S(1)} %variance_gradient.1), channel_id=1, source_target_pairs={{0,2},{1,3},{2,0},{3,1},{4,6},{5,7},{6,4},{7,5},{8,10},{9,11},{10,... | collective-permute-start | bytes 73736 | tf_op jit(solution)/shard_map/ppermute | solution.py:322
  82.9 2.6 %collective-permute-start.9 = (f32[16,3,128]{2,1,0:T(4,128)S(1)}, f32[16,3,128]{2,1,0:T(4,128)S(1)}, u32[]{:S(2)}, u32[]{:S(2)}) collective-permute-start(f32[16,3,128]{2,1,0:T(4,128)S(1)} %variance_gradient.1), channel_id=1, source_target_pairs={{0,1},{1,0},{2,3},{3,2},{4,5},{5,4},{6,7},{7,6},{8,9},{9,8},{10,11... | collective-permute-start | bytes 73736 | tf_op jit(solution)/shard_map/ppermute | solution.py:322

commit v5 on v4

--- a/solution.py
+++ b/solution.py
@@ -119,7 +119,7 @@
 
 
 def own_kernel(slots, rate_ref, own_ref, pos_ref, embed_ref, wproj_ref,
-               force_ref, first_ref, second_ref, tile_ref, proj_ref):
+               force_ref, first_ref, second_ref, tile_ref, proj_ref, sep_ref):
     rows, channels = own_ref.shape[1:]
     bases = wproj_ref.shape[1] // channels
     escale = 1.0 / math.sqrt(slots * rows)
@@ -134,6 +134,8 @@
         tile_ref[part] = tile.astype(jnp.bfloat16)
         cols = jnp.transpose(tile).astype(jnp.bfloat16)
         separators = [difference_rhs(tile, a, TILE) for a in range(3)]
+        for a in range(3):
+            sep_ref[part, a] = separators[a]
         total = [jnp.zeros((8, rows), jnp.float32) for _ in range(3)]
 
         def store(start, first, second, part=part):
@@ -147,7 +149,7 @@
 
 def pair_kernel(
     nbr_ref, cnt_ref, rate_ref, meta_ref,
-    own_proj, lo_a, lo_b, hi_a, hi_b, embed_ref, wproj_ref, own_tile, part_ref,
+    own_proj, lo_a, lo_b, hi_a, hi_b, embed_ref, wproj_ref, own_tile, part_ref, sep_ref,
     force_ref, first_ref, second_ref, rows_ref,
     proj_ref, col_ref, sem,
 ):
@@ -205,8 +207,7 @@
 
         def run(live):
             left = proj_ref[owned + block]
-            tile = own_tile[block].astype(jnp.float32)
-            separators = [difference_rhs(tile, a, TILE) for a in range(3)]
+            separators = [sep_ref[part, a] for a in range(3)]
             total = [jnp.zeros((8, rows), jnp.float32) for _ in range(3)]
             for slot in range(1, live):
                 source = nbr_ref[block, slot] - offset
@@ -227,9 +228,48 @@
     lax.fori_loop(0, STEP_BLOCKS, one_block, 0)
 
 
+def grad_slot(cols, sides, first_of, second_of, total):
+    rows = cols.shape[0]
+    parts = [jnp.dot(cols, r, preferred_element_type=jnp.float32) for r in sides]
+    for start in range(0, rows, CHUNK):
+        span = slice(start, start + CHUNK)
+        delta = [p[span] for p in parts[:3]]
+        change = [p[span] for p in parts[3:]]
+        first = first_of(span)
+        along = second_of(span) * (delta[0] * change[0] + delta[1] * change[1] + delta[2] * change[2])
+        for a in range(3):
+            term = first * change[a] + along * delta[a]
+            total[a] = total[a] + jnp.sum(term.reshape(CHUNK // 8, 8, rows), axis=0)
+
+
+def tangent_columns(tile, pieces):
+    filler = jnp.zeros((TILE - 3 * PIECES, tile.shape[1]), jnp.float32)
+    return jnp.transpose(jnp.concatenate([tile] + pieces + [filler], axis=0)).astype(jnp.bfloat16)
+
+
+def own_grad_kernel(slots, tile_ref, tan_ref, first_ref, second_ref, grad_ref, side_ref):
+    rows = first_ref.shape[1]
+    escale = 1.0 / math.sqrt(slots * rows)
+    for part in range(STEP_BLOCKS):
+        tile = tile_ref[part].astype(jnp.float32)
+        pieces = split(tan_ref[part])
+        sides = [difference_rhs(tile, a, 2 * TILE) for a in range(3)]
+        sides += [change_rhs(pieces, a, 2 * TILE) for a in range(3)]
+        for n in range(6):
+            side_ref[part, n] = sides[n]
+        total = [jnp.zeros((8, rows), jnp.float32) for _ in range(3)]
+        grad_slot(
+            tangent_columns(tile, pieces), sides,
+            lambda span, part=part: first_ref[part, span, :],
+            lambda span, part=part: second_ref[part, span, :],
+            total,
+        )
+        grad_ref[part] = gather_rows(total, 0.5 * escale)
+
+
 def grad_kernel(
     nbr_ref, cnt_ref, meta_ref, pos_ref, tan_own, tan_lo, tan_hi,
-    own_first, own_second, first_ref, second_ref,
+    part_ref, side_ref, first_ref, second_ref,
     grad_ref, col_ref,
 ):
     owned = tan_own.shape[0]
@@ -242,11 +282,7 @@
     def _():
         def spread(tan, base):
             def one(i, carry):
-                filler = jnp.zeros((TILE - 3 * PIECES, rows), jnp.float32)
-                tile = jnp.concatenate(
-                    [pos_ref[base + i].astype(jnp.float32)] + split(tan[i]) + [filler], axis=0
-                )
-                col_ref[base + i] = jnp.transpose(tile).astype(jnp.bfloat16)
+                col_ref[base + i] = tangent_columns(pos_ref[base + i].astype(jnp.float32), split(tan[i]))
                 return carry
 
             lax.fori_loop(0, owned, one, 0, unroll=4)
@@ -263,30 +299,19 @@
         count = cnt_ref[block]
 
         def run(live):
-            tile = pos_ref[owned + block].astype(jnp.float32)
-            pieces = split(tan_own[block])
-            sides = [difference_rhs(tile, a, 2 * TILE) for a in range(3)]
-            sides += [change_rhs(pieces, a, 2 * TILE) for a in range(3)]
+            sides = [side_ref[part, n] for n in range(6)]
             total = [jnp.zeros((8, rows), jnp.float32) for _ in range(3)]
-            for slot in range(live):
-                source = owned + block
-                if slot:
-                    source = nbr_ref[block, slot] - offset
-                    source = jnp.where(source < 0, source + total_blocks, source)
-                    source = jnp.where(source >= total_blocks, source - total_blocks, source)
-                cols = col_ref[source]
-                parts = [jnp.dot(cols, r, preferred_element_type=jnp.float32) for r in sides]
-                for start in range(0, rows, CHUNK):
-                    delta = [p[start:start + CHUNK] for p in parts[:3]]
-                    change = [p[start:start + CHUNK] for p in parts[3:]]
-                    span = slice(start, start + CHUNK)
-                    first = first_ref[part, slot - 1, span, :] if slot else own_first[part, span, :]
-                    second = second_ref[part, slot - 1, span, :] if slot else own_second[part, span, :]
-                    along = second * (delta[0] * change[0] + delta[1] * change[1] + delta[2] * change[2])
-                    for a in range(3):
-                        term = first * change[a] + along * delta[a]
-                        total[a] = total[a] + jnp.sum(term.reshape(CHUNK // 8, 8, rows), axis=0)
-            grad_ref[part] = gather_rows(total, 0.5 * escale)
+            for slot in range(1, live):
+                source = nbr_ref[block, slot] - offset
+                source = jnp.where(source < 0, source + total_blocks, source)
+                source = jnp.where(source >= total_blocks, source - total_blocks, source)
+                grad_slot(
+                    col_ref[source], sides,
+                    lambda span, slot=slot: first_ref[part, slot - 1, span, :],
+                    lambda span, slot=slot: second_ref[part, slot - 1, span, :],
+                    total,
+                )
+            grad_ref[part] = part_ref[part] + gather_rows(total, 0.5 * escale)
 
         for live in range(3, slots + 1):
             pl.when(count == live)(lambda live=live: run(live))
@@ -363,8 +388,10 @@
     tiles = jax.ShapeDtypeStruct((owned, TILE, rows), jnp.bfloat16)
     window = jax.ShapeDtypeStruct((3 * owned, TILE, rows), jnp.bfloat16)
     table = jax.ShapeDtypeStruct((owned, rows, width), jnp.bfloat16)
+    separate = jax.ShapeDtypeStruct((owned, dims, TILE, rows), jnp.bfloat16)
+    sides = jax.ShapeDtypeStruct((owned, 2 * dims, 2 * TILE, rows), jnp.bfloat16)
     steps = (owned // STEP_BLOCKS,)
-    part_force, own_first, own_second, own_tile, own_proj = pl.pallas_call(
+    part_force, own_first, own_second, own_tile, own_proj, separators = pl.pallas_call(
         functools.partial(own_kernel, slots),
         grid_spec=pltpu.PrefetchScalarGridSpec(
             num_scalar_prefetch=1,
@@ -372,10 +399,10 @@
             in_specs=[stepped((rows, channels)), stepped((dims, rows)), whole(w_embed[0]), whole(w_proj[0])],
             out_specs=[
                 stepped((dims, rows)), stepped(pair), stepped(pair),
-                stepped((TILE, rows)), stepped((rows, width)),
+                stepped((TILE, rows)), stepped((rows, width)), stepped((dims, TILE, rows)),
             ],
         ),
-        out_shape=[small, selfs, selfs, tiles, table],
+        out_shape=[small, selfs, selfs, tiles, table, separate],
         compiler_params=pltpu.CompilerParams(vmem_limit_bytes=8 << 20),
         name="own_pairs",
     )(rate, in_hbm(features), positions, embed, proj)
@@ -389,7 +416,7 @@
         grid_spec=pltpu.PrefetchScalarGridSpec(
             num_scalar_prefetch=4,
             grid=steps,
-            in_specs=[pl.BlockSpec(memory_space=pl.ANY)] + [whole(t) for t in halo] + [stepped((dims, rows))],
+            in_specs=[pl.BlockSpec(memory_space=pl.ANY)] + [whole(t) for t in halo] + [stepped((dims, rows)), stepped((dims, TILE, rows))],
             out_specs=[
                 stepped((dims, rows)), stepped((slots - 1,) + pair), stepped((slots - 1,) + pair), whole(window),
             ],
@@ -402,26 +429,35 @@
         out_shape=[small, pairs, pairs, window],
         compiler_params=pltpu.CompilerParams(vmem_limit_bytes=18 << 20),
         name="halo_pairs",
-    )(nbr_list, counts, rate, meta, own_proj, *halo, in_hbm(part_force))
+    )(nbr_list, counts, rate, meta, own_proj, *halo, in_hbm(part_force), separators)
 
     mean_force = member_sum(force) / members
     tangent = (2.0 / members) * (force - mean_force)
     tan_lo = lax.ppermute(tangent, "space", up)
     tan_hi = lax.ppermute(tangent, "space", down)
+    part_grad, side_table = pl.pallas_call(
+        functools.partial(own_grad_kernel, slots),
+        grid=steps,
+        in_specs=[stepped((TILE, rows)), stepped((dims, rows)), stepped(pair), stepped(pair)],
+        out_specs=[stepped((dims, rows)), stepped((2 * dims, 2 * TILE, rows))],
+        out_shape=[small, sides],
+        compiler_params=pltpu.CompilerParams(vmem_limit_bytes=8 << 20),
+        name="own_gradient",
+    )(own_tile, tangent, in_hbm(own_first), in_hbm(own_second))
     tensors = (pos_rows, tangent, tan_lo, tan_hi)
     grad = pl.pallas_call(
         grad_kernel,
         grid_spec=pltpu.PrefetchScalarGridSpec(
             num_scalar_prefetch=3,
             grid=steps,
-            in_specs=[whole(t) for t in tensors] + [stepped(pair)] * 2 + [stepped((slots - 1,) + pair)] * 2,
+            in_specs=[whole(t) for t in tensors] + [stepped((dims, rows)), stepped((2 * dims, 2 * TILE, rows))] + [stepped((slots - 1,) + pair)] * 2,
             out_specs=stepped((dims, rows)),
             scratch_shapes=[pltpu.VMEM((3 * owned, rows, 2 * TILE), jnp.bfloat16)],
         ),
         out_shape=small,
         compiler_params=pltpu.CompilerParams(vmem_limit_bytes=10 << 20),
         name="variance_gradient",
-    )(nbr_list, counts, meta, *tensors, in_hbm(own_first), in_hbm(own_second), first, second)
+    )(nbr_list, counts, meta, *tensors, part_grad, side_table, first, second)
     return (mean_force, member_sum(grad))
 
 

time: 85.7 us -> 84.7 us (0.988)
  waiting for transfers between devices: 23.7 us -> 18.9 us
  Pallas kernels: 33.7 us -> 36.9 us
    ppermute x1, waiting for transfers between devices: 7.02 us -> 3.47 us  [body(): tan_lo = lax.ppermute(tangent, 'space', up)]
    pallas_call x0 -> x1, Pallas kernels: none -> 3.52 us  [body(): pl.pallas_call(functools.partial(own_grad_kernel, slots), grid=steps, in_...]
    ppermute x1, starting transfers between devices: 1.77 us -> 0.08 us  [body(): tan_hi = lax.ppermute(tangent, 'space', down)]
    ppermute x1, starting transfers between devices: 0.67 us -> 2.35 us  [body(): tan_lo = lax.ppermute(tangent, 'space', up)]
    pallas_call x1, Pallas kernels: 9.82 us -> 8.25 us  [body(): pl.pallas_call(grad_kernel, grid_spec=pltpu.PrefetchScalarGridSpec(num_sc...]
    ppermute x1, waiting for transfers between devices: 1.4 us -> 0.01 us  [body(): tan_hi = lax.ppermute(tangent, 'space', down)]
    pallas_call x1, Pallas kernels: 16.4 us -> 17.5 us  [body(): pl.pallas_call(pair_kernel, grid_spec=pltpu.PrefetchScalarGridSpec(num_sc...]
  transfers between devices with their start and end apart: 12 -> 12, of which waited for: 10 -> 9; matrix products, arithmetic and copies ran while one was open for 2% -> 2% of each run, Pallas kernels for 7% -> 11%
where the time goes in v5:
time: 84.7 us; the launch traced here: 84.5 us
  Pallas kernels  36.9 us (44%)
  starting transfers between devices  22.5 us (27%)
  waiting for transfers between devices  18.9 us (22%)
  local copies, waits for them, and re-layouts  5.31 us (6%)
    pallas_call x1, Pallas kernels, body(): pl.pallas_call(pair_kernel, grid_spec=pltpu.PrefetchScalarGridSpec(num_sc...  17.5 us
    ppermute x1, starting transfers between devices, body(): hi_a = lax.ppermute(mine, 'space', down)  11.6 us
    pallas_call x1, Pallas kernels, body(): pl.pallas_call(grad_kernel, grid_spec=pltpu.PrefetchScalarGridSpec(num_sc...  8.25 us
    ppermute x6, starting transfers between devices, member_sum(): lax.ppermute(array, 'member', flip('member', bit))  6.57 us
    ppermute x1, waiting for transfers between devices, body(): lo_a = lax.ppermute(mine, 'space', up)  6.5 us
    pallas_call x1, Pallas kernels, body(): pl.pallas_call(functools.partial(own_kernel, slots), grid_spec=pltpu.Pref...  6.05 us
    unnamed x10, local copies, waits for them, and re-layouts  5.31 us
    ppermute x6, waiting for transfers between devices, member_sum(): lax.ppermute(array, 'member', flip('member', bit))  4.16 us
  transfers between devices with their start and end apart: 12, of which 9 were waited for; matrix products, arithmetic and copies ran while one was open for 2% of the time, Pallas kernels for 11%

profile of v5, /device:TPU:1, one launch (start us, length us, event | category | flops | bytes accessed | tf_op | source)
XLA Modules:
  0.0 84.5 jit_solution(12064665759547446019)
XLA Ops:
  0.6 0.8 copy.9.pos_ref
  1.4 0.1 pad_add_fusion.meta_ref
  1.5 1.5 %pack_halo.1 = bf16[8,144,128]{2,1,0:T(8,128)(2,1)S(1)} custom-call(s32[3]{0:T(128)S(1)} %pad_add_fusion.meta_ref, bf16[16,128,128]{2,1,0:T(8,128)(2,1)} %feat_ref.1, f32[16,3,128]{2,1,0:T(4,128)S(1)} %copy.9.pos_ref), custom_call_target="tpu_custom_call" | custom-call | tf_op jit(solution)/shard_map/pack_halo/pallas_call | solution.py:367
  3.0 11.6 %collective-permute-start.1 = (bf16[8,144,128]{2,1,0:T(8,128)(2,1)S(1)}, bf16[8,144,128]{2,1,0:T(8,128)(2,1)S(1)}, u32[]{:S(2)}, u32[]{:S(2)}) collective-permute-start(bf16[8,144,128]{2,1,0:T(8,128)(2,1)S(1)} %pack_halo.1), channel_id=1, source_target_pairs={{0,252},{4,0},{8,4},{12,8},{16,12},{20,16},{24,20},{28,24},{32,28}... | collective-permute-start | bytes 884744 | tf_op jit(solution)/shard_map/ppermute | solution.py:383
  14.6 0.0 collective-permute-start
  14.6 6.0 %own_pairs.1 = (f32[16,3,128]{2,1,0:T(4,128)S(1)}, f32[16,128,128]{2,1,0:T(8,128)S(1)}, f32[16,128,128]{2,1,0:T(8,128)S(1)}, bf16[16,16,128]{2,1,0:T(8,128)(2,1)...) custom-call(f32[4]{0:T(128)} %bitcast.9, bf16[16,128,128]{2,1,0:T(8,128)(2,1)} %feat_ref.1, ...), custom_call_target="tpu_custom_call" | custom-call | tf_op jit(solution)/shard_map/own_pairs/pallas_call | solution.py:394
  20.6 0.0 copy-start
  20.7 1.0 %copy-done = f32[16,128,128]{2,1,0:T(8,128)} copy-done((f32[16,128,128]{2,1,0:T(8,128)}, f32[16,128,128]{2,1,0:T(8,128)S(1)}, u32[]{:S(2)}) %copy-start) | copy-done | bytes 1048600
  21.6 0.0 copy-start.1
  21.6 1.0 %copy-done.1 = f32[16,128,128]{2,1,0:T(8,128)} copy-done((f32[16,128,128]{2,1,0:T(8,128)}, f32[16,128,128]{2,1,0:T(8,128)S(1)}, u32[]{:S(2)}) %copy-start.1) | copy-done | bytes 1048600
  22.6 0.0 copy-start.2
  22.6 0.6 copy-done.2
  23.2 3.9 %collective-permute-done.1.hi_a = bf16[8,144,128]{2,1,0:T(8,128)(2,1)S(1)} collective-permute-done((bf16[8,144,128]{2,1,0:T(8,128)(2,1)S(1)}, bf16[8,144,128]{2,1,0:T(8,128)(2,1)S(1)}, u32[]{:S(2)}, u32[]{:S(2)}) %collective-permute-start.1) | collective-permute-done | bytes 294944 | tf_op jit(solution)/shard_map/ppermute | solution.py:383
  27.2 6.5 %collective-permute-done.lo_a = bf16[8,144,128]{2,1,0:T(8,128)(2,1)S(1)} collective-permute-done((bf16[8,144,128]{2,1,0:T(8,128)(2,1)S(1)}, bf16[8,144,128]{2,1,0:T(8,128)(2,1)S(1)}, u32[]{:S(2)}, u32[]{:S(2)}) %collective-permute-start) | collective-permute-done | bytes 294944 | tf_op jit(solution)/shard_map/ppermute | solution.py:382
  33.7 1.9 %collective-permute-start.2 = (bf16[8,144,128]{2,1,0:T(8,128)(2,1)S(1)}, bf16[8,144,128]{2,1,0:T(8,128)(2,1)S(1)}, u32[]{:S(2)}, u32[]{:S(2)}) collective-permute-start(bf16[8,144,128]{2,1,0:T(8,128)(2,1)S(1)} %collective-permute-done.lo_a), channel_id=1, source_target_pairs={{0,1},{1,0},{2,3},{3,2},{4,5},{5,4},{6,7},{7,6},{8,9},{9,8},{10,11... | collective-permute-start | bytes 884744 | tf_op jit(solution)/shard_map/ppermute | solution.py:411
  35.5 0.0 collective-permute-start.3
  35.5 0.8 copy.11.nbr_ref
  36.3 0.4 collective-permute-done.2.lo_b
  36.8 0.4 collective-permute-done.3.hi_b
  37.2 17.5 %halo_pairs.1 = (f32[16,3,128]{2,1,0:T(4,128)S(1)}, f32[16,5,128,128]{3,2,1,0:T(8,128)S(1)}, f32[16,5,128,128]{3,2,1,0:T(8,128)S(1)}, bf16[48,16,128]{2,1,0:T(8,128)(2,1)S(1)}) custom-call(s32[16,6]{1,0:T(8,128)S(1)} %copy.11.nbr_ref, s32[16]{0:T(128)} %cnt_ref.3, f32[4]{0:T(128)} %bitcast.10, s32[3]{0:T(128)S(1)} %pad_add_fusion.meta_ref, ...), custom_call_target="tpu_custom_call" | custom-call | tf_op jit(solution)/shard_map/halo_pairs/pallas_call | solution.py:414
  54.7 2.2 %collective-permute-start.6 = (f32[16,3,128]{2,1,0:T(4,128)S(1)}, f32[16,3,128]{2,1,0:T(4,128)S(1)}, u32[]{:S(2)}, u32[]{:S(2)}) collective-permute-start(f32[16,3,128]{2,1,0:T(4,128)S(1)} %get-tuple-element.24), channel_id=1, source_target_pairs={{0,3},{1,2},{2,1},{3,0},{4,7},{5,6},{6,5},{7,4},{8,11},{9,10},{10,... | collective-permute-start | bytes 73736 | tf_op jit(solution)/shard_map/ppermute | solution.py:347
  56.9 0.0 collective-permute-start.5
  56.9 0.5 collective-permute-start.4
  57.4 1.1 %collective-permute-done.6 = f32[16,3,128]{2,1,0:T(4,128)S(1)} collective-permute-done((f32[16,3,128]{2,1,0:T(4,128)S(1)}, f32[16,3,128]{2,1,0:T(4,128)S(1)}, u32[]{:S(2)}, u32[]{:S(2)}) %collective-permute-start.6) | collective-permute-done | bytes 24608 | tf_op jit(solution)/shard_map/ppermute | solution.py:347
  58.5 1.2 %collective-permute-done.5 = f32[16,3,128]{2,1,0:T(4,128)S(1)} collective-permute-done((f32[16,3,128]{2,1,0:T(4,128)S(1)}, f32[16,3,128]{2,1,0:T(4,128)S(1)}, u32[]{:S(2)}, u32[]{:S(2)}) %collective-permute-start.5) | collective-permute-done | bytes 24608 | tf_op jit(solution)/shard_map/ppermute | solution.py:347
  59.7 0.0 collective-permute-done.4
  59.7 0.1 collective-permute-start.8
  59.8 2.4 %collective-permute-start.7 = (f32[16,3,128]{2,1,0:T(4,128)S(1)}, f32[16,3,128]{2,1,0:T(4,128)S(1)}, u32[]{:S(2)}, u32[]{:S(2)}) collective-permute-start(f32[16,3,128]{2,1,0:T(4,128)S(1)} %get-tuple-element.34.tan_ref.tan_own), channel_id=1, source_target_pairs={{0,4},{4,8},{8,12},{12,16},{16,20},{20,24},{24,28},{28,32},{32,36}... | collective-permute-start | bytes 73736 | tf_op jit(solution)/shard_map/ppermute | solution.py:436
  62.2 3.5 %own_gradient.1 = (f32[16,3,128]{2,1,0:T(4,128)S(1)}, bf16[16,6,32,128]{3,2,1,0:T(8,128)(2,1)S(1)}) custom-call(bf16[16,16,128]{2,1,0:T(8,128)(2,1)S(1)} %get-tuple-element.21.own_tile.tile_ref, f32[16,3,128]{2,1,0:T(4,128)S(1)} %get-tuple-element.34.tan_ref.tan_own, f32[16,128,128]{2,1,0:T(8,128)} %copy-done, f32[16,128,128]{2,1,0:T(8,128)} %copy-done.1), custom_call_target="tpu_custom_call" | custom-call | tf_op jit(solution)/shard_map/own_gradient/pallas_call | solution.py:438
  65.7 0.0 collective-permute-done.8.tan_hi
  65.7 3.5 %collective-permute-done.7.tan_lo = f32[16,3,128]{2,1,0:T(4,128)S(1)} collective-permute-done((f32[16,3,128]{2,1,0:T(4,128)S(1)}, f32[16,3,128]{2,1,0:T(4,128)S(1)}, u32[]{:S(2)}, u32[]{:S(2)}) %collective-permute-start.7) | collective-permute-done | bytes 24608 | tf_op jit(solution)/shard_map/ppermute | solution.py:436
  69.2 8.3 %variance_gradient.1 = f32[16,3,128]{2,1,0:T(4,128)S(1)} custom-call(s32[16,6]{1,0:T(8,128)S(1)} %copy.11.nbr_ref, s32[16]{0:T(128)} %cnt_ref.3, s32[3]{0:T(128)S(1)} %pad_add_fusion.meta_ref, bf16[48,16,128]{2,1,0:T(8,128)(2,1)S(1)} %get-tuple-element.25.pos_ref, f32[16,3,128]{2,1,0:T(4,128)S(1)} %get-tuple-element.34.tan_ref.tan_own, ...), custom_call_target="tpu_custom_call" | custom-call | tf_op jit(solution)/shard_map/variance_gradient/pallas_call | solution.py:448
  77.4 3.2 %collective-permute-start.11 = (f32[16,3,128]{2,1,0:T(4,128)S(1)}, f32[16,3,128]{2,1,0:T(4,128)S(1)}, u32[]{:S(2)}, u32[]{:S(2)}) collective-permute-start(f32[16,3,128]{2,1,0:T(4,128)S(1)} %variance_gradient.1), channel_id=1, source_target_pairs={{0,3},{1,2},{2,1},{3,0},{4,7},{5,6},{6,5},{7,4},{8,11},{9,10},{10,... | collective-permute-start | bytes 73736 | tf_op jit(solution)/shard_map/ppermute | solution.py:347
  80.6 0.7 collective-permute-start.10
  81.3 0.0 collective-permute-start.9
  81.3 0.6 copy.13
  81.9 0.3 collective-permute-done.11
  82.2 1.6 %collective-permute-done.10 = f32[16,3,128]{2,1,0:T(4,128)S(1)} collective-permute-done((f32[16,3,128]{2,1,0:T(4,128)S(1)}, f32[16,3,128]{2,1,0:T(4,128)S(1)}, u32[]{:S(2)}, u32[]{:S(2)}) %collective-permute-start.10) | collective-permute-done | bytes 24608 | tf_op jit(solution)/shard_map/ppermute | solution.py:347
  83.8 0.0 collective-permute-done.9
  83.8 0.6 copy.14
  (2 shorter events, 0.0 us)
Async XLA Ops:
  3.0 24.1 %collective-permute-start.1 = (bf16[8,144,128]{2,1,0:T(8,128)(2,1)S(1)}, bf16[8,144,128]{2,1,0:T(8,128)(2,1)S(1)}, u32[]{:S(2)}, u32[]{:S(2)}) collective-permute-start(bf16[8,144,128]{2,1,0:T(8,128)(2,1)S(1)} %pack_halo.1), channel_id=1, source_target_pairs={{0,252},{4,0},{8,4},{12,8},{16,12},{20,16},{24,20},{28,24},{32,28}... | collective-permute-start | bytes 884744 | tf_op jit(solution)/shard_map/ppermute | solution.py:383
  14.6 19.1 %collective-permute-start = (bf16[8,144,128]{2,1,0:T(8,128)(2,1)S(1)}, bf16[8,144,128]{2,1,0:T(8,128)(2,1)S(1)}, u32[]{:S(2)}, u32[]{:S(2)}) collective-permute-start(bf16[8,144,128]{2,1,0:T(8,128)(2,1)S(1)} %pack_halo.1), channel_id=1, source_target_pairs={{0,4},{4,8},{8,12},{12,16},{16,20},{20,24},{24,28},{28,32},{32,36}... | collective-permute-start | bytes 884744 | tf_op jit(solution)/shard_map/ppermute | solution.py:382
  20.6 1.0 %copy-start = (f32[16,128,128]{2,1,0:T(8,128)}, f32[16,128,128]{2,1,0:T(8,128)S(1)}, u32[]{:S(2)}) copy-start(f32[16,128,128]{2,1,0:T(8,128)S(1)} %get-tuple-element.26.first_ref) | copy-start | bytes 3145732
  21.6 1.0 %copy-start.1 = (f32[16,128,128]{2,1,0:T(8,128)}, f32[16,128,128]{2,1,0:T(8,128)S(1)}, u32[]{:S(2)}) copy-start(f32[16,128,128]{2,1,0:T(8,128)S(1)} %get-tuple-element.27.second_ref) | copy-start | bytes 3145732
  22.6 0.6 copy-start.2
  33.7 3.1 %collective-permute-start.2 = (bf16[8,144,128]{2,1,0:T(8,128)(2,1)S(1)}, bf16[8,144,128]{2,1,0:T(8,128)(2,1)S(1)}, u32[]{:S(2)}, u32[]{:S(2)}) collective-permute-start(bf16[8,144,128]{2,1,0:T(8,128)(2,1)S(1)} %collective-permute-done.lo_a), channel_id=1, source_target_pairs={{0,1},{1,0},{2,3},{3,2},{4,5},{5,4},{6,7},{7,6},{8,9},{9,8},{10,11... | collective-permute-start | bytes 884744 | tf_op jit(solution)/shard_map/ppermute | solution.py:411
  35.5 1.6 %collective-permute-start.3 = (bf16[8,144,128]{2,1,0:T(8,128)(2,1)S(1)}, bf16[8,144,128]{2,1,0:T(8,128)(2,1)S(1)}, u32[]{:S(2)}, u32[]{:S(2)}) collective-permute-start(bf16[8,144,128]{2,1,0:T(8,128)(2,1)S(1)} %collective-permute-done.1.hi_a), channel_id=1, source_target_pairs={{0,1},{1,0},{2,3},{3,2},{4,5},{5,4},{6,7},{7,6},{8,9},{9,8},{10,11... | collective-permute-start | bytes 884744 | tf_op jit(solution)/shard_map/ppermute | solution.py:412
  54.7 3.8 %collective-permute-start.6 = (f32[16,3,128]{2,1,0:T(4,128)S(1)}, f32[16,3,128]{2,1,0:T(4,128)S(1)}, u32[]{:S(2)}, u32[]{:S(2)}) collective-permute-start(f32[16,3,128]{2,1,0:T(4,128)S(1)} %get-tuple-element.24), channel_id=1, source_target_pairs={{0,3},{1,2},{2,1},{3,0},{4,7},{5,6},{6,5},{7,4},{8,11},{9,10},{10,... | collective-permute-start | bytes 73736 | tf_op jit(solution)/shard_map/ppermute | solution.py:347
  56.9 2.8 %collective-permute-start.5 = (f32[16,3,128]{2,1,0:T(4,128)S(1)}, f32[16,3,128]{2,1,0:T(4,128)S(1)}, u32[]{:S(2)}, u32[]{:S(2)}) collective-permute-start(f32[16,3,128]{2,1,0:T(4,128)S(1)} %get-tuple-element.24), channel_id=1, source_target_pairs={{0,2},{1,3},{2,0},{3,1},{4,6},{5,7},{6,4},{7,5},{8,10},{9,11},{10,... | collective-permute-start | bytes 73736 | tf_op jit(solution)/shard_map/ppermute | solution.py:347
  56.9 2.8 %collective-permute-start.4 = (f32[16,3,128]{2,1,0:T(4,128)S(1)}, f32[16,3,128]{2,1,0:T(4,128)S(1)}, u32[]{:S(2)}, u32[]{:S(2)}) collective-permute-start(f32[16,3,128]{2,1,0:T(4,128)S(1)} %get-tuple-element.24), channel_id=1, source_target_pairs={{0,1},{1,0},{2,3},{3,2},{4,5},{5,4},{6,7},{7,6},{8,9},{9,8},{10,11... | collective-permute-start | bytes 73736 | tf_op jit(solution)/shard_map/ppermute | solution.py:347
  59.7 6.0 %collective-permute-start.8 = (f32[16,3,128]{2,1,0:T(4,128)S(1)}, f32[16,3,128]{2,1,0:T(4,128)S(1)}, u32[]{:S(2)}, u32[]{:S(2)}) collective-permute-start(f32[16,3,128]{2,1,0:T(4,128)S(1)} %get-tuple-element.34.tan_ref.tan_own), channel_id=1, source_target_pairs={{0,252},{4,0},{8,4},{12,8},{16,12},{20,16},{24,20},{28,24},{32,28}... | collective-permute-start | bytes 73736 | tf_op jit(solution)/shard_map/ppermute | solution.py:437
  59.8 9.4 %collective-permute-start.7 = (f32[16,3,128]{2,1,0:T(4,128)S(1)}, f32[16,3,128]{2,1,0:T(4,128)S(1)}, u32[]{:S(2)}, u32[]{:S(2)}) collective-permute-start(f32[16,3,128]{2,1,0:T(4,128)S(1)} %get-tuple-element.34.tan_ref.tan_own), channel_id=1, source_target_pairs={{0,4},{4,8},{8,12},{12,16},{16,20},{20,24},{24,28},{28,32},{32,36}... | collective-permute-start | bytes 73736 | tf_op jit(solution)/shard_map/ppermute | solution.py:436
  77.4 4.8 %collective-permute-start.11 = (f32[16,3,128]{2,1,0:T(4,128)S(1)}, f32[16,3,128]{2,1,0:T(4,128)S(1)}, u32[]{:S(2)}, u32[]{:S(2)}) collective-permute-start(f32[16,3,128]{2,1,0:T(4,128)S(1)} %variance_gradient.1), channel_id=1, source_target_pairs={{0,3},{1,2},{2,1},{3,0},{4,7},{5,6},{6,5},{7,4},{8,11},{9,10},{10,... | collective-permute-start | bytes 73736 | tf_op jit(solution)/shard_map/ppermute | solution.py:347
  80.6 3.2 %collective-permute-start.10 = (f32[16,3,128]{2,1,0:T(4,128)S(1)}, f32[16,3,128]{2,1,0:T(4,128)S(1)}, u32[]{:S(2)}, u32[]{:S(2)}) collective-permute-start(f32[16,3,128]{2,1,0:T(4,128)S(1)} %variance_gradient.1), channel_id=1, source_target_pairs={{0,2},{1,3},{2,0},{3,1},{4,6},{5,7},{6,4},{7,5},{8,10},{9,11},{10,... | collective-permute-start | bytes 73736 | tf_op jit(solution)/shard_map/ppermute | solution.py:347
  81.3 2.5 %collective-permute-start.9 = (f32[16,3,128]{2,1,0:T(4,128)S(1)}, f32[16,3,128]{2,1,0:T(4,128)S(1)}, u32[]{:S(2)}, u32[]{:S(2)}) collective-permute-start(f32[16,3,128]{2,1,0:T(4,128)S(1)} %variance_gradient.1), channel_id=1, source_target_pairs={{0,1},{1,0},{2,3},{3,2},{4,5},{5,4},{6,7},{7,6},{8,9},{9,8},{10,11... | collective-permute-start | bytes 73736 | tf_op jit(solution)/shard_map/ppermute | solution.py:347

commit v6 on v5

--- a/solution.py
+++ b/solution.py
@@ -9,6 +9,7 @@
 from jax.sharding import PartitionSpec as P
 
 STEP_BLOCKS = 4
+PAIR_BLOCKS = 2
 CHUNK = 32
 PIECES = 3
 TILE = 16
@@ -202,7 +203,7 @@
     total_blocks = meta_ref[2]
 
     def one_block(part, carry):
-        block = step * STEP_BLOCKS + part
+        block = step * PAIR_BLOCKS + part
         count = cnt_ref[block]
 
         def run(live):
@@ -225,7 +226,7 @@
             pl.when(count == live)(lambda live=live: run(live))
         return carry
 
-    lax.fori_loop(0, STEP_BLOCKS, one_block, 0)
+    lax.fori_loop(0, PAIR_BLOCKS, one_block, 0)
 
 
 def grad_slot(cols, sides, first_of, second_of, total):
@@ -295,7 +296,7 @@
     total_blocks = meta_ref[2]
 
     def one_block(part, carry):
-        block = step * STEP_BLOCKS + part
+        block = step * PAIR_BLOCKS + part
         count = cnt_ref[block]
 
         def run(live):
@@ -317,7 +318,7 @@
             pl.when(count == live)(lambda live=live: run(live))
         return carry
 
-    lax.fori_loop(0, STEP_BLOCKS, one_block, 0)
+    lax.fori_loop(0, PAIR_BLOCKS, one_block, 0)
 
 
 def pack_kernel(meta_ref, feat_ref, pos_ref, out_ref):
@@ -338,8 +339,8 @@
     return pl.BlockSpec(array.shape, lambda *_: (0,) * len(array.shape), pipeline_mode=pl.Buffered(1))
 
 
-def stepped(shape):
-    return pl.BlockSpec((STEP_BLOCKS,) + shape, lambda i, *_: (i,) + (0,) * len(shape))
+def stepped(shape, blocks=STEP_BLOCKS):
+    return pl.BlockSpec((blocks,) + shape, lambda i, *_: (i,) + (0,) * len(shape))
 
 
 def member_sum(array):
@@ -415,10 +416,10 @@
         pair_kernel,
         grid_spec=pltpu.PrefetchScalarGridSpec(
             num_scalar_prefetch=4,
-            grid=steps,
-            in_specs=[pl.BlockSpec(memory_space=pl.ANY)] + [whole(t) for t in halo] + [stepped((dims, rows)), stepped((dims, TILE, rows))],
+            grid=(owned // PAIR_BLOCKS,),
+            in_specs=[pl.BlockSpec(memory_space=pl.ANY)] + [whole(t) for t in halo] + [stepped((dims, rows), PAIR_BLOCKS), stepped((dims, TILE, rows), PAIR_BLOCKS)],
             out_specs=[
-                stepped((dims, rows)), stepped((slots - 1,) + pair), stepped((slots - 1,) + pair), whole(window),
+                stepped((dims, rows), PAIR_BLOCKS), stepped((slots - 1,) + pair, PAIR_BLOCKS), stepped((slots - 1,) + pair, PAIR_BLOCKS), whole(window),
             ],
             scratch_shapes=[
                 pltpu.VMEM((3 * owned, rows, width), jnp.bfloat16),
@@ -449,9 +450,9 @@
         grad_kernel,
         grid_spec=pltpu.PrefetchScalarGridSpec(
             num_scalar_prefetch=3,
-            grid=steps,
-            in_specs=[whole(t) for t in tensors] + [stepped((dims, rows)), stepped((2 * dims, 2 * TILE, rows))] + [stepped((slots - 1,) + pair)] * 2,
-            out_specs=stepped((dims, rows)),
+            grid=(owned // PAIR_BLOCKS,),
+            in_specs=[whole(t) for t in tensors] + [stepped((dims, rows), PAIR_BLOCKS), stepped((2 * dims, 2 * TILE, rows), PAIR_BLOCKS)] + [stepped((slots - 1,) + pair, PAIR_BLOCKS)] * 2,
+            out_specs=stepped((dims, rows), PAIR_BLOCKS),
             scratch_shapes=[pltpu.VMEM((3 * owned, rows, 2 * TILE), jnp.bfloat16)],
         ),
         out_shape=small,

time: 84.7 us -> 85.4 us (level)
  no operation moved by 1% of the time
where the time goes in v6:
time: 85.4 us; the launch traced here: 85.1 us
  Pallas kernels  37.5 us (44%)
  starting transfers between devices  22.5 us (26%)
  waiting for transfers between devices  19 us (22%)
  local copies, waits for them, and re-layouts  5.31 us (6%)
    pallas_call x1, Pallas kernels, body(): pl.pallas_call(pair_kernel, grid_spec=pltpu.PrefetchScalarGridSpec(num_sc...  17.9 us
    ppermute x1, starting transfers between devices, body(): hi_a = lax.ppermute(mine, 'space', down)  11.6 us
    pallas_call x1, Pallas kernels, body(): pl.pallas_call(grad_kernel, grid_spec=pltpu.PrefetchScalarGridSpec(num_sc...  8.45 us
    ppermute x6, starting transfers between devices, member_sum(): lax.ppermute(array, 'member', flip('member', bit))  6.58 us
    ppermute x1, waiting for transfers between devices, body(): lo_a = lax.ppermute(mine, 'space', up)  6.5 us
    pallas_call x1, Pallas kernels, body(): pl.pallas_call(functools.partial(own_kernel, slots), grid_spec=pltpu.Pref...  6.05 us
    unnamed x10, local copies, waits for them, and re-layouts  5.31 us
    ppermute x6, waiting for transfers between devices, member_sum(): lax.ppermute(array, 'member', flip('member', bit))  4.19 us
  transfers between devices with their start and end apart: 12, of which 9 were waited for; matrix products, arithmetic and copies ran while one was open for 2% of the time, Pallas kernels for 11%

profile of v6, /device:TPU:1, one launch (start us, length us, event | category | flops | bytes accessed | tf_op | source)
XLA Modules:
  0.0 85.1 jit_solution(8503423319990793560)
XLA Ops:
  0.6 0.8 copy.9.pos_ref
  1.4 0.1 pad_add_fusion.meta_ref
  1.5 1.5 %pack_halo.1 = bf16[8,144,128]{2,1,0:T(8,128)(2,1)S(1)} custom-call(s32[3]{0:T(128)S(1)} %pad_add_fusion.meta_ref, bf16[16,128,128]{2,1,0:T(8,128)(2,1)} %feat_ref.1, f32[16,3,128]{2,1,0:T(4,128)S(1)} %copy.9.pos_ref), custom_call_target="tpu_custom_call" | custom-call | tf_op jit(solution)/shard_map/pack_halo/pallas_call | solution.py:368
  3.0 11.6 %collective-permute-start.1 = (bf16[8,144,128]{2,1,0:T(8,128)(2,1)S(1)}, bf16[8,144,128]{2,1,0:T(8,128)(2,1)S(1)}, u32[]{:S(2)}, u32[]{:S(2)}) collective-permute-start(bf16[8,144,128]{2,1,0:T(8,128)(2,1)S(1)} %pack_halo.1), channel_id=1, source_target_pairs={{0,252},{4,0},{8,4},{12,8},{16,12},{20,16},{24,20},{28,24},{32,28}... | collective-permute-start | bytes 884744 | tf_op jit(solution)/shard_map/ppermute | solution.py:384
  14.6 0.0 collective-permute-start
  14.6 6.0 %own_pairs.1 = (f32[16,3,128]{2,1,0:T(4,128)S(1)}, f32[16,128,128]{2,1,0:T(8,128)S(1)}, f32[16,128,128]{2,1,0:T(8,128)S(1)}, bf16[16,16,128]{2,1,0:T(8,128)(2,1)...) custom-call(f32[4]{0:T(128)} %bitcast.9, bf16[16,128,128]{2,1,0:T(8,128)(2,1)} %feat_ref.1, ...), custom_call_target="tpu_custom_call" | custom-call | tf_op jit(solution)/shard_map/own_pairs/pallas_call | solution.py:395
  20.6 0.0 copy-start
  20.7 1.0 %copy-done = f32[16,128,128]{2,1,0:T(8,128)} copy-done((f32[16,128,128]{2,1,0:T(8,128)}, f32[16,128,128]{2,1,0:T(8,128)S(1)}, u32[]{:S(2)}) %copy-start) | copy-done | bytes 1048600
  21.6 0.0 copy-start.1
  21.6 1.0 %copy-done.1 = f32[16,128,128]{2,1,0:T(8,128)} copy-done((f32[16,128,128]{2,1,0:T(8,128)}, f32[16,128,128]{2,1,0:T(8,128)S(1)}, u32[]{:S(2)}) %copy-start.1) | copy-done | bytes 1048600
  22.6 0.0 copy-start.2
  22.6 0.6 copy-done.2
  23.2 3.9 %collective-permute-done.1.hi_a = bf16[8,144,128]{2,1,0:T(8,128)(2,1)S(1)} collective-permute-done((bf16[8,144,128]{2,1,0:T(8,128)(2,1)S(1)}, bf16[8,144,128]{2,1,0:T(8,128)(2,1)S(1)}, u32[]{:S(2)}, u32[]{:S(2)}) %collective-permute-start.1) | collective-permute-done | bytes 294944 | tf_op jit(solution)/shard_map/ppermute | solution.py:384
  27.2 6.5 %collective-permute-done.lo_a = bf16[8,144,128]{2,1,0:T(8,128)(2,1)S(1)} collective-permute-done((bf16[8,144,128]{2,1,0:T(8,128)(2,1)S(1)}, bf16[8,144,128]{2,1,0:T(8,128)(2,1)S(1)}, u32[]{:S(2)}, u32[]{:S(2)}) %collective-permute-start) | collective-permute-done | bytes 294944 | tf_op jit(solution)/shard_map/ppermute | solution.py:383
  33.7 1.9 %collective-permute-start.2 = (bf16[8,144,128]{2,1,0:T(8,128)(2,1)S(1)}, bf16[8,144,128]{2,1,0:T(8,128)(2,1)S(1)}, u32[]{:S(2)}, u32[]{:S(2)}) collective-permute-start(bf16[8,144,128]{2,1,0:T(8,128)(2,1)S(1)} %collective-permute-done.lo_a), channel_id=1, source_target_pairs={{0,1},{1,0},{2,3},{3,2},{4,5},{5,4},{6,7},{7,6},{8,9},{9,8},{10,11... | collective-permute-start | bytes 884744 | tf_op jit(solution)/shard_map/ppermute | solution.py:412
  35.5 0.0 collective-permute-start.3
  35.5 0.8 copy.11.nbr_ref
  36.3 0.4 collective-permute-done.2.lo_b
  36.8 0.4 collective-permute-done.3.hi_b
  37.2 17.9 %halo_pairs.1 = (f32[16,3,128]{2,1,0:T(4,128)S(1)}, f32[16,5,128,128]{3,2,1,0:T(8,128)S(1)}, f32[16,5,128,128]{3,2,1,0:T(8,128)S(1)}, bf16[48,16,128]{2,1,0:T(8,128)(2,1)S(1)}) custom-call(s32[16,6]{1,0:T(8,128)S(1)} %copy.11.nbr_ref, s32[16]{0:T(128)} %cnt_ref.3, f32[4]{0:T(128)} %bitcast.10, s32[3]{0:T(128)S(1)} %pad_add_fusion.meta_ref, ...), custom_call_target="tpu_custom_call" | custom-call | tf_op jit(solution)/shard_map/halo_pairs/pallas_call | solution.py:415
  55.1 2.2 %collective-permute-start.6 = (f32[16,3,128]{2,1,0:T(4,128)S(1)}, f32[16,3,128]{2,1,0:T(4,128)S(1)}, u32[]{:S(2)}, u32[]{:S(2)}) collective-permute-start(f32[16,3,128]{2,1,0:T(4,128)S(1)} %get-tuple-element.24), channel_id=1, source_target_pairs={{0,3},{1,2},{2,1},{3,0},{4,7},{5,6},{6,5},{7,4},{8,11},{9,10},{10,... | collective-permute-start | bytes 73736 | tf_op jit(solution)/shard_map/ppermute | solution.py:348
  57.3 0.0 collective-permute-start.5
  57.3 0.5 collective-permute-start.4
  57.8 1.1 %collective-permute-done.6 = f32[16,3,128]{2,1,0:T(4,128)S(1)} collective-permute-done((f32[16,3,128]{2,1,0:T(4,128)S(1)}, f32[16,3,128]{2,1,0:T(4,128)S(1)}, u32[]{:S(2)}, u32[]{:S(2)}) %collective-permute-start.6) | collective-permute-done | bytes 24608 | tf_op jit(solution)/shard_map/ppermute | solution.py:348
  58.9 1.2 %collective-permute-done.5 = f32[16,3,128]{2,1,0:T(4,128)S(1)} collective-permute-done((f32[16,3,128]{2,1,0:T(4,128)S(1)}, f32[16,3,128]{2,1,0:T(4,128)S(1)}, u32[]{:S(2)}, u32[]{:S(2)}) %collective-permute-start.5) | collective-permute-done | bytes 24608 | tf_op jit(solution)/shard_map/ppermute | solution.py:348
  60.1 0.0 collective-permute-done.4
  60.1 0.1 collective-permute-start.8
  60.2 2.4 %collective-permute-start.7 = (f32[16,3,128]{2,1,0:T(4,128)S(1)}, f32[16,3,128]{2,1,0:T(4,128)S(1)}, u32[]{:S(2)}, u32[]{:S(2)}) collective-permute-start(f32[16,3,128]{2,1,0:T(4,128)S(1)} %get-tuple-element.34.tan_ref.tan_own), channel_id=1, source_target_pairs={{0,4},{4,8},{8,12},{12,16},{16,20},{20,24},{24,28},{28,32},{32,36}... | collective-permute-start | bytes 73736 | tf_op jit(solution)/shard_map/ppermute | solution.py:437
  62.6 3.5 %own_gradient.1 = (f32[16,3,128]{2,1,0:T(4,128)S(1)}, bf16[16,6,32,128]{3,2,1,0:T(8,128)(2,1)S(1)}) custom-call(bf16[16,16,128]{2,1,0:T(8,128)(2,1)S(1)} %get-tuple-element.21.own_tile.tile_ref, f32[16,3,128]{2,1,0:T(4,128)S(1)} %get-tuple-element.34.tan_ref.tan_own, f32[16,128,128]{2,1,0:T(8,128)} %copy-done, f32[16,128,128]{2,1,0:T(8,128)} %copy-done.1), custom_call_target="tpu_custom_call" | custom-call | tf_op jit(solution)/shard_map/own_gradient/pallas_call | solution.py:439
  66.1 0.0 collective-permute-done.8.tan_hi
  66.1 3.5 %collective-permute-done.7.tan_lo = f32[16,3,128]{2,1,0:T(4,128)S(1)} collective-permute-done((f32[16,3,128]{2,1,0:T(4,128)S(1)}, f32[16,3,128]{2,1,0:T(4,128)S(1)}, u32[]{:S(2)}, u32[]{:S(2)}) %collective-permute-start.7) | collective-permute-done | bytes 24608 | tf_op jit(solution)/shard_map/ppermute | solution.py:437
  69.6 8.4 %variance_gradient.1 = f32[16,3,128]{2,1,0:T(4,128)S(1)} custom-call(s32[16,6]{1,0:T(8,128)S(1)} %copy.11.nbr_ref, s32[16]{0:T(128)} %cnt_ref.3, s32[3]{0:T(128)S(1)} %pad_add_fusion.meta_ref, bf16[48,16,128]{2,1,0:T(8,128)(2,1)S(1)} %get-tuple-element.25.pos_ref, f32[16,3,128]{2,1,0:T(4,128)S(1)} %get-tuple-element.34.tan_ref.tan_own, ...), custom_call_target="tpu_custom_call" | custom-call | tf_op jit(solution)/shard_map/variance_gradient/pallas_call | solution.py:449
  78.0 3.2 %collective-permute-start.11 = (f32[16,3,128]{2,1,0:T(4,128)S(1)}, f32[16,3,128]{2,1,0:T(4,128)S(1)}, u32[]{:S(2)}, u32[]{:S(2)}) collective-permute-start(f32[16,3,128]{2,1,0:T(4,128)S(1)} %variance_gradient.1), channel_id=1, source_target_pairs={{0,3},{1,2},{2,1},{3,0},{4,7},{5,6},{6,5},{7,4},{8,11},{9,10},{10,... | collective-permute-start | bytes 73736 | tf_op jit(solution)/shard_map/ppermute | solution.py:348
  81.2 0.7 collective-permute-start.10
  81.9 0.0 collective-permute-start.9
  81.9 0.6 copy.13
  82.5 0.3 collective-permute-done.11
  82.8 1.6 %collective-permute-done.10 = f32[16,3,128]{2,1,0:T(4,128)S(1)} collective-permute-done((f32[16,3,128]{2,1,0:T(4,128)S(1)}, f32[16,3,128]{2,1,0:T(4,128)S(1)}, u32[]{:S(2)}, u32[]{:S(2)}) %collective-permute-start.10) | collective-permute-done | bytes 24608 | tf_op jit(solution)/shard_map/ppermute | solution.py:348
  84.4 0.0 collective-permute-done.9
  84.5 0.6 copy.14
  (2 shorter events, 0.0 us)
Async XLA Ops:
  3.0 24.1 %collective-permute-start.1 = (bf16[8,144,128]{2,1,0:T(8,128)(2,1)S(1)}, bf16[8,144,128]{2,1,0:T(8,128)(2,1)S(1)}, u32[]{:S(2)}, u32[]{:S(2)}) collective-permute-start(bf16[8,144,128]{2,1,0:T(8,128)(2,1)S(1)} %pack_halo.1), channel_id=1, source_target_pairs={{0,252},{4,0},{8,4},{12,8},{16,12},{20,16},{24,20},{28,24},{32,28}... | collective-permute-start | bytes 884744 | tf_op jit(solution)/shard_map/ppermute | solution.py:384
  14.6 19.1 %collective-permute-start = (bf16[8,144,128]{2,1,0:T(8,128)(2,1)S(1)}, bf16[8,144,128]{2,1,0:T(8,128)(2,1)S(1)}, u32[]{:S(2)}, u32[]{:S(2)}) collective-permute-start(bf16[8,144,128]{2,1,0:T(8,128)(2,1)S(1)} %pack_halo.1), channel_id=1, source_target_pairs={{0,4},{4,8},{8,12},{12,16},{16,20},{20,24},{24,28},{28,32},{32,36}... | collective-permute-start | bytes 884744 | tf_op jit(solution)/shard_map/ppermute | solution.py:383
  20.6 1.0 %copy-start = (f32[16,128,128]{2,1,0:T(8,128)}, f32[16,128,128]{2,1,0:T(8,128)S(1)}, u32[]{:S(2)}) copy-start(f32[16,128,128]{2,1,0:T(8,128)S(1)} %get-tuple-element.26.first_ref) | copy-start | bytes 3145732
  21.6 1.0 %copy-start.1 = (f32[16,128,128]{2,1,0:T(8,128)}, f32[16,128,128]{2,1,0:T(8,128)S(1)}, u32[]{:S(2)}) copy-start(f32[16,128,128]{2,1,0:T(8,128)S(1)} %get-tuple-element.27.second_ref) | copy-start | bytes 3145732
  22.6 0.6 copy-start.2
  33.7 3.1 %collective-permute-start.2 = (bf16[8,144,128]{2,1,0:T(8,128)(2,1)S(1)}, bf16[8,144,128]{2,1,0:T(8,128)(2,1)S(1)}, u32[]{:S(2)}, u32[]{:S(2)}) collective-permute-start(bf16[8,144,128]{2,1,0:T(8,128)(2,1)S(1)} %collective-permute-done.lo_a), channel_id=1, source_target_pairs={{0,1},{1,0},{2,3},{3,2},{4,5},{5,4},{6,7},{7,6},{8,9},{9,8},{10,11... | collective-permute-start | bytes 884744 | tf_op jit(solution)/shard_map/ppermute | solution.py:412
  35.5 1.6 %collective-permute-start.3 = (bf16[8,144,128]{2,1,0:T(8,128)(2,1)S(1)}, bf16[8,144,128]{2,1,0:T(8,128)(2,1)S(1)}, u32[]{:S(2)}, u32[]{:S(2)}) collective-permute-start(bf16[8,144,128]{2,1,0:T(8,128)(2,1)S(1)} %collective-permute-done.1.hi_a), channel_id=1, source_target_pairs={{0,1},{1,0},{2,3},{3,2},{4,5},{5,4},{6,7},{7,6},{8,9},{9,8},{10,11... | collective-permute-start | bytes 884744 | tf_op jit(solution)/shard_map/ppermute | solution.py:413
  55.1 3.8 %collective-permute-start.6 = (f32[16,3,128]{2,1,0:T(4,128)S(1)}, f32[16,3,128]{2,1,0:T(4,128)S(1)}, u32[]{:S(2)}, u32[]{:S(2)}) collective-permute-start(f32[16,3,128]{2,1,0:T(4,128)S(1)} %get-tuple-element.24), channel_id=1, source_target_pairs={{0,3},{1,2},{2,1},{3,0},{4,7},{5,6},{6,5},{7,4},{8,11},{9,10},{10,... | collective-permute-start | bytes 73736 | tf_op jit(solution)/shard_map/ppermute | solution.py:348
  57.3 2.8 %collective-permute-start.5 = (f32[16,3,128]{2,1,0:T(4,128)S(1)}, f32[16,3,128]{2,1,0:T(4,128)S(1)}, u32[]{:S(2)}, u32[]{:S(2)}) collective-permute-start(f32[16,3,128]{2,1,0:T(4,128)S(1)} %get-tuple-element.24), channel_id=1, source_target_pairs={{0,2},{1,3},{2,0},{3,1},{4,6},{5,7},{6,4},{7,5},{8,10},{9,11},{10,... | collective-permute-start | bytes 73736 | tf_op jit(solution)/shard_map/ppermute | solution.py:348
  57.3 2.8 %collective-permute-start.4 = (f32[16,3,128]{2,1,0:T(4,128)S(1)}, f32[16,3,128]{2,1,0:T(4,128)S(1)}, u32[]{:S(2)}, u32[]{:S(2)}) collective-permute-start(f32[16,3,128]{2,1,0:T(4,128)S(1)} %get-tuple-element.24), channel_id=1, source_target_pairs={{0,1},{1,0},{2,3},{3,2},{4,5},{5,4},{6,7},{7,6},{8,9},{9,8},{10,11... | collective-permute-start | bytes 73736 | tf_op jit(solution)/shard_map/ppermute | solution.py:348
  60.1 6.0 %collective-permute-start.8 = (f32[16,3,128]{2,1,0:T(4,128)S(1)}, f32[16,3,128]{2,1,0:T(4,128)S(1)}, u32[]{:S(2)}, u32[]{:S(2)}) collective-permute-start(f32[16,3,128]{2,1,0:T(4,128)S(1)} %get-tuple-element.34.tan_ref.tan_own), channel_id=1, source_target_pairs={{0,252},{4,0},{8,4},{12,8},{16,12},{20,16},{24,20},{28,24},{32,28}... | collective-permute-start | bytes 73736 | tf_op jit(solution)/shard_map/ppermute | solution.py:438
  60.2 9.4 %collective-permute-start.7 = (f32[16,3,128]{2,1,0:T(4,128)S(1)}, f32[16,3,128]{2,1,0:T(4,128)S(1)}, u32[]{:S(2)}, u32[]{:S(2)}) collective-permute-start(f32[16,3,128]{2,1,0:T(4,128)S(1)} %get-tuple-element.34.tan_ref.tan_own), channel_id=1, source_target_pairs={{0,4},{4,8},{8,12},{12,16},{16,20},{20,24},{24,28},{28,32},{32,36}... | collective-permute-start | bytes 73736 | tf_op jit(solution)/shard_map/ppermute | solution.py:437
  78.0 4.8 %collective-permute-start.11 = (f32[16,3,128]{2,1,0:T(4,128)S(1)}, f32[16,3,128]{2,1,0:T(4,128)S(1)}, u32[]{:S(2)}, u32[]{:S(2)}) collective-permute-start(f32[16,3,128]{2,1,0:T(4,128)S(1)} %variance_gradient.1), channel_id=1, source_target_pairs={{0,3},{1,2},{2,1},{3,0},{4,7},{5,6},{6,5},{7,4},{8,11},{9,10},{10,... | collective-permute-start | bytes 73736 | tf_op jit(solution)/shard_map/ppermute | solution.py:348
  81.2 3.2 %collective-permute-start.10 = (f32[16,3,128]{2,1,0:T(4,128)S(1)}, f32[16,3,128]{2,1,0:T(4,128)S(1)}, u32[]{:S(2)}, u32[]{:S(2)}) collective-permute-start(f32[16,3,128]{2,1,0:T(4,128)S(1)} %variance_gradient.1), channel_id=1, source_target_pairs={{0,2},{1,3},{2,0},{3,1},{4,6},{5,7},{6,4},{7,5},{8,10},{9,11},{10,... | collective-permute-start | bytes 73736 | tf_op jit(solution)/shard_map/ppermute | solution.py:348
  81.9 2.5 %collective-permute-start.9 = (f32[16,3,128]{2,1,0:T(4,128)S(1)}, f32[16,3,128]{2,1,0:T(4,128)S(1)}, u32[]{:S(2)}, u32[]{:S(2)}) collective-permute-start(f32[16,3,128]{2,1,0:T(4,128)S(1)} %variance_gradient.1), channel_id=1, source_target_pairs={{0,1},{1,0},{2,3},{3,2},{4,5},{5,4},{6,7},{7,6},{8,9},{9,8},{10,11... | collective-permute-start | bytes 73736 | tf_op jit(solution)/shard_map/ppermute | solution.py:348
